TPU v7x, 32 devices: a whole 2x2x4 slice. The times are simulated.
32 devices in a mesh: groups: 2 (over x), hist: 16 (over z, y, core).
Axes of the slice: x: 2, y: 2, z: 4, core: 2. Of those that a mesh axis runs over, the one named last changes fastest.
Arguments:
- history: bfloat16 [16384, 1024], P(('groups', 'hist')), parts along dimension 0, may hold values from -6 to 6
- candidates: bfloat16 [512, 1024], P(('groups', 'hist')), parts along dimension 0, may hold values from -6 to 6
- hist_length: int32 [2], P('groups'), parts along dimension 0, may hold values from 4096 to 8192
- visible: int32 [512], P(('groups', 'hist')), parts along dimension 0, may hold values from 1 to 8192
- w_proj: bfloat16 [1024, 4096], replicated, may hold values from -0.1875 to 0.1875
- w_out: bfloat16 [1024, 1024], replicated, may hold values from -0.1875 to 0.1875
Outputs:
- scored: bfloat16 [512, 1024], P(('groups', 'hist')), parts along dimension 0
There are 2 independent parts, one for each index of `groups`. A program takes and returns all parts, laid end to end along the dimension named above; an argument that names none is the same for every part. Nothing has to cross between parts.
All inputs are finite; a program needn't handle non-finite values.
Results may differ from a plain program's by a relative error of at most 0.0022.
The roundings to bfloat16 on the way count: a program that leaves them out, or rounds other values in their place, can miss the bound.
Values may be sent and summed in bfloat16 or wider, within the bound.
No kernel may reach another device: no remote copies, remote signals or barrier semaphores. Data moves between devices by JAX's collectives and lax.ppermute only.
A program may use at most 64 MiB of HBM per device.

v0:
```python
import jax
import jax.numpy as jnp
from jax import lax
from jax.sharding import PartitionSpec as P

HEADS = 8


EPS = 1e-06


def shifted(shard, axis, by):
    size = lax.axis_size(axis)
    return lax.ppermute(shard, axis, [(i, (i + by) % size) for i in range(size)])


def layer_norm(rows):
    rows = rows.astype(jnp.float32)
    centred = rows - jnp.mean(rows, axis=-1, keepdims=True)
    spread = jnp.mean(centred * centred, axis=-1, keepdims=True)
    return centred * lax.rsqrt(spread + EPS)


def attend(query, limit, keys, values, base, heads):
    rows = query.shape[0]
    n_keys = keys.shape[0]
    head_size = query.shape[1] // heads
    q_h = query.reshape(rows, heads, head_size)
    k_h = keys.reshape(n_keys, heads, head_size)
    v_h = values.reshape(n_keys, heads, head_size)
    scores = jnp.einsum("rhd,khd->hrk", q_h, k_h, preferred_element_type=jnp.float32)
    position = base + jnp.arange(n_keys, dtype=jnp.int32)
    seen = (position[None, :] < limit[:, None]).astype(jnp.float32)
    count = (limit + 1).astype(jnp.float32)
    weight = jax.nn.silu(scores * head_size ** (-0.5)) * seen[None] / count[None, :, None]
    weight = weight.astype(jnp.bfloat16)
    out = jnp.einsum("hrk,khd->rhd", weight, v_h, preferred_element_type=jnp.float32)
    return out.reshape(rows, -1)


def on_device(history, candidates, hist_length, visible, w_proj, w_out):
    width = w_out.shape[0]
    heads = HEADS
    head_size = width // heads
    hist_norm = layer_norm(history).astype(jnp.bfloat16)
    hist_kv = jax.nn.silu(
        jnp.dot(hist_norm, w_proj[:, 2 * width :], preferred_element_type=jnp.float32)
    ).astype(jnp.bfloat16)
    keys_local = hist_kv[:, :width]
    values_local = hist_kv[:, width:]
    cand_norm = layer_norm(candidates).astype(jnp.bfloat16)
    proj = jax.nn.silu(jnp.dot(cand_norm, w_proj, preferred_element_type=jnp.float32)).astype(
        jnp.bfloat16
    )
    gate = proj[:, :width]
    query = proj[:, width : 2 * width]
    self_key = proj[:, 2 * width : 3 * width]
    self_value = proj[:, 3 * width :]
    limit = jnp.minimum(visible, hist_length[0])
    count = (limit + 1).astype(jnp.float32)
    rows_here = query.shape[0]
    cycle_size = lax.axis_size("hist")
    base = lax.axis_index("hist") * history.shape[0]
    zeros = jnp.zeros((rows_here, width), jnp.float32)

    def turn(step, carry):
        query_now, limit_now, accum = carry
        accum = accum + attend(query_now, limit_now, keys_local, values_local, base, heads)
        return (
            shifted(query_now.astype(jnp.float32), "hist", 1).astype(query_now.dtype),
            shifted(limit_now, "hist", 1),
            shifted(accum, "hist", 1),
        )

    carried = lax.fori_loop(0, cycle_size, turn, (query, limit, zeros))
    attended = carried[2]
    self_scores = (
        (query.astype(jnp.float32) * self_key.astype(jnp.float32))
        .reshape(rows_here, heads, head_size)
        .sum(-1)
    )
    self_weight = (
        (jax.nn.silu(self_scores * head_size ** (-0.5)) / count[:, None])
        .astype(jnp.bfloat16)
        .astype(jnp.float32)
    )
    self_term = (
        self_weight[:, :, None]
        * self_value.astype(jnp.float32).reshape(rows_here, heads, head_size)
    ).reshape(rows_here, width)
    attended = attended + self_term
    mixed = (layer_norm(attended) * gate.astype(jnp.float32)).astype(jnp.bfloat16)
    result = candidates.astype(jnp.float32) + jnp.dot(
        mixed, w_out, preferred_element_type=jnp.float32
    )
    return result.astype(jnp.bfloat16)


def solution(mesh):
    in_specs = (
        P(("groups", "hist"), None),
        P(("groups", "hist"), None),
        P("groups"),
        P(("groups", "hist")),
        P(),
        P(),
    )
    out_specs = P(("groups", "hist"), None)
    return jax.shard_map(
        on_device, mesh=mesh, in_specs=in_specs, out_specs=out_specs, check_vma=False
    )
```

profile of v0, /device:TPU:0, one launch (start us, length us, event | category | flops | bytes accessed | tf_op | source)
XLA Modules:
  0.0 160.1 jit_solution(5999162046175047444)
XLA Ops:
  0.0 1.0 convert_reduce_fusion.1
  1.0 0.9 fusion.32
  2.0 4.8 %multiply_convert_fusion.1 = bf16[16,4096]{1,0:T(8,128)(2,1)S(1)} fusion(bf16[1024,4096]{1,0:T(8,128)(2,1)} %param.12, bf16[16,1024]{1,0:T(8,128)(2,1)} %param.9, f32[16]{0:T(128)S(1)} %add_rsqrt_fusion.2, f32[16]{0:T(128)S(1)} %broadcast_multiply_fusion.2), kind=kOutput, calls=%fused_computation.32 | convolution fusion | flops 134610944 | bytes 8552576 | tf_op jit(solution)/shard_map/dot_general | solution.py:52
  6.9 0.2 convert_reduce_fusion
  7.1 0.4 fusion.22
  7.5 0.6 copy-done.1
  8.2 2.8 %multiply_convert_fusion = bf16[512,2048]{1,0:T(8,128)(2,1)S(1)} fusion(bf16[1024,4096]{1,0:T(8,128)(2,1)S(1)} %copy-done.1, bf16[512,1024]{1,0:T(8,128)(2,1)S(1)} %copy-done.2, f32[512]{0:T(512)S(1)} %add_rsqrt_fusion, f32[512]{0:T(512)S(1)} %broadcast_multiply_fusion), kind=kOutput, calls=%fused_computation.19 | convolution fusion | flops 2154823680 | bytes 7344128 | tf_op jit(solution)/shard_map/dot_general | solution.py:47
  11.0 1.2 fusion.47
  12.9 143.1 %while.14 = (s32[]{:T(128)}, bf16[16,1024]{1,0:T(8,128)(2,1)S(1)}, s32[16]{0:T(128)S(1)}, f32[16,1024]{1,0:T(8,128)S(1)}, bf16[512,1024]{1,0:T(8,128)(2,1)}, /*i...) while((s32[]{:T(128)}, bf16[16,1024]{1,0:T(8,128)(2,1)S(1)}, s32[16]{0:T(128)S(1)}, ...), condition=%wide.region_5.6_spmd, body=%wide.region_4.5_spmd.sunk | while | flops 34112032 | bytes 2921297 | solution.py:75
  13.1 1.8 %convolution_bitcast_fusion.2 = f32[8,2,8,128]{3,2,1,0:T(8,128)S(1)} fusion(f32[16]{0:T(128)S(1)} %add_convert_fusion.3, f32[16,512]{1,0:T(8,128)S(1)} %compare_convert_fusion.2, bf16[512,1024]{1,0:T(8,128)(2,1)S(1)} %get-tuple-element.128, bf16[512,1024]{1,0:T(8,128)(2,1)} %get-tuple-element.126, bf16[16,1024]{1,0:T(8,128)(2,1)S(1)} %copy.64), kind=kOutput, calls=%fused_computation.1.clone.1 | convolution fusion | flops 34078720 | bytes 2228288 | tf_op jit(solution)/shard_map/while/body/eval_jaxpr/hrk,khd->rhd/dot_general | solution.py:37
  14.9 0.5 collective-permute-start.2
  15.4 2.6 %collective-permute-start = (bf16[16,1024]{1,0:T(8,128)(2,1)S(1)}, bf16[16,1024]{1,0:T(8,128)(2,1)S(1)}, u32[]{:S(2)}, u32[]{:S(2)}) collective-permute-start(bf16[16,1024]{1,0:T(8,128)(2,1)S(1)} %copy.64), channel_id=1, source_target_pairs={{0,1},{1,2},{2,3},{3,4},{4,5},{5,6},{6,7},{7,8},{8,9},{9,10},{10,1... | collective-permute-start | bytes 98312 | tf_op jit(solution)/shard_map/while/body/eval_jaxpr/ppermute | solution.py:14
  18.1 5.6 %collective-permute-done.1 = s32[16]{0:T(128)S(1)} collective-permute-done((s32[16]{0:T(128)S(1)}, s32[16]{0:T(128)S(1)}, u32[]{:S(2)}, u32[]{:S(2)}) %collective-permute-start.1) | collective-permute-done | bytes 96 | tf_op jit(solution)/shard_map/while/body/eval_jaxpr/ppermute | solution.py:14
  23.9 1.8 %convolution_bitcast_fusion.2 = f32[8,2,8,128]{3,2,1,0:T(8,128)S(1)} fusion(f32[16]{0:T(128)S(1)} %add_convert_fusion.3, f32[16,512]{1,0:T(8,128)S(1)} %compare_convert_fusion.2, bf16[512,1024]{1,0:T(8,128)(2,1)S(1)} %get-tuple-element.128, bf16[512,1024]{1,0:T(8,128)(2,1)} %get-tuple-element.126, bf16[16,1024]{1,0:T(8,128)(2,1)S(1)} %copy.64), kind=kOutput, calls=%fused_computation.1.clone.1 | convolution fusion | flops 34078720 | bytes 2228288 | tf_op jit(solution)/shard_map/while/body/eval_jaxpr/hrk,khd->rhd/dot_general | solution.py:37
  25.9 6.7 %collective-permute-done.1 = s32[16]{0:T(128)S(1)} collective-permute-done((s32[16]{0:T(128)S(1)}, s32[16]{0:T(128)S(1)}, u32[]{:S(2)}, u32[]{:S(2)}) %collective-permute-start.1) | collective-permute-done | bytes 96 | tf_op jit(solution)/shard_map/while/body/eval_jaxpr/ppermute | solution.py:14
  32.7 1.8 %convolution_bitcast_fusion.2 = f32[8,2,8,128]{3,2,1,0:T(8,128)S(1)} fusion(f32[16]{0:T(128)S(1)} %add_convert_fusion.3, f32[16,512]{1,0:T(8,128)S(1)} %compare_convert_fusion.2, bf16[512,1024]{1,0:T(8,128)(2,1)S(1)} %get-tuple-element.128, bf16[512,1024]{1,0:T(8,128)(2,1)} %get-tuple-element.126, bf16[16,1024]{1,0:T(8,128)(2,1)S(1)} %copy.64), kind=kOutput, calls=%fused_computation.1.clone.1 | convolution fusion | flops 34078720 | bytes 2228288 | tf_op jit(solution)/shard_map/while/body/eval_jaxpr/hrk,khd->rhd/dot_general | solution.py:37
  34.7 6.7 %collective-permute-done.1 = s32[16]{0:T(128)S(1)} collective-permute-done((s32[16]{0:T(128)S(1)}, s32[16]{0:T(128)S(1)}, u32[]{:S(2)}, u32[]{:S(2)}) %collective-permute-start.1) | collective-permute-done | bytes 96 | tf_op jit(solution)/shard_map/while/body/eval_jaxpr/ppermute | solution.py:14
  41.5 1.8 %convolution_bitcast_fusion.2 = f32[8,2,8,128]{3,2,1,0:T(8,128)S(1)} fusion(f32[16]{0:T(128)S(1)} %add_convert_fusion.3, f32[16,512]{1,0:T(8,128)S(1)} %compare_convert_fusion.2, bf16[512,1024]{1,0:T(8,128)(2,1)S(1)} %get-tuple-element.128, bf16[512,1024]{1,0:T(8,128)(2,1)} %get-tuple-element.126, bf16[16,1024]{1,0:T(8,128)(2,1)S(1)} %copy.64), kind=kOutput, calls=%fused_computation.1.clone.1 | convolution fusion | flops 34078720 | bytes 2228288 | tf_op jit(solution)/shard_map/while/body/eval_jaxpr/hrk,khd->rhd/dot_general | solution.py:37
  43.5 6.7 %collective-permute-done.1 = s32[16]{0:T(128)S(1)} collective-permute-done((s32[16]{0:T(128)S(1)}, s32[16]{0:T(128)S(1)}, u32[]{:S(2)}, u32[]{:S(2)}) %collective-permute-start.1) | collective-permute-done | bytes 96 | tf_op jit(solution)/shard_map/while/body/eval_jaxpr/ppermute | solution.py:14
  50.3 1.8 %convolution_bitcast_fusion.2 = f32[8,2,8,128]{3,2,1,0:T(8,128)S(1)} fusion(f32[16]{0:T(128)S(1)} %add_convert_fusion.3, f32[16,512]{1,0:T(8,128)S(1)} %compare_convert_fusion.2, bf16[512,1024]{1,0:T(8,128)(2,1)S(1)} %get-tuple-element.128, bf16[512,1024]{1,0:T(8,128)(2,1)} %get-tuple-element.126, bf16[16,1024]{1,0:T(8,128)(2,1)S(1)} %copy.64), kind=kOutput, calls=%fused_computation.1.clone.1 | convolution fusion | flops 34078720 | bytes 2228288 | tf_op jit(solution)/shard_map/while/body/eval_jaxpr/hrk,khd->rhd/dot_general | solution.py:37
  52.3 6.7 %collective-permute-done.1 = s32[16]{0:T(128)S(1)} collective-permute-done((s32[16]{0:T(128)S(1)}, s32[16]{0:T(128)S(1)}, u32[]{:S(2)}, u32[]{:S(2)}) %collective-permute-start.1) | collective-permute-done | bytes 96 | tf_op jit(solution)/shard_map/while/body/eval_jaxpr/ppermute | solution.py:14
  59.1 1.8 %convolution_bitcast_fusion.2 = f32[8,2,8,128]{3,2,1,0:T(8,128)S(1)} fusion(f32[16]{0:T(128)S(1)} %add_convert_fusion.3, f32[16,512]{1,0:T(8,128)S(1)} %compare_convert_fusion.2, bf16[512,1024]{1,0:T(8,128)(2,1)S(1)} %get-tuple-element.128, bf16[512,1024]{1,0:T(8,128)(2,1)} %get-tuple-element.126, bf16[16,1024]{1,0:T(8,128)(2,1)S(1)} %copy.64), kind=kOutput, calls=%fused_computation.1.clone.1 | convolution fusion | flops 34078720 | bytes 2228288 | tf_op jit(solution)/shard_map/while/body/eval_jaxpr/hrk,khd->rhd/dot_general | solution.py:37
  61.2 6.7 %collective-permute-done.1 = s32[16]{0:T(128)S(1)} collective-permute-done((s32[16]{0:T(128)S(1)}, s32[16]{0:T(128)S(1)}, u32[]{:S(2)}, u32[]{:S(2)}) %collective-permute-start.1) | collective-permute-done | bytes 96 | tf_op jit(solution)/shard_map/while/body/eval_jaxpr/ppermute | solution.py:14
  67.9 1.8 %convolution_bitcast_fusion.2 = f32[8,2,8,128]{3,2,1,0:T(8,128)S(1)} fusion(f32[16]{0:T(128)S(1)} %add_convert_fusion.3, f32[16,512]{1,0:T(8,128)S(1)} %compare_convert_fusion.2, bf16[512,1024]{1,0:T(8,128)(2,1)S(1)} %get-tuple-element.128, bf16[512,1024]{1,0:T(8,128)(2,1)} %get-tuple-element.126, bf16[16,1024]{1,0:T(8,128)(2,1)S(1)} %copy.64), kind=kOutput, calls=%fused_computation.1.clone.1 | convolution fusion | flops 34078720 | bytes 2228288 | tf_op jit(solution)/shard_map/while/body/eval_jaxpr/hrk,khd->rhd/dot_general | solution.py:37
  70.0 6.7 %collective-permute-done.1 = s32[16]{0:T(128)S(1)} collective-permute-done((s32[16]{0:T(128)S(1)}, s32[16]{0:T(128)S(1)}, u32[]{:S(2)}, u32[]{:S(2)}) %collective-permute-start.1) | collective-permute-done | bytes 96 | tf_op jit(solution)/shard_map/while/body/eval_jaxpr/ppermute | solution.py:14
  76.8 1.8 %convolution_bitcast_fusion.2 = f32[8,2,8,128]{3,2,1,0:T(8,128)S(1)} fusion(f32[16]{0:T(128)S(1)} %add_convert_fusion.3, f32[16,512]{1,0:T(8,128)S(1)} %compare_convert_fusion.2, bf16[512,1024]{1,0:T(8,128)(2,1)S(1)} %get-tuple-element.128, bf16[512,1024]{1,0:T(8,128)(2,1)} %get-tuple-element.126, bf16[16,1024]{1,0:T(8,128)(2,1)S(1)} %copy.64), kind=kOutput, calls=%fused_computation.1.clone.1 | convolution fusion | flops 34078720 | bytes 2228288 | tf_op jit(solution)/shard_map/while/body/eval_jaxpr/hrk,khd->rhd/dot_general | solution.py:37
  78.8 6.7 %collective-permute-done.1 = s32[16]{0:T(128)S(1)} collective-permute-done((s32[16]{0:T(128)S(1)}, s32[16]{0:T(128)S(1)}, u32[]{:S(2)}, u32[]{:S(2)}) %collective-permute-start.1) | collective-permute-done | bytes 96 | tf_op jit(solution)/shard_map/while/body/eval_jaxpr/ppermute | solution.py:14
  85.6 1.8 %convolution_bitcast_fusion.2 = f32[8,2,8,128]{3,2,1,0:T(8,128)S(1)} fusion(f32[16]{0:T(128)S(1)} %add_convert_fusion.3, f32[16,512]{1,0:T(8,128)S(1)} %compare_convert_fusion.2, bf16[512,1024]{1,0:T(8,128)(2,1)S(1)} %get-tuple-element.128, bf16[512,1024]{1,0:T(8,128)(2,1)} %get-tuple-element.126, bf16[16,1024]{1,0:T(8,128)(2,1)S(1)} %copy.64), kind=kOutput, calls=%fused_computation.1.clone.1 | convolution fusion | flops 34078720 | bytes 2228288 | tf_op jit(solution)/shard_map/while/body/eval_jaxpr/hrk,khd->rhd/dot_general | solution.py:37
  87.6 6.7 %collective-permute-done.1 = s32[16]{0:T(128)S(1)} collective-permute-done((s32[16]{0:T(128)S(1)}, s32[16]{0:T(128)S(1)}, u32[]{:S(2)}, u32[]{:S(2)}) %collective-permute-start.1) | collective-permute-done | bytes 96 | tf_op jit(solution)/shard_map/while/body/eval_jaxpr/ppermute | solution.py:14
  94.4 1.8 %convolution_bitcast_fusion.2 = f32[8,2,8,128]{3,2,1,0:T(8,128)S(1)} fusion(f32[16]{0:T(128)S(1)} %add_convert_fusion.3, f32[16,512]{1,0:T(8,128)S(1)} %compare_convert_fusion.2, bf16[512,1024]{1,0:T(8,128)(2,1)S(1)} %get-tuple-element.128, bf16[512,1024]{1,0:T(8,128)(2,1)} %get-tuple-element.126, bf16[16,1024]{1,0:T(8,128)(2,1)S(1)} %copy.64), kind=kOutput, calls=%fused_computation.1.clone.1 | convolution fusion | flops 34078720 | bytes 2228288 | tf_op jit(solution)/shard_map/while/body/eval_jaxpr/hrk,khd->rhd/dot_general | solution.py:37
  96.4 6.7 %collective-permute-done.1 = s32[16]{0:T(128)S(1)} collective-permute-done((s32[16]{0:T(128)S(1)}, s32[16]{0:T(128)S(1)}, u32[]{:S(2)}, u32[]{:S(2)}) %collective-permute-start.1) | collective-permute-done | bytes 96 | tf_op jit(solution)/shard_map/while/body/eval_jaxpr/ppermute | solution.py:14
  103.2 1.8 %convolution_bitcast_fusion.2 = f32[8,2,8,128]{3,2,1,0:T(8,128)S(1)} fusion(f32[16]{0:T(128)S(1)} %add_convert_fusion.3, f32[16,512]{1,0:T(8,128)S(1)} %compare_convert_fusion.2, bf16[512,1024]{1,0:T(8,128)(2,1)S(1)} %get-tuple-element.128, bf16[512,1024]{1,0:T(8,128)(2,1)} %get-tuple-element.126, bf16[16,1024]{1,0:T(8,128)(2,1)S(1)} %copy.64), kind=kOutput, calls=%fused_computation.1.clone.1 | convolution fusion | flops 34078720 | bytes 2228288 | tf_op jit(solution)/shard_map/while/body/eval_jaxpr/hrk,khd->rhd/dot_general | solution.py:37
  105.2 6.7 %collective-permute-done.1 = s32[16]{0:T(128)S(1)} collective-permute-done((s32[16]{0:T(128)S(1)}, s32[16]{0:T(128)S(1)}, u32[]{:S(2)}, u32[]{:S(2)}) %collective-permute-start.1) | collective-permute-done | bytes 96 | tf_op jit(solution)/shard_map/while/body/eval_jaxpr/ppermute | solution.py:14
  112.0 1.8 %convolution_bitcast_fusion.2 = f32[8,2,8,128]{3,2,1,0:T(8,128)S(1)} fusion(f32[16]{0:T(128)S(1)} %add_convert_fusion.3, f32[16,512]{1,0:T(8,128)S(1)} %compare_convert_fusion.2, bf16[512,1024]{1,0:T(8,128)(2,1)S(1)} %get-tuple-element.128, bf16[512,1024]{1,0:T(8,128)(2,1)} %get-tuple-element.126, bf16[16,1024]{1,0:T(8,128)(2,1)S(1)} %copy.64), kind=kOutput, calls=%fused_computation.1.clone.1 | convolution fusion | flops 34078720 | bytes 2228288 | tf_op jit(solution)/shard_map/while/body/eval_jaxpr/hrk,khd->rhd/dot_general | solution.py:37
  114.0 6.7 %collective-permute-done.1 = s32[16]{0:T(128)S(1)} collective-permute-done((s32[16]{0:T(128)S(1)}, s32[16]{0:T(128)S(1)}, u32[]{:S(2)}, u32[]{:S(2)}) %collective-permute-start.1) | collective-permute-done | bytes 96 | tf_op jit(solution)/shard_map/while/body/eval_jaxpr/ppermute | solution.py:14
  120.8 1.8 %convolution_bitcast_fusion.2 = f32[8,2,8,128]{3,2,1,0:T(8,128)S(1)} fusion(f32[16]{0:T(128)S(1)} %add_convert_fusion.3, f32[16,512]{1,0:T(8,128)S(1)} %compare_convert_fusion.2, bf16[512,1024]{1,0:T(8,128)(2,1)S(1)} %get-tuple-element.128, bf16[512,1024]{1,0:T(8,128)(2,1)} %get-tuple-element.126, bf16[16,1024]{1,0:T(8,128)(2,1)S(1)} %copy.64), kind=kOutput, calls=%fused_computation.1.clone.1 | convolution fusion | flops 34078720 | bytes 2228288 | tf_op jit(solution)/shard_map/while/body/eval_jaxpr/hrk,khd->rhd/dot_general | solution.py:37
  122.9 6.7 %collective-permute-done.1 = s32[16]{0:T(128)S(1)} collective-permute-done((s32[16]{0:T(128)S(1)}, s32[16]{0:T(128)S(1)}, u32[]{:S(2)}, u32[]{:S(2)}) %collective-permute-start.1) | collective-permute-done | bytes 96 | tf_op jit(solution)/shard_map/while/body/eval_jaxpr/ppermute | solution.py:14
  129.7 1.8 %convolution_bitcast_fusion.2 = f32[8,2,8,128]{3,2,1,0:T(8,128)S(1)} fusion(f32[16]{0:T(128)S(1)} %add_convert_fusion.3, f32[16,512]{1,0:T(8,128)S(1)} %compare_convert_fusion.2, bf16[512,1024]{1,0:T(8,128)(2,1)S(1)} %get-tuple-element.128, bf16[512,1024]{1,0:T(8,128)(2,1)} %get-tuple-element.126, bf16[16,1024]{1,0:T(8,128)(2,1)S(1)} %copy.64), kind=kOutput, calls=%fused_computation.1.clone.1 | convolution fusion | flops 34078720 | bytes 2228288 | tf_op jit(solution)/shard_map/while/body/eval_jaxpr/hrk,khd->rhd/dot_general | solution.py:37
  131.7 6.7 %collective-permute-done.1 = s32[16]{0:T(128)S(1)} collective-permute-done((s32[16]{0:T(128)S(1)}, s32[16]{0:T(128)S(1)}, u32[]{:S(2)}, u32[]{:S(2)}) %collective-permute-start.1) | collective-permute-done | bytes 96 | tf_op jit(solution)/shard_map/while/body/eval_jaxpr/ppermute | solution.py:14
  138.5 1.8 %convolution_bitcast_fusion.2 = f32[8,2,8,128]{3,2,1,0:T(8,128)S(1)} fusion(f32[16]{0:T(128)S(1)} %add_convert_fusion.3, f32[16,512]{1,0:T(8,128)S(1)} %compare_convert_fusion.2, bf16[512,1024]{1,0:T(8,128)(2,1)S(1)} %get-tuple-element.128, bf16[512,1024]{1,0:T(8,128)(2,1)} %get-tuple-element.126, bf16[16,1024]{1,0:T(8,128)(2,1)S(1)} %copy.64), kind=kOutput, calls=%fused_computation.1.clone.1 | convolution fusion | flops 34078720 | bytes 2228288 | tf_op jit(solution)/shard_map/while/body/eval_jaxpr/hrk,khd->rhd/dot_general | solution.py:37
  140.5 6.7 %collective-permute-done.1 = s32[16]{0:T(128)S(1)} collective-permute-done((s32[16]{0:T(128)S(1)}, s32[16]{0:T(128)S(1)}, u32[]{:S(2)}, u32[]{:S(2)}) %collective-permute-start.1) | collective-permute-done | bytes 96 | tf_op jit(solution)/shard_map/while/body/eval_jaxpr/ppermute | solution.py:14
  147.3 1.8 %convolution_bitcast_fusion.2 = f32[8,2,8,128]{3,2,1,0:T(8,128)S(1)} fusion(f32[16]{0:T(128)S(1)} %add_convert_fusion.3, f32[16,512]{1,0:T(8,128)S(1)} %compare_convert_fusion.2, bf16[512,1024]{1,0:T(8,128)(2,1)S(1)} %get-tuple-element.128, bf16[512,1024]{1,0:T(8,128)(2,1)} %get-tuple-element.126, bf16[16,1024]{1,0:T(8,128)(2,1)S(1)} %copy.64), kind=kOutput, calls=%fused_computation.1.clone.1 | convolution fusion | flops 34078720 | bytes 2228288 | tf_op jit(solution)/shard_map/while/body/eval_jaxpr/hrk,khd->rhd/dot_general | solution.py:37
  149.3 6.7 %collective-permute-done.1 = s32[16]{0:T(128)S(1)} collective-permute-done((s32[16]{0:T(128)S(1)}, s32[16]{0:T(128)S(1)}, u32[]{:S(2)}, u32[]{:S(2)}) %collective-permute-start.1) | collective-permute-done | bytes 96 | tf_op jit(solution)/shard_map/while/body/eval_jaxpr/ppermute | solution.py:14
  156.0 0.8 multiply_bitcast_fusion
  156.8 0.1 reduce_sum.67
  157.1 0.9 fusion.45
  158.1 0.2 multiply_reduce_fusion
  158.3 1.8 %fusion.26 = bf16[16,1024]{1,0:T(8,128)(2,1)} fusion(bf16[1024,1024]{1,0:T(8,128)(2,1)S(1)} %copy-done, bf16[16,1024]{1,0:T(8,128)(2,1)S(1)} %copy-done.3, f32[16,1024]{1,0:T(8,128)S(1)} %get-tuple-element.58, bf16[16,4096]{1,0:T(8,128)(2,1)} %copy-done.4, f32[16]{0:T(128)S(1)} %add_rsqrt_fusion.1, f32[16]{0:T(128)S(1)} %broadcast_multiply_fusion.1), kind=kOutput, calls=%fused_computation.29 | convolution fusion | flops 33685504 | bytes 2261120 | tf_op jit(solution)/shard_map/dot_general | solution.py:93
  (199 shorter events, 4.8 us)
Async XLA Ops:
  14.9 8.9 %collective-permute-start.2 = (f32[16,1024]{1,0:T(8,128)S(1)}, f32[16,1024]{1,0:T(8,128)S(1)}, u32[]{:S(2)}, u32[]{:S(2)}) collective-permute-start(f32[16,1024]{1,0:T(8,128)S(1)} %bitcast_add_fusion.2), channel_id=1, source_target_pairs={{0,1},{1,2},{2,3},{3,4},{4,5},{5,6},{6,7},{7,8},{8,9},{9,10},{10,1... | collective-permute-start | bytes 196616 | tf_op jit(solution)/shard_map/while/body/eval_jaxpr/ppermute | solution.py:14
  15.4 8.3 %collective-permute-start = (bf16[16,1024]{1,0:T(8,128)(2,1)S(1)}, bf16[16,1024]{1,0:T(8,128)(2,1)S(1)}, u32[]{:S(2)}, u32[]{:S(2)}) collective-permute-start(bf16[16,1024]{1,0:T(8,128)(2,1)S(1)} %copy.64), channel_id=1, source_target_pairs={{0,1},{1,2},{2,3},{3,4},{4,5},{5,6},{6,7},{7,8},{8,9},{9,10},{10,1... | collective-permute-start | bytes 98312 | tf_op jit(solution)/shard_map/while/body/eval_jaxpr/ppermute | solution.py:14
  18.1 5.7 %collective-permute-start.1 = (s32[16]{0:T(128)S(1)}, s32[16]{0:T(128)S(1)}, u32[]{:S(2)}, u32[]{:S(2)}) collective-permute-start(s32[16]{0:T(128)S(1)} %copy.65), channel_id=1, source_target_pairs={{0,1},{1,2},{2,3},{3,4},{4,5},{5,6},{6,7},{7,8},{8,9},{9,10},{10,1... | collective-permute-start | bytes 200 | tf_op jit(solution)/shard_map/while/body/eval_jaxpr/ppermute | solution.py:14
  25.7 6.9 %collective-permute-start.2 = (f32[16,1024]{1,0:T(8,128)S(1)}, f32[16,1024]{1,0:T(8,128)S(1)}, u32[]{:S(2)}, u32[]{:S(2)}) collective-permute-start(f32[16,1024]{1,0:T(8,128)S(1)} %bitcast_add_fusion.2), channel_id=1, source_target_pairs={{0,1},{1,2},{2,3},{3,4},{4,5},{5,6},{6,7},{7,8},{8,9},{9,10},{10,1... | collective-permute-start | bytes 196616 | tf_op jit(solution)/shard_map/while/body/eval_jaxpr/ppermute | solution.py:14
  25.8 6.8 %collective-permute-start = (bf16[16,1024]{1,0:T(8,128)(2,1)S(1)}, bf16[16,1024]{1,0:T(8,128)(2,1)S(1)}, u32[]{:S(2)}, u32[]{:S(2)}) collective-permute-start(bf16[16,1024]{1,0:T(8,128)(2,1)S(1)} %copy.64), channel_id=1, source_target_pairs={{0,1},{1,2},{2,3},{3,4},{4,5},{5,6},{6,7},{7,8},{8,9},{9,10},{10,1... | collective-permute-start | bytes 98312 | tf_op jit(solution)/shard_map/while/body/eval_jaxpr/ppermute | solution.py:14
  25.8 6.7 %collective-permute-start.1 = (s32[16]{0:T(128)S(1)}, s32[16]{0:T(128)S(1)}, u32[]{:S(2)}, u32[]{:S(2)}) collective-permute-start(s32[16]{0:T(128)S(1)} %copy.65), channel_id=1, source_target_pairs={{0,1},{1,2},{2,3},{3,4},{4,5},{5,6},{6,7},{7,8},{8,9},{9,10},{10,1... | collective-permute-start | bytes 200 | tf_op jit(solution)/shard_map/while/body/eval_jaxpr/ppermute | solution.py:14
  34.5 6.9 %collective-permute-start.2 = (f32[16,1024]{1,0:T(8,128)S(1)}, f32[16,1024]{1,0:T(8,128)S(1)}, u32[]{:S(2)}, u32[]{:S(2)}) collective-permute-start(f32[16,1024]{1,0:T(8,128)S(1)} %bitcast_add_fusion.2), channel_id=1, source_target_pairs={{0,1},{1,2},{2,3},{3,4},{4,5},{5,6},{6,7},{7,8},{8,9},{9,10},{10,1... | collective-permute-start | bytes 196616 | tf_op jit(solution)/shard_map/while/body/eval_jaxpr/ppermute | solution.py:14
  34.6 6.8 %collective-permute-start = (bf16[16,1024]{1,0:T(8,128)(2,1)S(1)}, bf16[16,1024]{1,0:T(8,128)(2,1)S(1)}, u32[]{:S(2)}, u32[]{:S(2)}) collective-permute-start(bf16[16,1024]{1,0:T(8,128)(2,1)S(1)} %copy.64), channel_id=1, source_target_pairs={{0,1},{1,2},{2,3},{3,4},{4,5},{5,6},{6,7},{7,8},{8,9},{9,10},{10,1... | collective-permute-start | bytes 98312 | tf_op jit(solution)/shard_map/while/body/eval_jaxpr/ppermute | solution.py:14
  34.6 6.7 %collective-permute-start.1 = (s32[16]{0:T(128)S(1)}, s32[16]{0:T(128)S(1)}, u32[]{:S(2)}, u32[]{:S(2)}) collective-permute-start(s32[16]{0:T(128)S(1)} %copy.65), channel_id=1, source_target_pairs={{0,1},{1,2},{2,3},{3,4},{4,5},{5,6},{6,7},{7,8},{8,9},{9,10},{10,1... | collective-permute-start | bytes 200 | tf_op jit(solution)/shard_map/while/body/eval_jaxpr/ppermute | solution.py:14
  43.3 6.9 %collective-permute-start.2 = (f32[16,1024]{1,0:T(8,128)S(1)}, f32[16,1024]{1,0:T(8,128)S(1)}, u32[]{:S(2)}, u32[]{:S(2)}) collective-permute-start(f32[16,1024]{1,0:T(8,128)S(1)} %bitcast_add_fusion.2), channel_id=1, source_target_pairs={{0,1},{1,2},{2,3},{3,4},{4,5},{5,6},{6,7},{7,8},{8,9},{9,10},{10,1... | collective-permute-start | bytes 196616 | tf_op jit(solution)/shard_map/while/body/eval_jaxpr/ppermute | solution.py:14
  43.4 6.8 %collective-permute-start = (bf16[16,1024]{1,0:T(8,128)(2,1)S(1)}, bf16[16,1024]{1,0:T(8,128)(2,1)S(1)}, u32[]{:S(2)}, u32[]{:S(2)}) collective-permute-start(bf16[16,1024]{1,0:T(8,128)(2,1)S(1)} %copy.64), channel_id=1, source_target_pairs={{0,1},{1,2},{2,3},{3,4},{4,5},{5,6},{6,7},{7,8},{8,9},{9,10},{10,1... | collective-permute-start | bytes 98312 | tf_op jit(solution)/shard_map/while/body/eval_jaxpr/ppermute | solution.py:14
  43.4 6.7 %collective-permute-start.1 = (s32[16]{0:T(128)S(1)}, s32[16]{0:T(128)S(1)}, u32[]{:S(2)}, u32[]{:S(2)}) collective-permute-start(s32[16]{0:T(128)S(1)} %copy.65), channel_id=1, source_target_pairs={{0,1},{1,2},{2,3},{3,4},{4,5},{5,6},{6,7},{7,8},{8,9},{9,10},{10,1... | collective-permute-start | bytes 200 | tf_op jit(solution)/shard_map/while/body/eval_jaxpr/ppermute | solution.py:14
  52.1 6.9 %collective-permute-start.2 = (f32[16,1024]{1,0:T(8,128)S(1)}, f32[16,1024]{1,0:T(8,128)S(1)}, u32[]{:S(2)}, u32[]{:S(2)}) collective-permute-start(f32[16,1024]{1,0:T(8,128)S(1)} %bitcast_add_fusion.2), channel_id=1, source_target_pairs={{0,1},{1,2},{2,3},{3,4},{4,5},{5,6},{6,7},{7,8},{8,9},{9,10},{10,1... | collective-permute-start | bytes 196616 | tf_op jit(solution)/shard_map/while/body/eval_jaxpr/ppermute | solution.py:14
  52.2 6.8 %collective-permute-start = (bf16[16,1024]{1,0:T(8,128)(2,1)S(1)}, bf16[16,1024]{1,0:T(8,128)(2,1)S(1)}, u32[]{:S(2)}, u32[]{:S(2)}) collective-permute-start(bf16[16,1024]{1,0:T(8,128)(2,1)S(1)} %copy.64), channel_id=1, source_target_pairs={{0,1},{1,2},{2,3},{3,4},{4,5},{5,6},{6,7},{7,8},{8,9},{9,10},{10,1... | collective-permute-start | bytes 98312 | tf_op jit(solution)/shard_map/while/body/eval_jaxpr/ppermute | solution.py:14
  52.3 6.7 %collective-permute-start.1 = (s32[16]{0:T(128)S(1)}, s32[16]{0:T(128)S(1)}, u32[]{:S(2)}, u32[]{:S(2)}) collective-permute-start(s32[16]{0:T(128)S(1)} %copy.65), channel_id=1, source_target_pairs={{0,1},{1,2},{2,3},{3,4},{4,5},{5,6},{6,7},{7,8},{8,9},{9,10},{10,1... | collective-permute-start | bytes 200 | tf_op jit(solution)/shard_map/while/body/eval_jaxpr/ppermute | solution.py:14
  60.9 6.9 %collective-permute-start.2 = (f32[16,1024]{1,0:T(8,128)S(1)}, f32[16,1024]{1,0:T(8,128)S(1)}, u32[]{:S(2)}, u32[]{:S(2)}) collective-permute-start(f32[16,1024]{1,0:T(8,128)S(1)} %bitcast_add_fusion.2), channel_id=1, source_target_pairs={{0,1},{1,2},{2,3},{3,4},{4,5},{5,6},{6,7},{7,8},{8,9},{9,10},{10,1... | collective-permute-start | bytes 196616 | tf_op jit(solution)/shard_map/while/body/eval_jaxpr/ppermute | solution.py:14
  61.0 6.8 %collective-permute-start = (bf16[16,1024]{1,0:T(8,128)(2,1)S(1)}, bf16[16,1024]{1,0:T(8,128)(2,1)S(1)}, u32[]{:S(2)}, u32[]{:S(2)}) collective-permute-start(bf16[16,1024]{1,0:T(8,128)(2,1)S(1)} %copy.64), channel_id=1, source_target_pairs={{0,1},{1,2},{2,3},{3,4},{4,5},{5,6},{6,7},{7,8},{8,9},{9,10},{10,1... | collective-permute-start | bytes 98312 | tf_op jit(solution)/shard_map/while/body/eval_jaxpr/ppermute | solution.py:14
  61.1 6.7 %collective-permute-start.1 = (s32[16]{0:T(128)S(1)}, s32[16]{0:T(128)S(1)}, u32[]{:S(2)}, u32[]{:S(2)}) collective-permute-start(s32[16]{0:T(128)S(1)} %copy.65), channel_id=1, source_target_pairs={{0,1},{1,2},{2,3},{3,4},{4,5},{5,6},{6,7},{7,8},{8,9},{9,10},{10,1... | collective-permute-start | bytes 200 | tf_op jit(solution)/shard_map/while/body/eval_jaxpr/ppermute | solution.py:14
  69.8 6.9 %collective-permute-start.2 = (f32[16,1024]{1,0:T(8,128)S(1)}, f32[16,1024]{1,0:T(8,128)S(1)}, u32[]{:S(2)}, u32[]{:S(2)}) collective-permute-start(f32[16,1024]{1,0:T(8,128)S(1)} %bitcast_add_fusion.2), channel_id=1, source_target_pairs={{0,1},{1,2},{2,3},{3,4},{4,5},{5,6},{6,7},{7,8},{8,9},{9,10},{10,1... | collective-permute-start | bytes 196616 | tf_op jit(solution)/shard_map/while/body/eval_jaxpr/ppermute | solution.py:14
  69.8 6.8 %collective-permute-start = (bf16[16,1024]{1,0:T(8,128)(2,1)S(1)}, bf16[16,1024]{1,0:T(8,128)(2,1)S(1)}, u32[]{:S(2)}, u32[]{:S(2)}) collective-permute-start(bf16[16,1024]{1,0:T(8,128)(2,1)S(1)} %copy.64), channel_id=1, source_target_pairs={{0,1},{1,2},{2,3},{3,4},{4,5},{5,6},{6,7},{7,8},{8,9},{9,10},{10,1... | collective-permute-start | bytes 98312 | tf_op jit(solution)/shard_map/while/body/eval_jaxpr/ppermute | solution.py:14
  69.9 6.7 %collective-permute-start.1 = (s32[16]{0:T(128)S(1)}, s32[16]{0:T(128)S(1)}, u32[]{:S(2)}, u32[]{:S(2)}) collective-permute-start(s32[16]{0:T(128)S(1)} %copy.65), channel_id=1, source_target_pairs={{0,1},{1,2},{2,3},{3,4},{4,5},{5,6},{6,7},{7,8},{8,9},{9,10},{10,1... | collective-permute-start | bytes 200 | tf_op jit(solution)/shard_map/while/body/eval_jaxpr/ppermute | solution.py:14
  78.6 6.9 %collective-permute-start.2 = (f32[16,1024]{1,0:T(8,128)S(1)}, f32[16,1024]{1,0:T(8,128)S(1)}, u32[]{:S(2)}, u32[]{:S(2)}) collective-permute-start(f32[16,1024]{1,0:T(8,128)S(1)} %bitcast_add_fusion.2), channel_id=1, source_target_pairs={{0,1},{1,2},{2,3},{3,4},{4,5},{5,6},{6,7},{7,8},{8,9},{9,10},{10,1... | collective-permute-start | bytes 196616 | tf_op jit(solution)/shard_map/while/body/eval_jaxpr/ppermute | solution.py:14
  78.6 6.8 %collective-permute-start = (bf16[16,1024]{1,0:T(8,128)(2,1)S(1)}, bf16[16,1024]{1,0:T(8,128)(2,1)S(1)}, u32[]{:S(2)}, u32[]{:S(2)}) collective-permute-start(bf16[16,1024]{1,0:T(8,128)(2,1)S(1)} %copy.64), channel_id=1, source_target_pairs={{0,1},{1,2},{2,3},{3,4},{4,5},{5,6},{6,7},{7,8},{8,9},{9,10},{10,1... | collective-permute-start | bytes 98312 | tf_op jit(solution)/shard_map/while/body/eval_jaxpr/ppermute | solution.py:14
  78.7 6.7 %collective-permute-start.1 = (s32[16]{0:T(128)S(1)}, s32[16]{0:T(128)S(1)}, u32[]{:S(2)}, u32[]{:S(2)}) collective-permute-start(s32[16]{0:T(128)S(1)} %copy.65), channel_id=1, source_target_pairs={{0,1},{1,2},{2,3},{3,4},{4,5},{5,6},{6,7},{7,8},{8,9},{9,10},{10,1... | collective-permute-start | bytes 200 | tf_op jit(solution)/shard_map/while/body/eval_jaxpr/ppermute | solution.py:14
  87.4 6.9 %collective-permute-start.2 = (f32[16,1024]{1,0:T(8,128)S(1)}, f32[16,1024]{1,0:T(8,128)S(1)}, u32[]{:S(2)}, u32[]{:S(2)}) collective-permute-start(f32[16,1024]{1,0:T(8,128)S(1)} %bitcast_add_fusion.2), channel_id=1, source_target_pairs={{0,1},{1,2},{2,3},{3,4},{4,5},{5,6},{6,7},{7,8},{8,9},{9,10},{10,1... | collective-permute-start | bytes 196616 | tf_op jit(solution)/shard_map/while/body/eval_jaxpr/ppermute | solution.py:14
  87.5 6.8 %collective-permute-start = (bf16[16,1024]{1,0:T(8,128)(2,1)S(1)}, bf16[16,1024]{1,0:T(8,128)(2,1)S(1)}, u32[]{:S(2)}, u32[]{:S(2)}) collective-permute-start(bf16[16,1024]{1,0:T(8,128)(2,1)S(1)} %copy.64), channel_id=1, source_target_pairs={{0,1},{1,2},{2,3},{3,4},{4,5},{5,6},{6,7},{7,8},{8,9},{9,10},{10,1... | collective-permute-start | bytes 98312 | tf_op jit(solution)/shard_map/while/body/eval_jaxpr/ppermute | solution.py:14
  87.5 6.7 %collective-permute-start.1 = (s32[16]{0:T(128)S(1)}, s32[16]{0:T(128)S(1)}, u32[]{:S(2)}, u32[]{:S(2)}) collective-permute-start(s32[16]{0:T(128)S(1)} %copy.65), channel_id=1, source_target_pairs={{0,1},{1,2},{2,3},{3,4},{4,5},{5,6},{6,7},{7,8},{8,9},{9,10},{10,1... | collective-permute-start | bytes 200 | tf_op jit(solution)/shard_map/while/body/eval_jaxpr/ppermute | solution.py:14
  96.2 6.9 %collective-permute-start.2 = (f32[16,1024]{1,0:T(8,128)S(1)}, f32[16,1024]{1,0:T(8,128)S(1)}, u32[]{:S(2)}, u32[]{:S(2)}) collective-permute-start(f32[16,1024]{1,0:T(8,128)S(1)} %bitcast_add_fusion.2), channel_id=1, source_target_pairs={{0,1},{1,2},{2,3},{3,4},{4,5},{5,6},{6,7},{7,8},{8,9},{9,10},{10,1... | collective-permute-start | bytes 196616 | tf_op jit(solution)/shard_map/while/body/eval_jaxpr/ppermute | solution.py:14
  96.3 6.8 %collective-permute-start = (bf16[16,1024]{1,0:T(8,128)(2,1)S(1)}, bf16[16,1024]{1,0:T(8,128)(2,1)S(1)}, u32[]{:S(2)}, u32[]{:S(2)}) collective-permute-start(bf16[16,1024]{1,0:T(8,128)(2,1)S(1)} %copy.64), channel_id=1, source_target_pairs={{0,1},{1,2},{2,3},{3,4},{4,5},{5,6},{6,7},{7,8},{8,9},{9,10},{10,1... | collective-permute-start | bytes 98312 | tf_op jit(solution)/shard_map/while/body/eval_jaxpr/ppermute | solution.py:14
  96.3 6.7 %collective-permute-start.1 = (s32[16]{0:T(128)S(1)}, s32[16]{0:T(128)S(1)}, u32[]{:S(2)}, u32[]{:S(2)}) collective-permute-start(s32[16]{0:T(128)S(1)} %copy.65), channel_id=1, source_target_pairs={{0,1},{1,2},{2,3},{3,4},{4,5},{5,6},{6,7},{7,8},{8,9},{9,10},{10,1... | collective-permute-start | bytes 200 | tf_op jit(solution)/shard_map/while/body/eval_jaxpr/ppermute | solution.py:14
  105.0 6.9 %collective-permute-start.2 = (f32[16,1024]{1,0:T(8,128)S(1)}, f32[16,1024]{1,0:T(8,128)S(1)}, u32[]{:S(2)}, u32[]{:S(2)}) collective-permute-start(f32[16,1024]{1,0:T(8,128)S(1)} %bitcast_add_fusion.2), channel_id=1, source_target_pairs={{0,1},{1,2},{2,3},{3,4},{4,5},{5,6},{6,7},{7,8},{8,9},{9,10},{10,1... | collective-permute-start | bytes 196616 | tf_op jit(solution)/shard_map/while/body/eval_jaxpr/ppermute | solution.py:14
  105.1 6.8 %collective-permute-start = (bf16[16,1024]{1,0:T(8,128)(2,1)S(1)}, bf16[16,1024]{1,0:T(8,128)(2,1)S(1)}, u32[]{:S(2)}, u32[]{:S(2)}) collective-permute-start(bf16[16,1024]{1,0:T(8,128)(2,1)S(1)} %copy.64), channel_id=1, source_target_pairs={{0,1},{1,2},{2,3},{3,4},{4,5},{5,6},{6,7},{7,8},{8,9},{9,10},{10,1... | collective-permute-start | bytes 98312 | tf_op jit(solution)/shard_map/while/body/eval_jaxpr/ppermute | solution.py:14
  105.2 6.7 %collective-permute-start.1 = (s32[16]{0:T(128)S(1)}, s32[16]{0:T(128)S(1)}, u32[]{:S(2)}, u32[]{:S(2)}) collective-permute-start(s32[16]{0:T(128)S(1)} %copy.65), channel_id=1, source_target_pairs={{0,1},{1,2},{2,3},{3,4},{4,5},{5,6},{6,7},{7,8},{8,9},{9,10},{10,1... | collective-permute-start | bytes 200 | tf_op jit(solution)/shard_map/while/body/eval_jaxpr/ppermute | solution.py:14
  113.8 6.9 %collective-permute-start.2 = (f32[16,1024]{1,0:T(8,128)S(1)}, f32[16,1024]{1,0:T(8,128)S(1)}, u32[]{:S(2)}, u32[]{:S(2)}) collective-permute-start(f32[16,1024]{1,0:T(8,128)S(1)} %bitcast_add_fusion.2), channel_id=1, source_target_pairs={{0,1},{1,2},{2,3},{3,4},{4,5},{5,6},{6,7},{7,8},{8,9},{9,10},{10,1... | collective-permute-start | bytes 196616 | tf_op jit(solution)/shard_map/while/body/eval_jaxpr/ppermute | solution.py:14
  113.9 6.8 %collective-permute-start = (bf16[16,1024]{1,0:T(8,128)(2,1)S(1)}, bf16[16,1024]{1,0:T(8,128)(2,1)S(1)}, u32[]{:S(2)}, u32[]{:S(2)}) collective-permute-start(bf16[16,1024]{1,0:T(8,128)(2,1)S(1)} %copy.64), channel_id=1, source_target_pairs={{0,1},{1,2},{2,3},{3,4},{4,5},{5,6},{6,7},{7,8},{8,9},{9,10},{10,1... | collective-permute-start | bytes 98312 | tf_op jit(solution)/shard_map/while/body/eval_jaxpr/ppermute | solution.py:14
  114.0 6.7 %collective-permute-start.1 = (s32[16]{0:T(128)S(1)}, s32[16]{0:T(128)S(1)}, u32[]{:S(2)}, u32[]{:S(2)}) collective-permute-start(s32[16]{0:T(128)S(1)} %copy.65), channel_id=1, source_target_pairs={{0,1},{1,2},{2,3},{3,4},{4,5},{5,6},{6,7},{7,8},{8,9},{9,10},{10,1... | collective-permute-start | bytes 200 | tf_op jit(solution)/shard_map/while/body/eval_jaxpr/ppermute | solution.py:14
  122.7 6.9 %collective-permute-start.2 = (f32[16,1024]{1,0:T(8,128)S(1)}, f32[16,1024]{1,0:T(8,128)S(1)}, u32[]{:S(2)}, u32[]{:S(2)}) collective-permute-start(f32[16,1024]{1,0:T(8,128)S(1)} %bitcast_add_fusion.2), channel_id=1, source_target_pairs={{0,1},{1,2},{2,3},{3,4},{4,5},{5,6},{6,7},{7,8},{8,9},{9,10},{10,1... | collective-permute-start | bytes 196616 | tf_op jit(solution)/shard_map/while/body/eval_jaxpr/ppermute | solution.py:14
  122.7 6.8 %collective-permute-start = (bf16[16,1024]{1,0:T(8,128)(2,1)S(1)}, bf16[16,1024]{1,0:T(8,128)(2,1)S(1)}, u32[]{:S(2)}, u32[]{:S(2)}) collective-permute-start(bf16[16,1024]{1,0:T(8,128)(2,1)S(1)} %copy.64), channel_id=1, source_target_pairs={{0,1},{1,2},{2,3},{3,4},{4,5},{5,6},{6,7},{7,8},{8,9},{9,10},{10,1... | collective-permute-start | bytes 98312 | tf_op jit(solution)/shard_map/while/body/eval_jaxpr/ppermute | solution.py:14
  122.8 6.7 %collective-permute-start.1 = (s32[16]{0:T(128)S(1)}, s32[16]{0:T(128)S(1)}, u32[]{:S(2)}, u32[]{:S(2)}) collective-permute-start(s32[16]{0:T(128)S(1)} %copy.65), channel_id=1, source_target_pairs={{0,1},{1,2},{2,3},{3,4},{4,5},{5,6},{6,7},{7,8},{8,9},{9,10},{10,1... | collective-permute-start | bytes 200 | tf_op jit(solution)/shard_map/while/body/eval_jaxpr/ppermute | solution.py:14
  131.5 6.9 %collective-permute-start.2 = (f32[16,1024]{1,0:T(8,128)S(1)}, f32[16,1024]{1,0:T(8,128)S(1)}, u32[]{:S(2)}, u32[]{:S(2)}) collective-permute-start(f32[16,1024]{1,0:T(8,128)S(1)} %bitcast_add_fusion.2), channel_id=1, source_target_pairs={{0,1},{1,2},{2,3},{3,4},{4,5},{5,6},{6,7},{7,8},{8,9},{9,10},{10,1... | collective-permute-start | bytes 196616 | tf_op jit(solution)/shard_map/while/body/eval_jaxpr/ppermute | solution.py:14
  131.5 6.8 %collective-permute-start = (bf16[16,1024]{1,0:T(8,128)(2,1)S(1)}, bf16[16,1024]{1,0:T(8,128)(2,1)S(1)}, u32[]{:S(2)}, u32[]{:S(2)}) collective-permute-start(bf16[16,1024]{1,0:T(8,128)(2,1)S(1)} %copy.64), channel_id=1, source_target_pairs={{0,1},{1,2},{2,3},{3,4},{4,5},{5,6},{6,7},{7,8},{8,9},{9,10},{10,1... | collective-permute-start | bytes 98312 | tf_op jit(solution)/shard_map/while/body/eval_jaxpr/ppermute | solution.py:14
  131.6 6.7 %collective-permute-start.1 = (s32[16]{0:T(128)S(1)}, s32[16]{0:T(128)S(1)}, u32[]{:S(2)}, u32[]{:S(2)}) collective-permute-start(s32[16]{0:T(128)S(1)} %copy.65), channel_id=1, source_target_pairs={{0,1},{1,2},{2,3},{3,4},{4,5},{5,6},{6,7},{7,8},{8,9},{9,10},{10,1... | collective-permute-start | bytes 200 | tf_op jit(solution)/shard_map/while/body/eval_jaxpr/ppermute | solution.py:14
  140.3 6.9 %collective-permute-start.2 = (f32[16,1024]{1,0:T(8,128)S(1)}, f32[16,1024]{1,0:T(8,128)S(1)}, u32[]{:S(2)}, u32[]{:S(2)}) collective-permute-start(f32[16,1024]{1,0:T(8,128)S(1)} %bitcast_add_fusion.2), channel_id=1, source_target_pairs={{0,1},{1,2},{2,3},{3,4},{4,5},{5,6},{6,7},{7,8},{8,9},{9,10},{10,1... | collective-permute-start | bytes 196616 | tf_op jit(solution)/shard_map/while/body/eval_jaxpr/ppermute | solution.py:14
  140.4 6.8 %collective-permute-start = (bf16[16,1024]{1,0:T(8,128)(2,1)S(1)}, bf16[16,1024]{1,0:T(8,128)(2,1)S(1)}, u32[]{:S(2)}, u32[]{:S(2)}) collective-permute-start(bf16[16,1024]{1,0:T(8,128)(2,1)S(1)} %copy.64), channel_id=1, source_target_pairs={{0,1},{1,2},{2,3},{3,4},{4,5},{5,6},{6,7},{7,8},{8,9},{9,10},{10,1... | collective-permute-start | bytes 98312 | tf_op jit(solution)/shard_map/while/body/eval_jaxpr/ppermute | solution.py:14
  140.4 6.7 %collective-permute-start.1 = (s32[16]{0:T(128)S(1)}, s32[16]{0:T(128)S(1)}, u32[]{:S(2)}, u32[]{:S(2)}) collective-permute-start(s32[16]{0:T(128)S(1)} %copy.65), channel_id=1, source_target_pairs={{0,1},{1,2},{2,3},{3,4},{4,5},{5,6},{6,7},{7,8},{8,9},{9,10},{10,1... | collective-permute-start | bytes 200 | tf_op jit(solution)/shard_map/while/body/eval_jaxpr/ppermute | solution.py:14
  149.1 6.9 %collective-permute-start.2 = (f32[16,1024]{1,0:T(8,128)S(1)}, f32[16,1024]{1,0:T(8,128)S(1)}, u32[]{:S(2)}, u32[]{:S(2)}) collective-permute-start(f32[16,1024]{1,0:T(8,128)S(1)} %bitcast_add_fusion.2), channel_id=1, source_target_pairs={{0,1},{1,2},{2,3},{3,4},{4,5},{5,6},{6,7},{7,8},{8,9},{9,10},{10,1... | collective-permute-start | bytes 196616 | tf_op jit(solution)/shard_map/while/body/eval_jaxpr/ppermute | solution.py:14
  149.2 6.8 %collective-permute-start = (bf16[16,1024]{1,0:T(8,128)(2,1)S(1)}, bf16[16,1024]{1,0:T(8,128)(2,1)S(1)}, u32[]{:S(2)}, u32[]{:S(2)}) collective-permute-start(bf16[16,1024]{1,0:T(8,128)(2,1)S(1)} %copy.64), channel_id=1, source_target_pairs={{0,1},{1,2},{2,3},{3,4},{4,5},{5,6},{6,7},{7,8},{8,9},{9,10},{10,1... | collective-permute-start | bytes 98312 | tf_op jit(solution)/shard_map/while/body/eval_jaxpr/ppermute | solution.py:14
  149.2 6.7 %collective-permute-start.1 = (s32[16]{0:T(128)S(1)}, s32[16]{0:T(128)S(1)}, u32[]{:S(2)}, u32[]{:S(2)}) collective-permute-start(s32[16]{0:T(128)S(1)} %copy.65), channel_id=1, source_target_pairs={{0,1},{1,2},{2,3},{3,4},{4,5},{5,6},{6,7},{7,8},{8,9},{9,10},{10,1... | collective-permute-start | bytes 200 | tf_op jit(solution)/shard_map/while/body/eval_jaxpr/ppermute | solution.py:14
  (6 other events, 317.2 us)
where the time goes:
time: 161 us; the launch traced here: 160 us
  waiting for transfers between devices  106 us (66%)
  matrix products  38.2 us (24%)
  other arithmetic  6.28 us (4%)
  starting transfers between devices  5.84 us (4%)
  local copies, waits for them, and re-layouts  2.2 us (1%)
    ppermute x48, waiting for transfers between devices, shifted(): lax.ppermute(shard, axis, [(i, (i + by) % size) for i in range(size)])  106 us
    dot_general x16, matrix products, attend(): jnp.einsum('hrk,khd->rhd', weight, v_h, preferred_element_type=jnp.float32)  28.7 us
    ppermute x48, starting transfers between devices, shifted(): lax.ppermute(shard, axis, [(i, (i + by) % size) for i in range(size)])  5.84 us
    dot_general x1, matrix products, on_device(): jnp.dot(cand_norm, w_proj, preferred_element_type=jnp.float32)  4.81 us
  transfers between devices with their start and end apart: 48, of which 16 were waited for; matrix products, arithmetic and copies ran while one was open for 0% of the time, Pallas kernels for 0%

commit v1 on v0

v1 whole, which is shorter than its diff:
```python
import jax
import jax.numpy as jnp
from jax import lax
from jax.experimental import pallas as pl
from jax.experimental.pallas import tpu as pltpu
from jax.sharding import PartitionSpec as P


HEADS = 8
EPS = 1e-06
EXTRA = 128
STEPS = 32000.0
GRANT = 8 * 1024 * 1024
PARAMS = pltpu.CompilerParams(vmem_limit_bytes=GRANT)


def swapped(shard, axis, mask):
    size = lax.axis_size(axis)
    return lax.ppermute(shard, axis, [(i, i ^ mask) for i in range(size)])


def norm(rows):
    centred = rows - jnp.mean(rows, axis=-1, keepdims=True)
    spread = jnp.mean(centred * centred, axis=-1, keepdims=True)
    return centred * lax.rsqrt(spread + EPS)


def silu(x):
    half = x * 0.5
    return half + half * jnp.tanh(half)


def whole():
    return pl.BlockSpec(memory_space=pltpu.VMEM)


def encode(rows, out_ref):
    count, width = rows.shape
    top = jnp.max(jnp.abs(rows), axis=-1, keepdims=True)
    exponent = jnp.ceil(jnp.log2(jnp.maximum(top, 1e-30)))
    code = jnp.round(rows * (STEPS * jnp.exp2(-exponent)))
    out_ref[:, :width] = code.astype(jnp.int32).astype(jnp.int16)
    out_ref[:, width:] = (
        jnp.broadcast_to(exponent, (count, EXTRA)).astype(jnp.int32).astype(jnp.int16)
    )


def decode(code, width):
    code = code.astype(jnp.int32).astype(jnp.float32)
    return code[:, :width] * (jnp.exp2(code[:, width : width + 1]) * (1 / STEPS))


def pack_kernel(length_ref, cand_ref, visible_ref, out_ref):
    rows, width = cand_ref.shape
    out_ref[:, :width] = norm(cand_ref[...].astype(jnp.float32)).astype(jnp.bfloat16)
    seen = jnp.broadcast_to(visible_ref[...], (rows, rows))
    diagonal = lax.broadcasted_iota(jnp.int32, (rows, rows), 0) == lax.broadcasted_iota(
        jnp.int32, (rows, rows), 1
    )
    limit = jnp.minimum(seen, length_ref[0]).astype(jnp.float32)
    limit = jnp.sum(jnp.where(diagonal, limit, 0.0), axis=1, keepdims=True)
    high = jnp.floor(limit * (1 / 256))
    low = limit - high * 256
    lane = lax.broadcasted_iota(jnp.int32, (rows, EXTRA), 1)
    out_ref[:, width:] = jnp.where(lane == 0, high, low).astype(jnp.bfloat16)


def pack(candidates, hist_length, visible):
    rows, width = candidates.shape
    return pl.pallas_call(
        pack_kernel,
        out_shape=jax.ShapeDtypeStruct((rows, width + EXTRA), jnp.bfloat16),
        in_specs=[pl.BlockSpec(memory_space=pltpu.SMEM), whole(), whole()],
        out_specs=whole(),
        compiler_params=PARAMS,
        name="pack",
    )(hist_length, candidates, visible.reshape(1, rows))


def limits_of(packed, width):
    high = packed[:, width : width + 1].astype(jnp.float32)
    low = packed[:, width + 1 : width + 2].astype(jnp.float32)
    return high * 256 + low


def project_kernel(first, tile, hist_ref, packed_ref, w_ref, out_ref, self_ref, rows_ref):
    n_keys, width = hist_ref.shape
    rows_ref[:n_keys] = norm(hist_ref[...].astype(jnp.float32)).astype(jnp.bfloat16)
    rows_ref[n_keys:] = packed_ref[:, :width]
    for start in range(0, width, tile):
        made = silu(
            jnp.dot(
                rows_ref[...],
                w_ref[:, first + start : first + start + tile],
                preferred_element_type=jnp.float32,
            )
        ).astype(jnp.bfloat16)
        out_ref[:, start : start + tile] = made[:n_keys]
        self_ref[:, start : start + tile] = made[n_keys:]


def project(history, packed, w_proj, first):
    n_keys, width = history.shape
    rows = packed.shape[0]
    tile = min(256, width)

    def body(*refs):
        project_kernel(first, tile, *refs)

    return pl.pallas_call(
        body,
        out_shape=(
            jax.ShapeDtypeStruct((n_keys, width), jnp.bfloat16),
            jax.ShapeDtypeStruct((rows, width), jnp.bfloat16),
        ),
        in_specs=[whole()] * 3,
        out_specs=(whole(), whole()),
        scratch_shapes=[pltpu.VMEM((n_keys + rows, width), jnp.bfloat16)],
        cost_estimate=pl.CostEstimate(
            flops=2 * (n_keys + rows) * width * width,
            bytes_accessed=4 * width * width,
            transcendentals=(n_keys + rows) * width,
        ),
        compiler_params=PARAMS,
    )(history, packed, w_proj)


def attend_kernel(heads, coded, base_ref, packed_ref, w_ref, k0, v0, k1, v1, out_ref, acc_ref):
    n_keys, width = k0.shape
    size = width // heads
    rows = packed_ref.shape[0]
    limit = limits_of(packed_ref[...], width)
    inverse = 1.0 / (limit + 1.0)
    position = lax.broadcasted_iota(jnp.int32, (rows, n_keys), 1).astype(jnp.float32)
    share = []
    for side in range(2):
        base = base_ref[side].astype(jnp.float32)
        share.append(jnp.where(position + base < limit, inverse, 0.0))
    pair = 2 * size
    for start in range(0, width, pair):
        query = silu(
            jnp.dot(
                packed_ref[:, :width],
                w_ref[:, width + start : width + start + pair],
                preferred_element_type=jnp.float32,
            )
        ).astype(jnp.bfloat16)
        for sub in range(0, pair, size):
            cols = slice(start + sub, start + sub + size)
            total = None
            for side, (k, v) in enumerate(((k0, v0), (k1, v1))):
                scores = lax.dot_general(
                    query[:, sub : sub + size],
                    k[:, cols],
                    (((1,), (1,)), ((), ())),
                    preferred_element_type=jnp.float32,
                )
                weight = (silu(scores * size ** (-0.5)) * share[side]).astype(jnp.bfloat16)
                part = jnp.dot(weight, v[:, cols], preferred_element_type=jnp.float32)
                total = part if total is None else total + part
            acc_ref[:, cols] = total
    made = acc_ref[...]
    made = made - jnp.mean(made, axis=-1, keepdims=True)
    if coded:
        encode(made, out_ref)
    else:
        out_ref[...] = made


def attend(bases, packed, w_proj, k0, v0, k1, v1, heads, coded):
    rows = packed.shape[0]
    n_keys, width = k0.shape

    def body(*refs):
        attend_kernel(heads, coded, *refs)

    return pl.pallas_call(
        body,
        out_shape=jax.ShapeDtypeStruct((rows, width + EXTRA), jnp.int16)
        if coded
        else jax.ShapeDtypeStruct((rows, width), jnp.float32),
        in_specs=[pl.BlockSpec(memory_space=pltpu.SMEM)] + [whole()] * 6,
        out_specs=whole(),
        scratch_shapes=[pltpu.VMEM((rows, width), jnp.float32)],
        cost_estimate=pl.CostEstimate(
            flops=2 * rows * width * (width + 4 * n_keys),
            bytes_accessed=4 * width * width,
            transcendentals=rows * width * 2 * n_keys // 128,
        ),
        compiler_params=PARAMS,
    )(bases, packed, w_proj, k0, v0, k1, v1)


def own_kernel(heads, packed_ref, w_ref, key_ref, value_ref, gate_ref, term_ref):
    _, width = key_ref.shape
    size = width // heads
    both = silu(
        jnp.dot(
            packed_ref[:, :width], w_ref[:, : 2 * width], preferred_element_type=jnp.float32
        )
    ).astype(jnp.bfloat16)
    gate_ref[...] = both[:, :width]
    query = both[:, width:].astype(jnp.float32)
    inverse = 1.0 / (limits_of(packed_ref[...], width) + 1.0)
    products = query * key_ref[...].astype(jnp.float32)
    for head in range(heads):
        cols = slice(head * size, (head + 1) * size)
        score = jnp.sum(products[:, cols], axis=-1, keepdims=True)
        weight = (silu(score * size ** (-0.5)) * inverse).astype(jnp.bfloat16)
        term_ref[:, cols] = weight.astype(jnp.float32) * value_ref[:, cols].astype(jnp.float32)


def own(packed, w_proj, self_key, self_value, heads):
    rows, width = self_key.shape

    def body(*refs):
        own_kernel(heads, *refs)

    return pl.pallas_call(
        body,
        out_shape=(
            jax.ShapeDtypeStruct((rows, width), jnp.bfloat16),
            jax.ShapeDtypeStruct((rows, width), jnp.float32),
        ),
        in_specs=[whole()] * 4,
        out_specs=(whole(), whole()),
        cost_estimate=pl.CostEstimate(
            flops=4 * rows * width * width,
            bytes_accessed=4 * width * width,
            transcendentals=rows * width,
        ),
        compiler_params=PARAMS,
        name="own",
    )(packed, w_proj, self_key, self_value)


def finish_kernel(cand_ref, kept_ref, got_ref, term_ref, gate_ref, w_ref, out_ref):
    attended = kept_ref[...] + decode(got_ref[...], kept_ref.shape[1]) + term_ref[...]
    mixed = (norm(attended) * gate_ref[...].astype(jnp.float32)).astype(jnp.bfloat16)
    out_ref[...] = (
        cand_ref[...].astype(jnp.float32)
        + jnp.dot(mixed, w_ref[...], preferred_element_type=jnp.float32)
    ).astype(jnp.bfloat16)


def finish(candidates, kept, got, term, gate, w_out):
    return pl.pallas_call(
        finish_kernel,
        out_shape=jax.ShapeDtypeStruct(candidates.shape, jnp.bfloat16),
        in_specs=[whole()] * 6,
        out_specs=whole(),
        compiler_params=PARAMS,
        name="finish",
    )(candidates, kept, got, term, gate, w_out)


def combine_kernel(kept_ref, got_ref, sent_ref, out_ref):
    half, width = out_ref.shape
    encode(kept_ref[half:] + decode(got_ref[half:], width), sent_ref)
    out_ref[...] = kept_ref[:half] + decode(got_ref[:half], width)


def combine(kept, got):
    half, width = kept.shape[0] // 2, kept.shape[1]
    return pl.pallas_call(
        combine_kernel,
        out_shape=(
            jax.ShapeDtypeStruct((half, width + EXTRA), jnp.int16),
            jax.ShapeDtypeStruct((half, width), jnp.float32),
        ),
        in_specs=[whole()] * 2,
        out_specs=(whole(), whole()),
        compiler_params=PARAMS,
        name="combine",
    )(kept, got)


def layer(history, candidates, hist_length, visible, w_proj, w_out):
    width = w_out.shape[0]
    n_keys = history.shape[0]
    size = lax.axis_size("hist")
    me = lax.axis_index("hist")
    masks = []
    bit = size // 2
    while bit > 1:
        masks.append(bit | 1)
        bit //= 2
    bases = jnp.stack([me, me ^ 1]).astype(jnp.int32) * n_keys
    packed = pack(candidates, hist_length, visible)
    keys, self_key = project(history, packed, w_proj, 2 * width)
    values, self_value = project(history, packed, w_proj, 3 * width)
    other_keys = swapped(keys, "hist", 1)
    other_values = swapped(values, "hist", 1)
    gathered = packed
    for mask in masks[:-1]:
        got = swapped(gathered, "hist", mask)
        gathered = jnp.concatenate([gathered, got], axis=0)
    far = swapped(gathered, "hist", masks[-1])
    shards = (w_proj, keys, values, other_keys, other_values)
    kept = attend(bases, gathered, *shards, HEADS, False)
    sent = attend(bases, far, *shards, HEADS, True)
    gate, term = own(packed, w_proj, self_key, self_value, HEADS)
    got = swapped(sent, "hist", masks[-1])
    for mask in masks[-2::-1]:
        sent, kept = combine(kept, got)
        got = swapped(sent, "hist", mask)
    return finish(candidates, kept, got, term, gate, w_out)


def solution(mesh):
    in_specs = (
        P(("groups", "hist"), None),
        P(("groups", "hist"), None),
        P("groups"),
        P(("groups", "hist")),
        P(),
        P(),
    )
    out_specs = P(("groups", "hist"), None)
    return jax.shard_map(
        layer, mesh=mesh, in_specs=in_specs, out_specs=out_specs, check_vma=False
    )
```

time: 161 us -> 52.5 us (0.33)
  waiting for transfers between devices: 106 us -> 11.2 us
  matrix products: 38.2 us -> 0 us
  Pallas kernels: 0 us -> 15.4 us
  starting transfers between devices: 5.84 us -> 15.3 us
  local copies, waits for them, and re-layouts: 2.2 us -> 9.42 us
  other arithmetic: 6.28 us -> 0.1 us
    ppermute x48 -> x8, waiting for transfers between devices: 106 us -> 11.2 us  [swapped(): return lax.ppermute(shard, axis, [(i, i ^ mask) for i in range(size)])]
    dot_general x19 -> x0, matrix products: 38.2 us -> none  [the longest x16 28.7 us: attend(): jnp.einsum('hrk,khd->rhd', weight, v_h, preferred_element_type=jnp.float32)]
    pallas_call x0 -> x9, Pallas kernels: none -> 15.4 us  [the longest x2 9.04 us: attend(): pl.pallas_call(body, out_shape=jax.ShapeDtypeStruct((rows, width + EXTRA)...]
    ppermute x48 -> x8, starting transfers between devices: 5.84 us -> 15.3 us  [swapped(): return lax.ppermute(shard, axis, [(i, i ^ mask) for i in range(size)])]
    unnamed x13 -> x18, local copies, waits for them, and re-layouts: 0.69 us -> 9.42 us
    reduce_sum x7 -> x0, other arithmetic: 3.79 us -> none  [the longest x3 2.15 us: layer_norm(): centred = rows - jnp.mean(rows, axis=-1, keepdims=True)]
  transfers between devices with their start and end apart: 48 -> 8, of which waited for: 16 -> 5; matrix products, arithmetic and copies ran while one was open for 0% -> 0% of each run, Pallas kernels for 0% -> 14%
where the time goes in v1:
time: 52.5 us; the launch traced here: 52.1 us
  Pallas kernels  15.4 us (29%)
  starting transfers between devices  15.3 us (29%)
  waiting for transfers between devices  11.2 us (21%)
  local copies, waits for them, and re-layouts  9.42 us (18%)
  between operations  0.77 us (1%)
    ppermute x8, starting transfers between devices, swapped(): return lax.ppermute(shard, axis, [(i, i ^ mask) for i in range(size)])  15.3 us
    ppermute x8, waiting for transfers between devices, swapped(): return lax.ppermute(shard, axis, [(i, i ^ mask) for i in range(size)])  11.2 us
    unnamed x18, local copies, waits for them, and re-layouts  9.42 us
    pallas_call x2, Pallas kernels, attend(): pl.pallas_call(body, out_shape=jax.ShapeDtypeStruct((rows, width + EXTRA)...  9.04 us
    pallas_call x2, Pallas kernels, project(): pl.pallas_call(body, out_shape=(jax.ShapeDtypeStruct((n_keys, width), jnp...  3.71 us
    pallas_call x1, Pallas kernels, finish(): pl.pallas_call(finish_kernel, out_shape=jax.ShapeDtypeStruct(candidates.s...  1.23 us
  transfers between devices with their start and end apart: 8, of which 5 were waited for; matrix products, arithmetic and copies ran while one was open for 0% of the time, Pallas kernels for 14%

profile of v1, /device:TPU:0, one launch (start us, length us, event | category | flops | bytes accessed | tf_op | source)
XLA Modules:
  0.0 52.1 jit_solution(13137525008123303817)
XLA Ops:
  0.7 0.0 copy-start.4
  0.7 0.7 %copy-done.4 = bf16[16,1024]{1,0:T(8,128)(2,1)S(1)} copy-done((bf16[16,1024]{1,0:T(8,128)(2,1)S(1)}, bf16[16,1024]{1,0:T(8,128)(2,1)}, u32[]{:S(2)}) %copy-start.4) | copy-done | bytes 32792
  1.4 0.0 copy-start.6
  1.4 0.7 %copy-done.6 = s32[16]{0:T(128)S(1)} copy-done((s32[16]{0:T(128)S(1)}, s32[16]{0:T(128)}, u32[]{:S(2)}) %copy-start.6) | copy-done | bytes 88
  2.1 0.2 pack.1.refs_1_.refs_0_
  2.3 0.0 copy-start
  2.3 3.4 %copy-done = bf16[1024,4096]{1,0:T(8,128)(2,1)S(1)} copy-done((bf16[1024,4096]{1,0:T(8,128)(2,1)S(1)}, bf16[1024,4096]{1,0:T(8,128)(2,1)}, u32[]{:S(2)}) %copy-start) | copy-done | bytes 8388632
  5.6 0.0 copy-start.2
  5.6 1.2 %copy-done.2 = bf16[512,1024]{1,0:T(8,128)(2,1)S(1)} copy-done((bf16[512,1024]{1,0:T(8,128)(2,1)S(1)}, bf16[512,1024]{1,0:T(8,128)(2,1)}, u32[]{:S(2)}) %copy-start.2) | copy-done | bytes 1048600
  6.9 1.9 %shard_map.65 = (bf16[512,1024]{1,0:T(8,128)(2,1)S(1)}, bf16[16,1024]{1,0:T(8,128)(2,1)S(1)}) custom-call(bf16[512,1024]{1,0:T(8,128)(2,1)S(1)} %copy-done.2, bf16[16,1152]{1,0:T(8,128)(2,1)S(1)} %pack.1.refs_1_.refs_0_, bf16[1024,4096]{1,0:T(8,128)(2,1)S(1)} %copy-done), custom_call_target="tpu_custom_call" | custom-call | flops 1107296256 | bytes 4194304 | tf_op jit(solution)/shard_map/pallas_call | solution.py:110
  8.7 0.6 %collective-permute-start.3 = (bf16[512,1024]{1,0:T(8,128)(2,1)S(1)}, bf16[512,1024]{1,0:T(8,128)(2,1)S(1)}, u32[]{:S(2)}, u32[]{:S(2)}) collective-permute-start(bf16[512,1024]{1,0:T(8,128)(2,1)S(1)} %get-tuple-element.16.refs_4_), channel_id=1, source_target_pairs={{0,1},{1,0},{2,3},{3,2},{4,5},{5,4},{6,7},{7,6},{8,9},{9,8},{10,11... | collective-permute-start | bytes 3145736 | tf_op jit(solution)/shard_map/ppermute | solution.py:19
  9.3 1.9 %shard_map.64 = (bf16[512,1024]{1,0:T(8,128)(2,1)S(1)}, bf16[16,1024]{1,0:T(8,128)(2,1)S(1)}) custom-call(bf16[512,1024]{1,0:T(8,128)(2,1)S(1)} %copy-done.2, bf16[16,1152]{1,0:T(8,128)(2,1)S(1)} %pack.1.refs_1_.refs_0_, bf16[1024,4096]{1,0:T(8,128)(2,1)S(1)} %copy-done), custom_call_target="tpu_custom_call" | custom-call | flops 1107296256 | bytes 4194304 | tf_op jit(solution)/shard_map/pallas_call | solution.py:110
  11.1 0.1 collective-permute-start.2
  11.2 3.7 %collective-permute-start = (bf16[16,1152]{1,0:T(8,128)(2,1)S(1)}, bf16[16,1152]{1,0:T(8,128)(2,1)S(1)}, u32[]{:S(2)}, u32[]{:S(2)}) collective-permute-start(bf16[16,1152]{1,0:T(8,128)(2,1)S(1)} %pack.1.refs_1_.refs_0_), channel_id=1, source_target_pairs={{0,9},{1,8},{2,11},{3,10},{4,13},{5,12},{6,15},{7,14},{8,1},{9,0},... | collective-permute-start | bytes 110600 | tf_op jit(solution)/shard_map/ppermute | solution.py:19
  15.0 1.6 %collective-permute-done = bf16[16,1152]{1,0:T(8,128)(2,1)S(1)} collective-permute-done((bf16[16,1152]{1,0:T(8,128)(2,1)S(1)}, bf16[16,1152]{1,0:T(8,128)(2,1)S(1)}, u32[]{:S(2)}, u32[]{:S(2)}) %collective-permute-start) | collective-permute-done | bytes 36896 | tf_op jit(solution)/shard_map/ppermute | solution.py:19
  16.6 1.8 %collective-permute-start.1 = (bf16[32,1152]{1,0:T(8,128)(2,1)S(1)}, bf16[32,1152]{1,0:T(8,128)(2,1)S(1)}, u32[]{:S(2)}, u32[]{:S(2)}) collective-permute-start(bf16[32,1152]{1,0:T(8,128)(2,1)S(1)} %pad_maximum_fusion.1), channel_id=1, source_target_pairs={{0,5},{1,4},{2,7},{3,6},{4,1},{5,0},{6,3},{7,2},{8,13},{9,12},{10,... | collective-permute-start | bytes 221192 | tf_op jit(solution)/shard_map/ppermute | solution.py:19
  18.4 2.5 %collective-permute-done.1 = bf16[32,1152]{1,0:T(8,128)(2,1)S(1)} collective-permute-done((bf16[32,1152]{1,0:T(8,128)(2,1)S(1)}, bf16[32,1152]{1,0:T(8,128)(2,1)S(1)}, u32[]{:S(2)}, u32[]{:S(2)}) %collective-permute-start.1) | collective-permute-done | bytes 73760 | tf_op jit(solution)/shard_map/ppermute | solution.py:19
  21.0 1.8 %collective-permute-start.4 = (bf16[64,1152]{1,0:T(8,128)(2,1)S(1)}, bf16[64,1152]{1,0:T(8,128)(2,1)S(1)}, u32[]{:S(2)}, u32[]{:S(2)}) collective-permute-start(bf16[64,1152]{1,0:T(8,128)(2,1)S(1)} %pad_maximum_fusion.refs_1_), channel_id=1, source_target_pairs={{0,3},{1,2},{2,1},{3,0},{4,7},{5,6},{6,5},{7,4},{8,11},{9,10},{10,... | collective-permute-start | bytes 442376 | tf_op jit(solution)/shard_map/ppermute | solution.py:19
  22.7 0.1 add_multiply_fusion.refs_0_
  22.8 3.9 %collective-permute-done.4.refs_1_ = bf16[64,1152]{1,0:T(8,128)(2,1)S(1)} collective-permute-done((bf16[64,1152]{1,0:T(8,128)(2,1)S(1)}, bf16[64,1152]{1,0:T(8,128)(2,1)S(1)}, u32[]{:S(2)}, u32[]{:S(2)}) %collective-permute-start.4) | collective-permute-done | bytes 147488 | tf_op jit(solution)/shard_map/ppermute | solution.py:19
  26.7 0.0 collective-permute-done.3.refs_6_
  26.7 0.0 collective-permute-done.2.refs_5_
  26.7 0.0 copy-start.1
  26.7 3.4 %copy-done.1 = bf16[1024,4096]{1,0:T(8,128)(2,1)S(1)} copy-done((bf16[1024,4096]{1,0:T(8,128)(2,1)S(1)}, bf16[1024,4096]{1,0:T(8,128)(2,1)}, u32[]{:S(2)}) %copy-start.1) | copy-done | bytes 8388632
  30.1 0.0 slice-start
  30.1 4.6 %shard_map.67 = s16[64,1152]{1,0:T(8,128)(2,1)S(1)} custom-call(s32[2]{0:T(128)S(1)} %add_multiply_fusion.refs_0_, bf16[64,1152]{1,0:T(8,128)(2,1)S(1)} %collective-permute-done.4.refs_1_, bf16[1024,4096]{1,0:T(8,128)(2,1)S(1)} %copy-done.1, bf16[512,1024]{1,0:T(8,128)(2,1)S(1)} %get-tuple-element.15.refs_3_, ...), custom_call_target="tpu_custom_call" | custom-call | flops 402653184 | bytes 4194304 | tf_op jit(solution)/shard_map/pallas_call | solution.py:177
  34.7 0.0 slice-start.1
  34.7 0.0 copy-start.3
  34.7 0.0 copy-start.5
  34.8 2.0 %collective-permute-start.5 = (s16[64,1152]{1,0:T(8,128)(2,1)S(1)}, s16[64,1152]{1,0:T(8,128)(2,1)S(1)}, u32[]{:S(2)}, u32[]{:S(2)}) collective-permute-start(s16[64,1152]{1,0:T(8,128)(2,1)S(1)} %shard_map.67), channel_id=1, source_target_pairs={{0,3},{1,2},{2,1},{3,0},{4,7},{5,6},{6,5},{7,4},{8,11},{9,10},{10,... | collective-permute-start | bytes 442376 | tf_op jit(solution)/shard_map/ppermute | solution.py:19
  36.7 4.4 %shard_map.66.kept_ref = f32[64,1024]{1,0:T(8,128)S(1)} custom-call(s32[2]{0:T(128)S(1)} %add_multiply_fusion.refs_0_, bf16[64,1152]{1,0:T(8,128)(2,1)S(1)} %pad_maximum_fusion.refs_1_, bf16[1024,4096]{1,0:T(8,128)(2,1)S(1)} %copy-done.1, bf16[512,1024]{1,0:T(8,128)(2,1)S(1)} %get-tuple-element.15.refs_3_, bf16[512,1024]{1,0:T(8,128)(2,1)S(1)} %get-tuple-element.16.refs_4_, ...), custom_call_target="tpu_custom_call" | custom-call | flops 402653184 | bytes 4194304 | tf_op jit(solution)/shard_map/pallas_call | solution.py:177
  41.1 0.0 collective-permute-done.5.got_ref
  41.1 0.2 combine.2
  41.3 2.2 %collective-permute-start.6 = (s16[32,1152]{1,0:T(8,128)(2,1)S(1)}, s16[32,1152]{1,0:T(8,128)(2,1)S(1)}, u32[]{:S(2)}, u32[]{:S(2)}) collective-permute-start(s16[32,1152]{1,0:T(8,128)(2,1)S(1)} %get-tuple-element.18), channel_id=1, source_target_pairs={{0,5},{1,4},{2,7},{3,6},{4,1},{5,0},{6,3},{7,2},{8,13},{9,12},{10,... | collective-permute-start | bytes 221192 | tf_op jit(solution)/shard_map/ppermute | solution.py:19
  43.6 2.4 %collective-permute-done.6.got_ref = s16[32,1152]{1,0:T(8,128)(2,1)S(1)} collective-permute-done((s16[32,1152]{1,0:T(8,128)(2,1)S(1)}, s16[32,1152]{1,0:T(8,128)(2,1)S(1)}, u32[]{:S(2)}, u32[]{:S(2)}) %collective-permute-start.6) | collective-permute-done | bytes 73760 | tf_op jit(solution)/shard_map/ppermute | solution.py:19
  45.9 0.2 combine.3
  46.1 3.1 %collective-permute-start.7 = (s16[16,1152]{1,0:T(8,128)(2,1)S(1)}, s16[16,1152]{1,0:T(8,128)(2,1)S(1)}, u32[]{:S(2)}, u32[]{:S(2)}) collective-permute-start(s16[16,1152]{1,0:T(8,128)(2,1)S(1)} %get-tuple-element.20), channel_id=1, source_target_pairs={{0,9},{1,8},{2,11},{3,10},{4,13},{5,12},{6,15},{7,14},{8,1},{9,0},... | collective-permute-start | bytes 110600 | tf_op jit(solution)/shard_map/ppermute | solution.py:19
  49.3 0.0 slice-done
  49.3 0.0 slice-done.1
  49.3 0.9 %own.1 = (bf16[16,1024]{1,0:T(8,128)(2,1)S(1)}, f32[16,1024]{1,0:T(8,128)S(1)}) custom-call(bf16[16,1152]{1,0:T(8,128)(2,1)S(1)} %pack.1.refs_1_.refs_0_, bf16[1024,4096]{1,0:T(8,128)(2,1)S(1)} %bitcast.4, bf16[16,1024]{1,0:T(8,128)(2,1)S(1)} %get-tuple-element.21.refs_2_, bf16[16,1024]{1,0:T(8,128)(2,1)S(1)} %get-tuple-element.22.refs_3_), custom_call_target="tpu_custom_call" | custom-call | flops 67108864 | bytes 4194304 | tf_op jit(solution)/shard_map/own/pallas_call | solution.py:219
  50.1 0.8 %collective-permute-done.7.got_ref = s16[16,1152]{1,0:T(8,128)(2,1)S(1)} collective-permute-done((s16[16,1152]{1,0:T(8,128)(2,1)S(1)}, s16[16,1152]{1,0:T(8,128)(2,1)S(1)}, u32[]{:S(2)}, u32[]{:S(2)}) %collective-permute-start.7) | collective-permute-done | bytes 36896 | tf_op jit(solution)/shard_map/ppermute | solution.py:19
  50.9 0.0 copy-done.3
  50.9 0.0 copy-done.5
  50.9 1.2 %finish.1 = bf16[16,1024]{1,0:T(8,128)(2,1)} custom-call(bf16[16,1024]{1,0:T(8,128)(2,1)S(1)} %copy-done.5, f32[16,1024]{1,0:T(8,128)S(1)} %get-tuple-element.19.kept_ref, s16[16,1152]{1,0:T(8,128)(2,1)S(1)} %collective-permute-done.7.got_ref, f32[16,1024]{1,0:T(8,128)S(1)} %get-tuple-element.23.term_ref, bf16[16,1024]{1,0:T(8,128)(2,1)S(1)} %get-tuple-element.24.gate_ref, ...), custom_call_target="tpu_custom_call" | custom-call | tf_op jit(solution)/shard_map/finish/pallas_call | solution.py:247
  (3 shorter events, 0.0 us)
Async XLA Ops:
  0.7 0.8 %copy-start.4 = (bf16[16,1024]{1,0:T(8,128)(2,1)S(1)}, bf16[16,1024]{1,0:T(8,128)(2,1)}, u32[]{:S(2)}) copy-start(bf16[16,1024]{1,0:T(8,128)(2,1)} %cand_ref.3) | copy-start | bytes 98308
  1.4 0.7 %copy-start.6 = (s32[16]{0:T(128)S(1)}, s32[16]{0:T(128)}, u32[]{:S(2)}) copy-start(s32[16]{0:T(128)} %param.9) | copy-start | bytes 196
  2.3 3.4 %copy-start = (bf16[1024,4096]{1,0:T(8,128)(2,1)S(1)}, bf16[1024,4096]{1,0:T(8,128)(2,1)}, u32[]{:S(2)}) copy-start(bf16[1024,4096]{1,0:T(8,128)(2,1)} %refs_1_.1) | copy-start | bytes 25165828
  5.6 1.2 %copy-start.2 = (bf16[512,1024]{1,0:T(8,128)(2,1)S(1)}, bf16[512,1024]{1,0:T(8,128)(2,1)}, u32[]{:S(2)}) copy-start(bf16[512,1024]{1,0:T(8,128)(2,1)} %refs_0_.3) | copy-start | bytes 3145732
  8.7 17.9 %collective-permute-start.3 = (bf16[512,1024]{1,0:T(8,128)(2,1)S(1)}, bf16[512,1024]{1,0:T(8,128)(2,1)S(1)}, u32[]{:S(2)}, u32[]{:S(2)}) collective-permute-start(bf16[512,1024]{1,0:T(8,128)(2,1)S(1)} %get-tuple-element.16.refs_4_), channel_id=1, source_target_pairs={{0,1},{1,0},{2,3},{3,2},{4,5},{5,4},{6,7},{7,6},{8,9},{9,8},{10,11... | collective-permute-start | bytes 3145736 | tf_op jit(solution)/shard_map/ppermute | solution.py:19
  11.1 15.5 %collective-permute-start.2 = (bf16[512,1024]{1,0:T(8,128)(2,1)S(1)}, bf16[512,1024]{1,0:T(8,128)(2,1)}, u32[]{:S(2)}, u32[]{:S(2)}) collective-permute-start(bf16[512,1024]{1,0:T(8,128)(2,1)S(1)} %get-tuple-element.15.refs_3_), channel_id=1, source_target_pairs={{0,1},{1,0},{2,3},{3,2},{4,5},{5,4},{6,7},{7,6},{8,9},{9,8},{10,11... | collective-permute-start | bytes 3145736 | tf_op jit(solution)/shard_map/ppermute | solution.py:19
  11.2 5.4 %collective-permute-start = (bf16[16,1152]{1,0:T(8,128)(2,1)S(1)}, bf16[16,1152]{1,0:T(8,128)(2,1)S(1)}, u32[]{:S(2)}, u32[]{:S(2)}) collective-permute-start(bf16[16,1152]{1,0:T(8,128)(2,1)S(1)} %pack.1.refs_1_.refs_0_), channel_id=1, source_target_pairs={{0,9},{1,8},{2,11},{3,10},{4,13},{5,12},{6,15},{7,14},{8,1},{9,0},... | collective-permute-start | bytes 110600 | tf_op jit(solution)/shard_map/ppermute | solution.py:19
  16.6 4.3 %collective-permute-start.1 = (bf16[32,1152]{1,0:T(8,128)(2,1)S(1)}, bf16[32,1152]{1,0:T(8,128)(2,1)S(1)}, u32[]{:S(2)}, u32[]{:S(2)}) collective-permute-start(bf16[32,1152]{1,0:T(8,128)(2,1)S(1)} %pad_maximum_fusion.1), channel_id=1, source_target_pairs={{0,5},{1,4},{2,7},{3,6},{4,1},{5,0},{6,3},{7,2},{8,13},{9,12},{10,... | collective-permute-start | bytes 221192 | tf_op jit(solution)/shard_map/ppermute | solution.py:19
  21.0 5.7 %collective-permute-start.4 = (bf16[64,1152]{1,0:T(8,128)(2,1)S(1)}, bf16[64,1152]{1,0:T(8,128)(2,1)S(1)}, u32[]{:S(2)}, u32[]{:S(2)}) collective-permute-start(bf16[64,1152]{1,0:T(8,128)(2,1)S(1)} %pad_maximum_fusion.refs_1_), channel_id=1, source_target_pairs={{0,3},{1,2},{2,1},{3,0},{4,7},{5,6},{6,5},{7,4},{8,11},{9,10},{10,... | collective-permute-start | bytes 442376 | tf_op jit(solution)/shard_map/ppermute | solution.py:19
  26.7 3.4 %copy-start.1 = (bf16[1024,4096]{1,0:T(8,128)(2,1)S(1)}, bf16[1024,4096]{1,0:T(8,128)(2,1)}, u32[]{:S(2)}) copy-start(bf16[1024,4096]{1,0:T(8,128)(2,1)} %refs_1_.1) | copy-start | bytes 25165828
  30.1 19.2 %slice-start = ((s8[8388608]{0:T(1024)(128)(4,1)}), s8[4194304]{0:T(1024)(128)(4,1)S(1)}, s32[]{:S(2)}) async-start(s8[8388608]{0:T(1024)(128)(4,1)} %bitcast.3), calls=%async_computation | async-start | bytes 8388608
  34.7 14.5 %slice-start.1 = ((s8[8388608]{0:T(1024)(128)(4,1)}), s8[4194304]{0:T(1024)(128)(4,1)S(1)}, s32[]{:S(2)}) async-start(s8[8388608]{0:T(1024)(128)(4,1)} %bitcast.3), calls=%async_computation.1 | async-start | bytes 8388608
  34.7 16.2 %copy-start.3 = (bf16[1024,1024]{1,0:T(8,128)(2,1)S(1)}, bf16[1024,1024]{1,0:T(8,128)(2,1)}, u32[]{:S(2)}) copy-start(bf16[1024,1024]{1,0:T(8,128)(2,1)} %w_ref.1) | copy-start | bytes 6291460
  34.7 16.2 %copy-start.5 = (bf16[16,1024]{1,0:T(8,128)(2,1)S(1)}, bf16[16,1024]{1,0:T(8,128)(2,1)}, u32[]{:S(2)}) copy-start(bf16[16,1024]{1,0:T(8,128)(2,1)} %cand_ref.3) | copy-start | bytes 98308
  34.8 6.4 %collective-permute-start.5 = (s16[64,1152]{1,0:T(8,128)(2,1)S(1)}, s16[64,1152]{1,0:T(8,128)(2,1)S(1)}, u32[]{:S(2)}, u32[]{:S(2)}) collective-permute-start(s16[64,1152]{1,0:T(8,128)(2,1)S(1)} %shard_map.67), channel_id=1, source_target_pairs={{0,3},{1,2},{2,1},{3,0},{4,7},{5,6},{6,5},{7,4},{8,11},{9,10},{10,... | collective-permute-start | bytes 442376 | tf_op jit(solution)/shard_map/ppermute | solution.py:19
  41.3 4.6 %collective-permute-start.6 = (s16[32,1152]{1,0:T(8,128)(2,1)S(1)}, s16[32,1152]{1,0:T(8,128)(2,1)S(1)}, u32[]{:S(2)}, u32[]{:S(2)}) collective-permute-start(s16[32,1152]{1,0:T(8,128)(2,1)S(1)} %get-tuple-element.18), channel_id=1, source_target_pairs={{0,5},{1,4},{2,7},{3,6},{4,1},{5,0},{6,3},{7,2},{8,13},{9,12},{10,... | collective-permute-start | bytes 221192 | tf_op jit(solution)/shard_map/ppermute | solution.py:19
  46.1 4.8 %collective-permute-start.7 = (s16[16,1152]{1,0:T(8,128)(2,1)S(1)}, s16[16,1152]{1,0:T(8,128)(2,1)S(1)}, u32[]{:S(2)}, u32[]{:S(2)}) collective-permute-start(s16[16,1152]{1,0:T(8,128)(2,1)S(1)} %get-tuple-element.20), channel_id=1, source_target_pairs={{0,9},{1,8},{2,11},{3,10},{4,13},{5,12},{6,15},{7,14},{8,1},{9,0},... | collective-permute-start | bytes 110600 | tf_op jit(solution)/shard_map/ppermute | solution.py:19

commit v2 on v1

v2 whole, which is shorter than its diff:
```python
import jax
import jax.numpy as jnp
from jax import lax
from jax.experimental import pallas as pl
from jax.experimental.pallas import tpu as pltpu
from jax.sharding import PartitionSpec as P


HEADS = 8
EPS = 1e-06
EXTRA = 128
STEPS = 32000.0
GRANT = 8 * 1024 * 1024
PARAMS = pltpu.CompilerParams(vmem_limit_bytes=GRANT)


def swapped(shard, axis, mask):
    size = lax.axis_size(axis)
    return lax.ppermute(shard, axis, [(i, i ^ mask) for i in range(size)])


def norm(rows):
    centred = rows - jnp.mean(rows, axis=-1, keepdims=True)
    spread = jnp.mean(centred * centred, axis=-1, keepdims=True)
    return centred * lax.rsqrt(spread + EPS)


def silu(x):
    half = x * 0.5
    return half + half * jnp.tanh(half)


def whole():
    return pl.BlockSpec(memory_space=pltpu.VMEM)


def encode(rows, out_ref):
    count, width = rows.shape
    top = jnp.max(jnp.abs(rows), axis=-1, keepdims=True)
    exponent = jnp.ceil(jnp.log2(jnp.maximum(top, 1e-30)))
    code = jnp.round(rows * (STEPS * jnp.exp2(-exponent)))
    out_ref[:, :width] = code.astype(jnp.int32).astype(jnp.int16)
    out_ref[:, width:] = (
        jnp.broadcast_to(exponent, (count, EXTRA)).astype(jnp.int32).astype(jnp.int16)
    )


def decode(code, width):
    code = code.astype(jnp.int32).astype(jnp.float32)
    return code[:, :width] * (jnp.exp2(code[:, width : width + 1]) * (1 / STEPS))


def stay(array):
    return pltpu.with_memory_space_constraint(array, pltpu.HBM)


def near_by(*arrays):
    return [pltpu.with_memory_space_constraint(array, pltpu.VMEM) for array in arrays]


def hbm():
    return pl.BlockSpec(memory_space=pltpu.HBM)


def limits_of(packed, width):
    high = packed[:, width : width + 1].astype(jnp.float32)
    low = packed[:, width + 1 : width + 2].astype(jnp.float32)
    return high * 256 + low


def begin_kernel(length_ref, cand_ref, visible_ref, out_ref, cand, visible, sems):
    rows, width = cand.shape
    loads = [
        pltpu.make_async_copy(cand_ref, cand, sems.at[0]),
        pltpu.make_async_copy(visible_ref, visible, sems.at[1]),
    ]
    for load in loads:
        load.start()
    loads[1].wait()
    seen = jnp.broadcast_to(visible[...], (rows, rows))
    diagonal = lax.broadcasted_iota(jnp.int32, (rows, rows), 0) == lax.broadcasted_iota(
        jnp.int32, (rows, rows), 1
    )
    limit = jnp.minimum(seen, length_ref[0]).astype(jnp.float32)
    limit = jnp.sum(jnp.where(diagonal, limit, 0.0), axis=1, keepdims=True)
    high = jnp.floor(limit * (1 / 256))
    low = limit - high * 256
    lane = lax.broadcasted_iota(jnp.int32, (rows, EXTRA), 1)
    out_ref[:, width:] = jnp.where(lane == 0, high, low).astype(jnp.bfloat16)
    loads[0].wait()
    out_ref[:, :width] = norm(cand[...].astype(jnp.float32)).astype(jnp.bfloat16)


def begin(candidates, hist_length, visible):
    rows, width = candidates.shape
    return pl.pallas_call(
        begin_kernel,
        out_shape=jax.ShapeDtypeStruct((rows, width + EXTRA), jnp.bfloat16),
        in_specs=[pl.BlockSpec(memory_space=pltpu.SMEM)] + [hbm()] * 2,
        out_specs=whole(),
        scratch_shapes=[
            pltpu.VMEM((rows, width), jnp.bfloat16),
            pltpu.VMEM((1, rows), jnp.int32),
            pltpu.SemaphoreType.DMA((2,)),
        ],
        compiler_params=PARAMS,
        cost_estimate=pl.CostEstimate(
            flops=6 * width**3, bytes_accessed=20 * width**2, transcendentals=0
        ),
        name="begin",
    )(hist_length, stay(candidates), stay(visible.reshape(1, rows)))


def project(rows_ref, w_ref, first, tile, n_keys, out_ref, self_ref):
    width = out_ref.shape[1]
    for at in range(0, width, tile):
        made = silu(
            jnp.dot(
                rows_ref[...],
                w_ref[:, first + at : first + at + tile],
                preferred_element_type=jnp.float32,
            )
        ).astype(jnp.bfloat16)
        out_ref[:, at : at + tile] = made[:n_keys]
        self_ref[:, at : at + tile] = made[n_keys:]


def project_keys(history, packed, w_proj):
    n_keys, width = history.shape
    rows = packed.shape[0]
    tile = min(256, width)

    def body(hist_ref, packed_ref, w_ref, key_ref, self_ref, rows_ref):
        rows_ref[n_keys:] = packed_ref[:, :width]
        rows_ref[:n_keys] = norm(hist_ref[...].astype(jnp.float32)).astype(jnp.bfloat16)
        project(rows_ref, w_ref, 2 * width, tile, n_keys, key_ref, self_ref)

    return pl.pallas_call(
        body,
        out_shape=(
            jax.ShapeDtypeStruct((n_keys, width), jnp.bfloat16),
            jax.ShapeDtypeStruct((rows, width), jnp.bfloat16),
            jax.ShapeDtypeStruct((n_keys + rows, width), jnp.bfloat16),
        ),
        in_specs=[whole()] * 3,
        out_specs=[whole()] * 3,
        compiler_params=PARAMS,
        name="keys",
    )(*near_by(history, packed, w_proj))


def project_values(rows_both, w_proj, rows):
    width = rows_both.shape[1]
    n_keys = rows_both.shape[0] - rows
    tile = min(256, width)

    def body(rows_ref, w_ref, value_ref, self_ref):
        project(rows_ref, w_ref, 3 * width, tile, n_keys, value_ref, self_ref)

    return pl.pallas_call(
        body,
        out_shape=(
            jax.ShapeDtypeStruct((n_keys, width), jnp.bfloat16),
            jax.ShapeDtypeStruct((rows, width), jnp.bfloat16),
        ),
        in_specs=[whole()] * 2,
        out_specs=[whole()] * 2,
        compiler_params=PARAMS,
        name="values",
    )(*near_by(rows_both, w_proj))


def project_queries(packed, got, w_proj):
    rows = packed.shape[0]
    width = w_proj.shape[0]
    tile = min(256, width)

    def body(packed_ref, got_ref, w_ref, out_ref):
        out_ref[:rows, width:] = packed_ref[:, width:]
        out_ref[rows:, width:] = got_ref[:, width:]
        both = jnp.concatenate([packed_ref[:, :width], got_ref[:, :width]], axis=0)
        for at in range(0, width, tile):
            out_ref[:, at : at + tile] = silu(
                jnp.dot(
                    both,
                    w_ref[:, width + at : width + at + tile],
                    preferred_element_type=jnp.float32,
                )
            ).astype(jnp.bfloat16)

    return pl.pallas_call(
        body,
        out_shape=jax.ShapeDtypeStruct((2 * rows, packed.shape[1]), jnp.bfloat16),
        in_specs=[whole()] * 3,
        out_specs=whole(),
        compiler_params=PARAMS,
        name="queries",
    )(*near_by(packed, got, w_proj))


def join(first, second):
    rows = first.shape[0]

    def body(first_ref, second_ref, out_ref):
        out_ref[:rows] = first_ref[...]
        out_ref[rows:] = second_ref[...]

    return pl.pallas_call(
        body,
        out_shape=jax.ShapeDtypeStruct((2 * rows, first.shape[1]), first.dtype),
        in_specs=[whole()] * 2,
        out_specs=whole(),
        compiler_params=PARAMS,
        name="join",
    )(first, second)


def attend_kernel(heads, coded, query_ref, k0, v0, k1, v1, out_ref, acc_ref):
    n_keys, width = k0.shape
    size = width // heads
    rows = query_ref.shape[0]
    limit = limits_of(query_ref[...], width)
    inverse = 1.0 / (limit + 1.0)
    position = lax.broadcasted_iota(jnp.int32, (rows, n_keys), 1).astype(jnp.float32)
    share = []
    for side in range(2):
        base = ((lax.axis_index("hist") ^ side) * n_keys).astype(jnp.float32)
        share.append(jnp.where(position + base < limit, inverse, 0.0))
    for head in range(heads):
        cols = slice(head * size, (head + 1) * size)
        total = None
        for side, (k, v) in enumerate(((k0, v0), (k1, v1))):
            scores = lax.dot_general(
                query_ref[:, cols],
                k[:, cols],
                (((1,), (1,)), ((), ())),
                preferred_element_type=jnp.float32,
            )
            weight = (silu(scores * size ** (-0.5)) * share[side]).astype(jnp.bfloat16)
            part = jnp.dot(weight, v[:, cols], preferred_element_type=jnp.float32)
            total = part if total is None else total + part
        acc_ref[:, cols] = total
    made = acc_ref[...]
    made = made - jnp.mean(made, axis=-1, keepdims=True)
    if coded:
        encode(made, out_ref)
    else:
        out_ref[...] = made


def attend(query, k0, v0, k1, v1, heads, coded):
    rows = query.shape[0]
    _, width = k0.shape

    def body(*refs):
        attend_kernel(heads, coded, *refs)

    return pl.pallas_call(
        body,
        out_shape=jax.ShapeDtypeStruct((rows, width + EXTRA), jnp.int16)
        if coded
        else jax.ShapeDtypeStruct((rows, width), jnp.float32),
        in_specs=[whole()] * 5,
        out_specs=whole(),
        scratch_shapes=[pltpu.VMEM((rows, width), jnp.float32)],
        compiler_params=PARAMS,
    )(*near_by(query, k0, v0, k1, v1))


def own_kernel(heads, tile, query_ref, packed_ref, w_ref, key_ref, value_ref, gate_ref, term_ref):
    rows, width = key_ref.shape
    size = width // heads
    query = query_ref[:rows, :width].astype(jnp.float32)
    inverse = 1.0 / (limits_of(packed_ref[...], width) + 1.0)
    products = query * key_ref[...].astype(jnp.float32)
    for head in range(heads):
        cols = slice(head * size, (head + 1) * size)
        score = jnp.sum(products[:, cols], axis=-1, keepdims=True)
        weight = (silu(score * size ** (-0.5)) * inverse).astype(jnp.bfloat16)
        term_ref[:, cols] = weight.astype(jnp.float32) * value_ref[:, cols].astype(jnp.float32)
    for at in range(0, width, tile):
        gate_ref[:, at : at + tile] = silu(
            jnp.dot(
                packed_ref[:, :width],
                w_ref[:, at : at + tile],
                preferred_element_type=jnp.float32,
            )
        ).astype(jnp.bfloat16)


def own(query, packed, w_proj, self_key, self_value, heads):
    rows, width = self_key.shape
    tile = min(256, width)

    def body(*refs):
        own_kernel(heads, tile, *refs)

    return pl.pallas_call(
        body,
        out_shape=(
            jax.ShapeDtypeStruct((rows, width), jnp.bfloat16),
            jax.ShapeDtypeStruct((rows, width), jnp.float32),
        ),
        in_specs=[whole()] * 5,
        out_specs=[whole()] * 2,
        compiler_params=PARAMS,
        name="own",
    )(*near_by(query, packed, w_proj, self_key, self_value))


def finish_kernel(cand_ref, kept_ref, got_ref, term_ref, gate_ref, w_ref, out_ref):
    attended = kept_ref[...] + decode(got_ref[...], kept_ref.shape[1]) + term_ref[...]
    mixed = (norm(attended) * gate_ref[...].astype(jnp.float32)).astype(jnp.bfloat16)
    out_ref[...] = (
        cand_ref[...].astype(jnp.float32)
        + jnp.dot(mixed, w_ref[...], preferred_element_type=jnp.float32)
    ).astype(jnp.bfloat16)


def finish(candidates, kept, got, term, gate, w_out):
    return pl.pallas_call(
        finish_kernel,
        out_shape=jax.ShapeDtypeStruct(candidates.shape, jnp.bfloat16),
        in_specs=[whole()] * 6,
        out_specs=whole(),
        compiler_params=PARAMS,
        name="finish",
    )(candidates, kept, got, term, gate, w_out)


def combine_kernel(kept_ref, got_ref, sent_ref, out_ref):
    half, width = out_ref.shape
    encode(kept_ref[half:] + decode(got_ref[half:], width), sent_ref)
    out_ref[...] = kept_ref[:half] + decode(got_ref[:half], width)


def combine(kept, got):
    half, width = kept.shape[0] // 2, kept.shape[1]
    return pl.pallas_call(
        combine_kernel,
        out_shape=(
            jax.ShapeDtypeStruct((half, width + EXTRA), jnp.int16),
            jax.ShapeDtypeStruct((half, width), jnp.float32),
        ),
        in_specs=[whole()] * 2,
        out_specs=(whole(), whole()),
        compiler_params=PARAMS,
        name="combine",
    )(kept, got)


def layer(history, candidates, hist_length, visible, w_proj, w_out):
    size = lax.axis_size("hist")
    masks = []
    bit = size // 2
    while bit > 1:
        masks.append(bit | 1)
        bit //= 2
    packed = begin(candidates, hist_length, visible)
    keys, self_key, rows_both = project_keys(history, packed, w_proj)
    values, self_value = project_values(rows_both, w_proj, packed.shape[0])
    other_keys = swapped(keys, "hist", 1)
    other_values = swapped(values, "hist", 1)
    gathered = packed
    for step, mask in enumerate(masks[:-1]):
        got = swapped(gathered, "hist", mask)
        gathered = join(gathered, got) if step else project_queries(packed, got, w_proj)
    far = swapped(gathered, "hist", masks[-1])
    shards = (keys, values, other_keys, other_values)
    kept = attend(gathered, *shards, HEADS, False)
    sent = attend(far, *shards, HEADS, True)
    gate, term = own(gathered, packed, w_proj, self_key, self_value, HEADS)
    got = swapped(sent, "hist", masks[-1])
    for mask in masks[-2::-1]:
        sent, kept = combine(kept, got)
        got = swapped(sent, "hist", mask)
    return finish(candidates, kept, got, term, gate, w_out)


def solution(mesh):
    in_specs = (
        P(("groups", "hist"), None),
        P(("groups", "hist"), None),
        P("groups"),
        P(("groups", "hist")),
        P(),
        P(),
    )
    out_specs = P(("groups", "hist"), None)
    return jax.shard_map(
        layer, mesh=mesh, in_specs=in_specs, out_specs=out_specs, check_vma=False
    )
```

time: 52.5 us -> 43.8 us (0.83)
  local copies, waits for them, and re-layouts: 9.42 us -> 2.52 us
  Pallas kernels: 15.4 us -> 11.7 us
  waiting for transfers between devices: 11.2 us -> 13.3 us
    unnamed x18 -> x8, local copies, waits for them, and re-layouts: 9.42 us -> 2.52 us
    pallas_call x2, Pallas kernels: 9.04 us -> 4.79 us  [attend(): pl.pallas_call(body, out_shape=jax.ShapeDtypeStruct((rows, width + EXTRA)...]
    ppermute x8, waiting for transfers between devices: 11.2 us -> 13.3 us  [swapped(): return lax.ppermute(shard, axis, [(i, i ^ mask) for i in range(size)])]
    pallas_call x3 -> x5, Pallas kernels: 3.89 us -> 4.87 us  [the longest x1 1.84 us: project_keys(): pl.pallas_call(body, out_shape=(jax.ShapeDtypeStruct((n_keys, width), jnp...]
  transfers between devices with their start and end apart: 8 -> 8, of which waited for: 5 -> 6; matrix products, arithmetic and copies ran while one was open for 0% -> 0% of each run, Pallas kernels for 14% -> 7%
where the time goes in v2:
time: 43.8 us; the launch traced here: 43.6 us
  starting transfers between devices  15.4 us (35%)
  waiting for transfers between devices  13.3 us (30%)
  Pallas kernels  11.7 us (27%)
  local copies, waits for them, and re-layouts  2.52 us (6%)
  between operations  0.75 us (2%)
    ppermute x8, starting transfers between devices, swapped(): return lax.ppermute(shard, axis, [(i, i ^ mask) for i in range(size)])  15.4 us
    ppermute x8, waiting for transfers between devices, swapped(): return lax.ppermute(shard, axis, [(i, i ^ mask) for i in range(size)])  13.3 us
    pallas_call x2, Pallas kernels, attend(): pl.pallas_call(body, out_shape=jax.ShapeDtypeStruct((rows, width + EXTRA)...  4.79 us
    unnamed x8, local copies, waits for them, and re-layouts  2.52 us
    pallas_call x1, Pallas kernels, project_keys(): pl.pallas_call(body, out_shape=(jax.ShapeDtypeStruct((n_keys, width), jnp...  1.84 us
    pallas_call x1, Pallas kernels, project_values(): pl.pallas_call(body, out_shape=(jax.ShapeDtypeStruct((n_keys, width), jnp...  1.42 us
    pallas_call x1, Pallas kernels, finish(): pl.pallas_call(finish_kernel, out_shape=jax.ShapeDtypeStruct(candidates.s...  1.24 us
    pallas_call x1, Pallas kernels, begin(): pl.pallas_call(begin_kernel, out_shape=jax.ShapeDtypeStruct((rows, width...  1.11 us
  transfers between devices with their start and end apart: 8, of which 6 were waited for; matrix products, arithmetic and copies ran while one was open for 0% of the time, Pallas kernels for 7%

profile of v2, /device:TPU:0, one launch (start us, length us, event | category | flops | bytes accessed | tf_op | source)
XLA Modules:
  0.0 43.6 jit_solution(2910260379404817292)
XLA Ops:
  0.7 0.0 copy-start
  0.7 0.0 copy-start.2
  0.7 1.1 %begin.1.packed_ref.refs_1_ = bf16[16,1152]{1,0:T(8,128)(2,1)S(1)} custom-call(s32[1]{0:T(128)S(6)} %copy.7.length_ref, bf16[16,1024]{1,0:T(8,128)(2,1)} %cand_ref.3, s32[1,16]{1,0:T(1,128)} %bitcast.1), custom_call_target="tpu_custom_call" | custom-call | flops 6442450944 | bytes 20971520 | tf_op jit(solution)/shard_map/begin/pallas_call | solution.py:96
  1.8 2.3 %copy-done = bf16[1024,4096]{1,0:T(8,128)(2,1)S(1)} copy-done((bf16[1024,4096]{1,0:T(8,128)(2,1)S(1)}, bf16[1024,4096]{1,0:T(8,128)(2,1)}, u32[]{:S(2)}) %copy-start) | copy-done | bytes 8388632
  4.1 0.2 copy-done.2
  4.3 1.8 %keys.1 = (bf16[512,1024]{1,0:T(8,128)(2,1)S(1)}, bf16[16,1024]{1,0:T(8,128)(2,1)S(1)}, bf16[528,1024]{1,0:T(8,128)(2,1)S(1)}) custom-call(bf16[512,1024]{1,0:T(8,128)(2,1)S(1)} %copy-done.2, bf16[16,1152]{1,0:T(8,128)(2,1)S(1)} %begin.1.packed_ref.refs_1_, bf16[1024,4096]{1,0:T(8,128)(2,1)S(1)} %copy-done), custom_call_target="tpu_custom_call" | custom-call | tf_op jit(solution)/shard_map/keys/pallas_call | solution.py:138
  6.1 1.4 %values.1 = (bf16[512,1024]{1,0:T(8,128)(2,1)S(1)}, bf16[16,1024]{1,0:T(8,128)(2,1)S(1)}) custom-call(bf16[528,1024]{1,0:T(8,128)(2,1)S(1)} %get-tuple-element.17.rows_ref, bf16[1024,4096]{1,0:T(8,128)(2,1)S(1)} %copy-done), custom_call_target="tpu_custom_call" | custom-call | tf_op jit(solution)/shard_map/values/pallas_call | solution.py:160
  7.6 0.6 %collective-permute-start.3 = (bf16[512,1024]{1,0:T(8,128)(2,1)S(1)}, bf16[512,1024]{1,0:T(8,128)(2,1)S(1)}, u32[]{:S(2)}, u32[]{:S(2)}) collective-permute-start(bf16[512,1024]{1,0:T(8,128)(2,1)S(1)} %get-tuple-element.18.refs_2_), channel_id=1, source_target_pairs={{0,1},{1,0},{2,3},{3,2},{4,5},{5,4},{6,7},{7,6},{8,9},{9,8},{10,11... | collective-permute-start | bytes 3145736 | tf_op jit(solution)/shard_map/ppermute | solution.py:19
  8.1 0.1 collective-permute-start.2
  8.2 3.7 %collective-permute-start = (bf16[16,1152]{1,0:T(8,128)(2,1)S(1)}, bf16[16,1152]{1,0:T(8,128)(2,1)S(1)}, u32[]{:S(2)}, u32[]{:S(2)}) collective-permute-start(bf16[16,1152]{1,0:T(8,128)(2,1)S(1)} %begin.1.packed_ref.refs_1_), channel_id=1, source_target_pairs={{0,9},{1,8},{2,11},{3,10},{4,13},{5,12},{6,15},{7,14},{8,1},{9,0},... | collective-permute-start | bytes 110600 | tf_op jit(solution)/shard_map/ppermute | solution.py:19
  11.9 1.6 %collective-permute-done.got_ref = bf16[16,1152]{1,0:T(8,128)(2,1)S(1)} collective-permute-done((bf16[16,1152]{1,0:T(8,128)(2,1)S(1)}, bf16[16,1152]{1,0:T(8,128)(2,1)S(1)}, u32[]{:S(2)}, u32[]{:S(2)}) %collective-permute-start) | collective-permute-done | bytes 36896 | tf_op jit(solution)/shard_map/ppermute | solution.py:19
  13.5 0.5 %queries.1.first_ref = bf16[32,1152]{1,0:T(8,128)(2,1)S(1)} custom-call(bf16[16,1152]{1,0:T(8,128)(2,1)S(1)} %begin.1.packed_ref.refs_1_, bf16[16,1152]{1,0:T(8,128)(2,1)S(1)} %collective-permute-done.got_ref, bf16[1024,4096]{1,0:T(8,128)(2,1)S(1)} %copy-done), custom_call_target="tpu_custom_call" | custom-call | tf_op jit(solution)/shard_map/queries/pallas_call | solution.py:191
  14.0 1.9 %collective-permute-start.1 = (bf16[32,1152]{1,0:T(8,128)(2,1)S(1)}, bf16[32,1152]{1,0:T(8,128)(2,1)S(1)}, u32[]{:S(2)}, u32[]{:S(2)}) collective-permute-start(bf16[32,1152]{1,0:T(8,128)(2,1)S(1)} %queries.1.first_ref), channel_id=1, source_target_pairs={{0,5},{1,4},{2,7},{3,6},{4,1},{5,0},{6,3},{7,2},{8,13},{9,12},{10,... | collective-permute-start | bytes 221192 | tf_op jit(solution)/shard_map/ppermute | solution.py:19
  15.9 2.5 %collective-permute-done.1.second_ref = bf16[32,1152]{1,0:T(8,128)(2,1)S(1)} collective-permute-done((bf16[32,1152]{1,0:T(8,128)(2,1)S(1)}, bf16[32,1152]{1,0:T(8,128)(2,1)S(1)}, u32[]{:S(2)}, u32[]{:S(2)}) %collective-permute-start.1) | collective-permute-done | bytes 73760 | tf_op jit(solution)/shard_map/ppermute | solution.py:19
  18.4 1.8 %collective-permute-start.4 = (bf16[64,1152]{1,0:T(8,128)(2,1)S(1)}, bf16[64,1152]{1,0:T(8,128)(2,1)S(1)}, u32[]{:S(2)}, u32[]{:S(2)}) collective-permute-start(bf16[64,1152]{1,0:T(8,128)(2,1)S(1)} %join.1.refs_0_), channel_id=1, source_target_pairs={{0,3},{1,2},{2,1},{3,0},{4,7},{5,6},{6,5},{7,4},{8,11},{9,10},{10,... | collective-permute-start | bytes 442376 | tf_op jit(solution)/shard_map/ppermute | solution.py:19
  20.2 3.9 %collective-permute-done.4.refs_0_ = bf16[64,1152]{1,0:T(8,128)(2,1)S(1)} collective-permute-done((bf16[64,1152]{1,0:T(8,128)(2,1)S(1)}, bf16[64,1152]{1,0:T(8,128)(2,1)S(1)}, u32[]{:S(2)}, u32[]{:S(2)}) %collective-permute-start.4) | collective-permute-done | bytes 147488 | tf_op jit(solution)/shard_map/ppermute | solution.py:19
  24.2 0.0 collective-permute-done.3.refs_4_
  24.2 0.0 collective-permute-done.2.refs_3_
  24.2 2.5 %shard_map.65 = s16[64,1152]{1,0:T(8,128)(2,1)S(1)} custom-call(bf16[64,1152]{1,0:T(8,128)(2,1)S(1)} %collective-permute-done.4.refs_0_, bf16[512,1024]{1,0:T(8,128)(2,1)S(1)} %get-tuple-element.16.refs_1_, bf16[512,1024]{1,0:T(8,128)(2,1)S(1)} %get-tuple-element.18.refs_2_, bf16[512,1024]{1,0:T(8,128)(2,1)S(1)} %collective-permute-done.2.refs_3_, ...), custom_call_target="tpu_custom_call" | custom-call | tf_op jit(solution)/shard_map/pallas_call | solution.py:258
  26.6 2.0 %collective-permute-start.5 = (s16[64,1152]{1,0:T(8,128)(2,1)S(1)}, s16[64,1152]{1,0:T(8,128)(2,1)S(1)}, u32[]{:S(2)}, u32[]{:S(2)}) collective-permute-start(s16[64,1152]{1,0:T(8,128)(2,1)S(1)} %shard_map.65), channel_id=1, source_target_pairs={{0,3},{1,2},{2,1},{3,0},{4,7},{5,6},{6,5},{7,4},{8,11},{9,10},{10,... | collective-permute-start | bytes 442376 | tf_op jit(solution)/shard_map/ppermute | solution.py:19
  28.6 2.3 %shard_map.64.kept_ref = f32[64,1024]{1,0:T(8,128)S(1)} custom-call(bf16[64,1152]{1,0:T(8,128)(2,1)S(1)} %join.1.refs_0_, bf16[512,1024]{1,0:T(8,128)(2,1)S(1)} %get-tuple-element.16.refs_1_, bf16[512,1024]{1,0:T(8,128)(2,1)S(1)} %get-tuple-element.18.refs_2_, bf16[512,1024]{1,0:T(8,128)(2,1)S(1)} %collective-permute-done.2.refs_3_, ...), custom_call_target="tpu_custom_call" | custom-call | tf_op jit(solution)/shard_map/pallas_call | solution.py:258
  30.9 1.6 %collective-permute-done.5.got_ref = s16[64,1152]{1,0:T(8,128)(2,1)S(1)} collective-permute-done((s16[64,1152]{1,0:T(8,128)(2,1)S(1)}, s16[64,1152]{1,0:T(8,128)(2,1)S(1)}, u32[]{:S(2)}, u32[]{:S(2)}) %collective-permute-start.5) | collective-permute-done | bytes 147488 | tf_op jit(solution)/shard_map/ppermute | solution.py:19
  32.5 0.2 combine.2
  32.7 2.4 %collective-permute-start.6 = (s16[32,1152]{1,0:T(8,128)(2,1)S(1)}, s16[32,1152]{1,0:T(8,128)(2,1)S(1)}, u32[]{:S(2)}, u32[]{:S(2)}) collective-permute-start(s16[32,1152]{1,0:T(8,128)(2,1)S(1)} %get-tuple-element.20), channel_id=1, source_target_pairs={{0,5},{1,4},{2,7},{3,6},{4,1},{5,0},{6,3},{7,2},{8,13},{9,12},{10,... | collective-permute-start | bytes 221192 | tf_op jit(solution)/shard_map/ppermute | solution.py:19
  35.1 2.4 %collective-permute-done.6.got_ref = s16[32,1152]{1,0:T(8,128)(2,1)S(1)} collective-permute-done((s16[32,1152]{1,0:T(8,128)(2,1)S(1)}, s16[32,1152]{1,0:T(8,128)(2,1)S(1)}, u32[]{:S(2)}, u32[]{:S(2)}) %collective-permute-start.6) | collective-permute-done | bytes 73760 | tf_op jit(solution)/shard_map/ppermute | solution.py:19
  37.4 0.2 combine.3
  37.6 3.1 %collective-permute-start.7 = (s16[16,1152]{1,0:T(8,128)(2,1)S(1)}, s16[16,1152]{1,0:T(8,128)(2,1)S(1)}, u32[]{:S(2)}, u32[]{:S(2)}) collective-permute-start(s16[16,1152]{1,0:T(8,128)(2,1)S(1)} %get-tuple-element.22), channel_id=1, source_target_pairs={{0,9},{1,8},{2,11},{3,10},{4,13},{5,12},{6,15},{7,14},{8,1},{9,0},... | collective-permute-start | bytes 110600 | tf_op jit(solution)/shard_map/ppermute | solution.py:19
  40.8 0.0 copy-start.1
  40.8 0.0 copy-start.3
  40.8 0.4 own.1
  41.2 1.2 %collective-permute-done.7.got_ref = s16[16,1152]{1,0:T(8,128)(2,1)S(1)} collective-permute-done((s16[16,1152]{1,0:T(8,128)(2,1)S(1)}, s16[16,1152]{1,0:T(8,128)(2,1)S(1)}, u32[]{:S(2)}, u32[]{:S(2)}) %collective-permute-start.7) | collective-permute-done | bytes 36896 | tf_op jit(solution)/shard_map/ppermute | solution.py:19
  42.4 0.0 copy-done.1
  42.4 0.0 copy-done.3
  42.4 1.2 %finish.1 = bf16[16,1024]{1,0:T(8,128)(2,1)} custom-call(bf16[16,1024]{1,0:T(8,128)(2,1)S(1)} %copy-done.3, f32[16,1024]{1,0:T(8,128)S(1)} %get-tuple-element.21.kept_ref, s16[16,1152]{1,0:T(8,128)(2,1)S(1)} %collective-permute-done.7.got_ref, f32[16,1024]{1,0:T(8,128)S(1)} %get-tuple-element.25.term_ref, bf16[16,1024]{1,0:T(8,128)(2,1)S(1)} %get-tuple-element.26.gate_ref, ...), custom_call_target="tpu_custom_call" | custom-call | tf_op jit(solution)/shard_map/finish/pallas_call | solution.py:321
  (1 shorter events, 0.0 us)
Async XLA Ops:
  0.7 3.4 %copy-start = (bf16[1024,4096]{1,0:T(8,128)(2,1)S(1)}, bf16[1024,4096]{1,0:T(8,128)(2,1)}, u32[]{:S(2)}) copy-start(bf16[1024,4096]{1,0:T(8,128)(2,1)} %refs_2_.1) | copy-start | bytes 25165828
  0.7 3.6 %copy-start.2 = (bf16[512,1024]{1,0:T(8,128)(2,1)S(1)}, bf16[512,1024]{1,0:T(8,128)(2,1)}, u32[]{:S(2)}) copy-start(bf16[512,1024]{1,0:T(8,128)(2,1)} %hist_ref.1) | copy-start | bytes 3145732
  7.6 16.6 %collective-permute-start.3 = (bf16[512,1024]{1,0:T(8,128)(2,1)S(1)}, bf16[512,1024]{1,0:T(8,128)(2,1)S(1)}, u32[]{:S(2)}, u32[]{:S(2)}) collective-permute-start(bf16[512,1024]{1,0:T(8,128)(2,1)S(1)} %get-tuple-element.18.refs_2_), channel_id=1, source_target_pairs={{0,1},{1,0},{2,3},{3,2},{4,5},{5,4},{6,7},{7,6},{8,9},{9,8},{10,11... | collective-permute-start | bytes 3145736 | tf_op jit(solution)/shard_map/ppermute | solution.py:19
  8.1 16.0 %collective-permute-start.2 = (bf16[512,1024]{1,0:T(8,128)(2,1)S(1)}, bf16[512,1024]{1,0:T(8,128)(2,1)S(1)}, u32[]{:S(2)}, u32[]{:S(2)}) collective-permute-start(bf16[512,1024]{1,0:T(8,128)(2,1)S(1)} %get-tuple-element.16.refs_1_), channel_id=1, source_target_pairs={{0,1},{1,0},{2,3},{3,2},{4,5},{5,4},{6,7},{7,6},{8,9},{9,8},{10,11... | collective-permute-start | bytes 3145736 | tf_op jit(solution)/shard_map/ppermute | solution.py:19
  8.2 5.3 %collective-permute-start = (bf16[16,1152]{1,0:T(8,128)(2,1)S(1)}, bf16[16,1152]{1,0:T(8,128)(2,1)S(1)}, u32[]{:S(2)}, u32[]{:S(2)}) collective-permute-start(bf16[16,1152]{1,0:T(8,128)(2,1)S(1)} %begin.1.packed_ref.refs_1_), channel_id=1, source_target_pairs={{0,9},{1,8},{2,11},{3,10},{4,13},{5,12},{6,15},{7,14},{8,1},{9,0},... | collective-permute-start | bytes 110600 | tf_op jit(solution)/shard_map/ppermute | solution.py:19
  14.0 4.4 %collective-permute-start.1 = (bf16[32,1152]{1,0:T(8,128)(2,1)S(1)}, bf16[32,1152]{1,0:T(8,128)(2,1)S(1)}, u32[]{:S(2)}, u32[]{:S(2)}) collective-permute-start(bf16[32,1152]{1,0:T(8,128)(2,1)S(1)} %queries.1.first_ref), channel_id=1, source_target_pairs={{0,5},{1,4},{2,7},{3,6},{4,1},{5,0},{6,3},{7,2},{8,13},{9,12},{10,... | collective-permute-start | bytes 221192 | tf_op jit(solution)/shard_map/ppermute | solution.py:19
  18.4 5.7 %collective-permute-start.4 = (bf16[64,1152]{1,0:T(8,128)(2,1)S(1)}, bf16[64,1152]{1,0:T(8,128)(2,1)S(1)}, u32[]{:S(2)}, u32[]{:S(2)}) collective-permute-start(bf16[64,1152]{1,0:T(8,128)(2,1)S(1)} %join.1.refs_0_), channel_id=1, source_target_pairs={{0,3},{1,2},{2,1},{3,0},{4,7},{5,6},{6,5},{7,4},{8,11},{9,10},{10,... | collective-permute-start | bytes 442376 | tf_op jit(solution)/shard_map/ppermute | solution.py:19
  26.6 5.9 %collective-permute-start.5 = (s16[64,1152]{1,0:T(8,128)(2,1)S(1)}, s16[64,1152]{1,0:T(8,128)(2,1)S(1)}, u32[]{:S(2)}, u32[]{:S(2)}) collective-permute-start(s16[64,1152]{1,0:T(8,128)(2,1)S(1)} %shard_map.65), channel_id=1, source_target_pairs={{0,3},{1,2},{2,1},{3,0},{4,7},{5,6},{6,5},{7,4},{8,11},{9,10},{10,... | collective-permute-start | bytes 442376 | tf_op jit(solution)/shard_map/ppermute | solution.py:19
  32.7 4.7 %collective-permute-start.6 = (s16[32,1152]{1,0:T(8,128)(2,1)S(1)}, s16[32,1152]{1,0:T(8,128)(2,1)S(1)}, u32[]{:S(2)}, u32[]{:S(2)}) collective-permute-start(s16[32,1152]{1,0:T(8,128)(2,1)S(1)} %get-tuple-element.20), channel_id=1, source_target_pairs={{0,5},{1,4},{2,7},{3,6},{4,1},{5,0},{6,3},{7,2},{8,13},{9,12},{10,... | collective-permute-start | bytes 221192 | tf_op jit(solution)/shard_map/ppermute | solution.py:19
  37.6 4.8 %collective-permute-start.7 = (s16[16,1152]{1,0:T(8,128)(2,1)S(1)}, s16[16,1152]{1,0:T(8,128)(2,1)S(1)}, u32[]{:S(2)}, u32[]{:S(2)}) collective-permute-start(s16[16,1152]{1,0:T(8,128)(2,1)S(1)} %get-tuple-element.22), channel_id=1, source_target_pairs={{0,9},{1,8},{2,11},{3,10},{4,13},{5,12},{6,15},{7,14},{8,1},{9,0},... | collective-permute-start | bytes 110600 | tf_op jit(solution)/shard_map/ppermute | solution.py:19
  40.8 1.6 %copy-start.1 = (bf16[1024,1024]{1,0:T(8,128)(2,1)S(1)}, bf16[1024,1024]{1,0:T(8,128)(2,1)}, u32[]{:S(2)}) copy-start(bf16[1024,1024]{1,0:T(8,128)(2,1)} %w_ref.7) | copy-start | bytes 6291460
  40.8 1.6 %copy-start.3 = (bf16[16,1024]{1,0:T(8,128)(2,1)S(1)}, bf16[16,1024]{1,0:T(8,128)(2,1)}, u32[]{:S(2)}) copy-start(bf16[16,1024]{1,0:T(8,128)(2,1)} %cand_ref.3) | copy-start | bytes 98308

commit v3 on v2

--- a/solution.py
+++ b/solution.py
@@ -215,56 +215,76 @@
     )(first, second)
 
 
-def attend_kernel(heads, coded, query_ref, k0, v0, k1, v1, out_ref, acc_ref):
+def attend_kernel(heads, query, k0, v0, k1, v1, acc_ref):
     n_keys, width = k0.shape
     size = width // heads
-    rows = query_ref.shape[0]
-    limit = limits_of(query_ref[...], width)
+    rows = query.shape[0]
+    limit = limits_of(query, width)
     inverse = 1.0 / (limit + 1.0)
     position = lax.broadcasted_iota(jnp.int32, (rows, n_keys), 1).astype(jnp.float32)
+    sides = ((k0, v0), (k1, v1))
     share = []
     for side in range(2):
         base = ((lax.axis_index("hist") ^ side) * n_keys).astype(jnp.float32)
         share.append(jnp.where(position + base < limit, inverse, 0.0))
-    for head in range(heads):
+
+    def scores_of(head):
         cols = slice(head * size, (head + 1) * size)
-        total = None
-        for side, (k, v) in enumerate(((k0, v0), (k1, v1))):
-            scores = lax.dot_general(
-                query_ref[:, cols],
+        return [
+            lax.dot_general(
+                query[:, cols],
                 k[:, cols],
                 (((1,), (1,)), ((), ())),
                 preferred_element_type=jnp.float32,
             )
-            weight = (silu(scores * size ** (-0.5)) * share[side]).astype(jnp.bfloat16)
+            for k, _ in sides
+        ]
+
+    ahead = scores_of(0)
+    for head in range(heads):
+        scores = ahead
+        if head + 1 < heads:
+            ahead = scores_of(head + 1)
+        cols = slice(head * size, (head + 1) * size)
+        total = None
+        for side, (_, v) in enumerate(sides):
+            weight = (silu(scores[side] * size ** (-0.5)) * share[side]).astype(jnp.bfloat16)
             part = jnp.dot(weight, v[:, cols], preferred_element_type=jnp.float32)
             total = part if total is None else total + part
         acc_ref[:, cols] = total
     made = acc_ref[...]
-    made = made - jnp.mean(made, axis=-1, keepdims=True)
-    if coded:
-        encode(made, out_ref)
-    else:
-        out_ref[...] = made
-
-
-def attend(query, k0, v0, k1, v1, heads, coded):
-    rows = query.shape[0]
-    _, width = k0.shape
+    return made - jnp.mean(made, axis=-1, keepdims=True)
+
+
+def attend(queries, shards, heads, coded):
+    rows = queries[0].shape[0]
+    _, width = shards[0].shape
+    blocks = len(queries)
 
     def body(*refs):
-        attend_kernel(heads, coded, *refs)
-
-    return pl.pallas_call(
-        body,
-        out_shape=jax.ShapeDtypeStruct((rows, width + EXTRA), jnp.int16)
+        ins, shard_refs, outs = refs[:blocks], refs[blocks : blocks + 4], refs[blocks + 4 : -1]
+        query = jnp.concatenate([ref[...] for ref in ins], axis=0)
+        made = attend_kernel(heads, query, *shard_refs, refs[-1])
+        for block, out_ref in enumerate(outs):
+            part = made[block * rows : (block + 1) * rows]
+            if coded:
+                encode(part, out_ref)
+            else:
+                out_ref[...] = part
+
+    out = (
+        jax.ShapeDtypeStruct((rows, width + EXTRA), jnp.int16)
         if coded
-        else jax.ShapeDtypeStruct((rows, width), jnp.float32),
-        in_specs=[whole()] * 5,
-        out_specs=whole(),
-        scratch_shapes=[pltpu.VMEM((rows, width), jnp.float32)],
-        compiler_params=PARAMS,
-    )(*near_by(query, k0, v0, k1, v1))
+        else jax.ShapeDtypeStruct((rows, width), jnp.float32)
+    )
+    return pl.pallas_call(
+        body,
+        out_shape=[out] * blocks,
+        in_specs=[whole()] * (blocks + 4),
+        out_specs=[whole()] * blocks,
+        scratch_shapes=[pltpu.VMEM((blocks * rows, width), jnp.float32)],
+        compiler_params=PARAMS,
+    )(*near_by(*queries, *shards))
 
 
 def own_kernel(heads, tile, query_ref, packed_ref, w_ref, key_ref, value_ref, gate_ref, term_ref):
@@ -308,48 +328,72 @@
     )(*near_by(query, packed, w_proj, self_key, self_value))
 
 
-def finish_kernel(cand_ref, kept_ref, got_ref, term_ref, gate_ref, w_ref, out_ref):
-    attended = kept_ref[...] + decode(got_ref[...], kept_ref.shape[1]) + term_ref[...]
-    mixed = (norm(attended) * gate_ref[...].astype(jnp.float32)).astype(jnp.bfloat16)
-    out_ref[...] = (
-        cand_ref[...].astype(jnp.float32)
-        + jnp.dot(mixed, w_ref[...], preferred_element_type=jnp.float32)
-    ).astype(jnp.bfloat16)
-
-
-def finish(candidates, kept, got, term, gate, w_out):
-    return pl.pallas_call(
-        finish_kernel,
+def total_of(terms, refs, rows, width):
+    total = None
+    for place, first in terms:
+        part = refs[place][first : first + rows]
+        if part.dtype == jnp.int16:
+            part = decode(part, width)
+        total = part if total is None else total + part
+    return total
+
+
+def placed(pieces):
+    arrays = []
+    lists = []
+    for terms in pieces:
+        listed = []
+        for array, first in terms:
+            place = next((i for i, seen in enumerate(arrays) if seen is array), None)
+            if place is None:
+                place = len(arrays)
+                arrays.append(array)
+            listed.append((place, first))
+        lists.append(listed)
+    return arrays, lists
+
+
+def emit(pieces, rows, width):
+    arrays, lists = placed(pieces)
+
+    def body(*refs):
+        for terms, out_ref in zip(lists, refs[len(arrays) :]):
+            encode(total_of(terms, refs, rows, width), out_ref)
+
+    return pl.pallas_call(
+        body,
+        out_shape=[jax.ShapeDtypeStruct((rows, width + EXTRA), jnp.int16)] * len(pieces),
+        in_specs=[whole()] * len(arrays),
+        out_specs=[whole()] * len(pieces),
+        compiler_params=PARAMS,
+        name="emit",
+    )(*arrays)
+
+
+def finish(candidates, terms, term, gate, w_out):
+    arrays, (listed,) = placed([terms])
+
+    def body(cand_ref, term_ref, gate_ref, w_ref, *refs):
+        rows, width = cand_ref.shape
+        attended = total_of(listed, refs, rows, width) + term_ref[...]
+        mixed = (norm(attended) * gate_ref[...].astype(jnp.float32)).astype(jnp.bfloat16)
+        refs[-1][...] = (
+            cand_ref[...].astype(jnp.float32)
+            + jnp.dot(mixed, w_ref[...], preferred_element_type=jnp.float32)
+        ).astype(jnp.bfloat16)
+
+    return pl.pallas_call(
+        body,
         out_shape=jax.ShapeDtypeStruct(candidates.shape, jnp.bfloat16),
-        in_specs=[whole()] * 6,
+        in_specs=[whole()] * (4 + len(arrays)),
         out_specs=whole(),
         compiler_params=PARAMS,
         name="finish",
-    )(candidates, kept, got, term, gate, w_out)
-
-
-def combine_kernel(kept_ref, got_ref, sent_ref, out_ref):
-    half, width = out_ref.shape
-    encode(kept_ref[half:] + decode(got_ref[half:], width), sent_ref)
-    out_ref[...] = kept_ref[:half] + decode(got_ref[:half], width)
-
-
-def combine(kept, got):
-    half, width = kept.shape[0] // 2, kept.shape[1]
-    return pl.pallas_call(
-        combine_kernel,
-        out_shape=(
-            jax.ShapeDtypeStruct((half, width + EXTRA), jnp.int16),
-            jax.ShapeDtypeStruct((half, width), jnp.float32),
-        ),
-        in_specs=[whole()] * 2,
-        out_specs=(whole(), whole()),
-        compiler_params=PARAMS,
-        name="combine",
-    )(kept, got)
+    )(candidates, term, gate, w_out, *arrays)
 
 
 def layer(history, candidates, hist_length, visible, w_proj, w_out):
+    width = w_out.shape[0]
     size = lax.axis_size("hist")
     masks = []
     bit = size // 2
@@ -361,20 +405,45 @@
     values, self_value = project_values(rows_both, w_proj, packed.shape[0])
     other_keys = swapped(keys, "hist", 1)
     other_values = swapped(values, "hist", 1)
-    gathered = packed
-    for step, mask in enumerate(masks[:-1]):
-        got = swapped(gathered, "hist", mask)
-        gathered = join(gathered, got) if step else project_queries(packed, got, w_proj)
-    far = swapped(gathered, "hist", masks[-1])
+    inner = packed
+    for step, mask in enumerate(masks[:-2]):
+        got = swapped(inner, "hist", mask)
+        inner = join(inner, got) if step else project_queries(packed, got, w_proj)
+    outer = swapped(inner, "hist", masks[-2])
+    far_inner = swapped(inner, "hist", masks[-1])
+    far_outer = swapped(outer, "hist", masks[-1])
     shards = (keys, values, other_keys, other_values)
-    kept = attend(gathered, *shards, HEADS, False)
-    sent = attend(far, *shards, HEADS, True)
-    gate, term = own(gathered, packed, w_proj, self_key, self_value, HEADS)
-    got = swapped(sent, "hist", masks[-1])
-    for mask in masks[-2::-1]:
-        sent, kept = combine(kept, got)
-        got = swapped(sent, "hist", mask)
-    return finish(candidates, kept, got, term, gate, w_out)
+    sent_inner, sent_outer = attend([far_inner, far_outer], shards, HEADS, True)
+    got_outer = swapped(sent_outer, "hist", masks[-1])
+    got_inner = swapped(sent_inner, "hist", masks[-1])
+    near_inner, near_outer = attend([inner, outer], shards, HEADS, False)
+    gate, term = own(inner, packed, w_proj, self_key, self_value, HEADS)
+    rows = packed.shape[0]
+    blocks = inner.shape[0] // rows
+    terms = [(near_outer, 0), (got_outer, 0)]
+    last = []
+    stage = len(masks) - 2
+    while True:
+        sides = 2 if blocks > 1 else 1
+        piece = blocks * rows // sides
+        sent = emit(
+            [[(array, first + side * piece) for array, first in terms] for side in range(sides)],
+            piece,
+            width,
+        )
+        got = [None] * sides
+        for side in reversed(range(sides)):
+            got[side] = swapped(sent[side], "hist", masks[stage])
+        last.append(got[0])
+        if sides == 1:
+            break
+        blocks //= 2
+        first = blocks * rows
+        terms = [(near_inner, first), (got_inner, first)]
+        terms += [(array, first) for array in last[:-1]] + [(got[1], 0)]
+        stage -= 1
+    terms = [(near_inner, 0), (got_inner, 0)] + [(array, 0) for array in last]
+    return finish(candidates, terms, term, gate, w_out)
 
 
 def solution(mesh):
@@ -387,6 +456,4 @@
         P(),
     )
     out_specs = P(("groups", "hist"), None)
-    return jax.shard_map(
-        layer, mesh=mesh, in_specs=in_specs, out_specs=out_specs, check_vma=False
-    )
+    return jax.shard_map(layer, mesh=mesh, in_specs=in_specs, out_specs=out_specs, check_vma=False)

time: 43.8 us -> 40 us (0.913)
  waiting for transfers between devices: 13.3 us -> 8.66 us
  starting transfers between devices: 15.4 us -> 17.3 us
  Pallas kernels: 11.7 us -> 10.6 us
    ppermute x8 -> x11, waiting for transfers between devices: 13.3 us -> 8.66 us  [swapped(): return lax.ppermute(shard, axis, [(i, i ^ mask) for i in range(size)])]
    ppermute x8 -> x11, starting transfers between devices: 15.4 us -> 17.3 us  [swapped(): return lax.ppermute(shard, axis, [(i, i ^ mask) for i in range(size)])]
    pallas_call x6 -> x5, Pallas kernels: 6.41 us -> 5.35 us  [the longest x2 3.73 us: attend(): pl.pallas_call(body, out_shape=[out] * blocks, in_specs=[whole()] * (bloc...]
  transfers between devices with their start and end apart: 8 -> 11, of which waited for: 6 -> 6; matrix products, arithmetic and copies ran while one was open for 0% -> 0% of each run, Pallas kernels for 7% -> 11%
where the time goes in v3:
time: 40 us; the launch traced here: 39.8 us
  starting transfers between devices  17.3 us (43%)
  Pallas kernels  10.6 us (26%)
  waiting for transfers between devices  8.66 us (22%)
  local copies, waits for them, and re-layouts  2.52 us (6%)
  between operations  0.75 us (2%)
    ppermute x11, starting transfers between devices, swapped(): return lax.ppermute(shard, axis, [(i, i ^ mask) for i in range(size)])  17.3 us
    ppermute x11, waiting for transfers between devices, swapped(): return lax.ppermute(shard, axis, [(i, i ^ mask) for i in range(size)])  8.66 us
    pallas_call x2, Pallas kernels, attend(): pl.pallas_call(body, out_shape=[out] * blocks, in_specs=[whole()] * (bloc...  3.73 us
    unnamed x8, local copies, waits for them, and re-layouts  2.52 us
    pallas_call x1, Pallas kernels, project_keys(): pl.pallas_call(body, out_shape=(jax.ShapeDtypeStruct((n_keys, width), jnp...  1.85 us
    pallas_call x1, Pallas kernels, project_values(): pl.pallas_call(body, out_shape=(jax.ShapeDtypeStruct((n_keys, width), jnp...  1.43 us
    pallas_call x1, Pallas kernels, finish(): pl.pallas_call(body, out_shape=jax.ShapeDtypeStruct(candidates.shape, jnp...  1.25 us
    pallas_call x1, Pallas kernels, begin(): pl.pallas_call(begin_kernel, out_shape=jax.ShapeDtypeStruct((rows, width...  1.11 us
  transfers between devices with their start and end apart: 11, of which 6 were waited for; matrix products, arithmetic and copies ran while one was open for 0% of the time, Pallas kernels for 11%

profile of v3, /device:TPU:0, one launch (start us, length us, event | category | flops | bytes accessed | tf_op | source)
XLA Modules:
  0.0 39.8 jit_solution(5089921601051440514)
XLA Ops:
  0.7 0.0 copy-start
  0.7 0.0 copy-start.2
  0.7 1.1 %begin.1.packed_ref.refs_1_ = bf16[16,1152]{1,0:T(8,128)(2,1)S(1)} custom-call(s32[1]{0:T(128)S(6)} %copy.7.length_ref, bf16[16,1024]{1,0:T(8,128)(2,1)} %cand_ref.3, s32[1,16]{1,0:T(1,128)} %bitcast.1), custom_call_target="tpu_custom_call" | custom-call | flops 6442450944 | bytes 20971520 | tf_op jit(solution)/shard_map/begin/pallas_call | solution.py:96
  1.8 2.3 %copy-done = bf16[1024,4096]{1,0:T(8,128)(2,1)S(1)} copy-done((bf16[1024,4096]{1,0:T(8,128)(2,1)S(1)}, bf16[1024,4096]{1,0:T(8,128)(2,1)}, u32[]{:S(2)}) %copy-start) | copy-done | bytes 8388632
  4.1 0.2 copy-done.2
  4.3 1.9 %keys.1 = (bf16[512,1024]{1,0:T(8,128)(2,1)S(1)}, bf16[16,1024]{1,0:T(8,128)(2,1)S(1)}, bf16[528,1024]{1,0:T(8,128)(2,1)S(1)}) custom-call(bf16[512,1024]{1,0:T(8,128)(2,1)S(1)} %copy-done.2, bf16[16,1152]{1,0:T(8,128)(2,1)S(1)} %begin.1.packed_ref.refs_1_, bf16[1024,4096]{1,0:T(8,128)(2,1)S(1)} %copy-done), custom_call_target="tpu_custom_call" | custom-call | tf_op jit(solution)/shard_map/keys/pallas_call | solution.py:138
  6.2 0.6 %collective-permute-start.2 = (bf16[512,1024]{1,0:T(8,128)(2,1)S(1)}, bf16[512,1024]{1,0:T(8,128)(2,1)S(1)}, u32[]{:S(2)}, u32[]{:S(2)}) collective-permute-start(bf16[512,1024]{1,0:T(8,128)(2,1)S(1)} %get-tuple-element.23.refs_2_), channel_id=1, source_target_pairs={{0,1},{1,0},{2,3},{3,2},{4,5},{5,4},{6,7},{7,6},{8,9},{9,8},{10,11... | collective-permute-start | bytes 3145736 | tf_op jit(solution)/shard_map/ppermute | solution.py:19
  6.7 1.4 %values.1 = (bf16[512,1024]{1,0:T(8,128)(2,1)S(1)}, bf16[16,1024]{1,0:T(8,128)(2,1)S(1)}) custom-call(bf16[528,1024]{1,0:T(8,128)(2,1)S(1)} %get-tuple-element.19.rows_ref, bf16[1024,4096]{1,0:T(8,128)(2,1)S(1)} %copy-done), custom_call_target="tpu_custom_call" | custom-call | tf_op jit(solution)/shard_map/values/pallas_call | solution.py:160
  8.2 0.1 collective-permute-start.3
  8.2 3.7 %collective-permute-start = (bf16[16,1152]{1,0:T(8,128)(2,1)S(1)}, bf16[16,1152]{1,0:T(8,128)(2,1)S(1)}, u32[]{:S(2)}, u32[]{:S(2)}) collective-permute-start(bf16[16,1152]{1,0:T(8,128)(2,1)S(1)} %begin.1.packed_ref.refs_1_), channel_id=1, source_target_pairs={{0,9},{1,8},{2,11},{3,10},{4,13},{5,12},{6,15},{7,14},{8,1},{9,0},... | collective-permute-start | bytes 110600 | tf_op jit(solution)/shard_map/ppermute | solution.py:19
  12.0 1.6 %collective-permute-done.got_ref = bf16[16,1152]{1,0:T(8,128)(2,1)S(1)} collective-permute-done((bf16[16,1152]{1,0:T(8,128)(2,1)S(1)}, bf16[16,1152]{1,0:T(8,128)(2,1)S(1)}, u32[]{:S(2)}, u32[]{:S(2)}) %collective-permute-start) | collective-permute-done | bytes 36896 | tf_op jit(solution)/shard_map/ppermute | solution.py:19
  13.6 0.5 %queries.1.refs_0_ = bf16[32,1152]{1,0:T(8,128)(2,1)S(1)} custom-call(bf16[16,1152]{1,0:T(8,128)(2,1)S(1)} %begin.1.packed_ref.refs_1_, bf16[16,1152]{1,0:T(8,128)(2,1)S(1)} %collective-permute-done.got_ref, bf16[1024,4096]{1,0:T(8,128)(2,1)S(1)} %copy-done), custom_call_target="tpu_custom_call" | custom-call | tf_op jit(solution)/shard_map/queries/pallas_call | solution.py:191
  14.1 1.9 %collective-permute-start.1 = (bf16[32,1152]{1,0:T(8,128)(2,1)S(1)}, bf16[32,1152]{1,0:T(8,128)(2,1)S(1)}, u32[]{:S(2)}, u32[]{:S(2)}) collective-permute-start(bf16[32,1152]{1,0:T(8,128)(2,1)S(1)} %queries.1.refs_0_), channel_id=1, source_target_pairs={{0,5},{1,4},{2,7},{3,6},{4,1},{5,0},{6,3},{7,2},{8,13},{9,12},{10,... | collective-permute-start | bytes 221192 | tf_op jit(solution)/shard_map/ppermute | solution.py:19
  16.0 1.7 %collective-permute-start.4 = (bf16[32,1152]{1,0:T(8,128)(2,1)S(1)}, bf16[32,1152]{1,0:T(8,128)(2,1)S(1)}, u32[]{:S(2)}, u32[]{:S(2)}) collective-permute-start(bf16[32,1152]{1,0:T(8,128)(2,1)S(1)} %queries.1.refs_0_), channel_id=1, source_target_pairs={{0,3},{1,2},{2,1},{3,0},{4,7},{5,6},{6,5},{7,4},{8,11},{9,10},{10,... | collective-permute-start | bytes 221192 | tf_op jit(solution)/shard_map/ppermute | solution.py:19
  17.7 0.8 %collective-permute-done.1.refs_1_ = bf16[32,1152]{1,0:T(8,128)(2,1)S(1)} collective-permute-done((bf16[32,1152]{1,0:T(8,128)(2,1)S(1)}, bf16[32,1152]{1,0:T(8,128)(2,1)S(1)}, u32[]{:S(2)}, u32[]{:S(2)}) %collective-permute-start.1) | collective-permute-done | bytes 73760 | tf_op jit(solution)/shard_map/ppermute | solution.py:19
  18.5 2.0 %collective-permute-start.5 = (bf16[32,1152]{1,0:T(8,128)(2,1)S(1)}, bf16[32,1152]{1,0:T(8,128)(2,1)S(1)}, u32[]{:S(2)}, u32[]{:S(2)}) collective-permute-start(bf16[32,1152]{1,0:T(8,128)(2,1)S(1)} %collective-permute-done.1.refs_1_), channel_id=1, source_target_pairs={{0,3},{1,2},{2,1},{3,0},{4,7},{5,6},{6,5},{7,4},{8,11},{9,10},{10,... | collective-permute-start | bytes 221192 | tf_op jit(solution)/shard_map/ppermute | solution.py:19
  20.5 0.0 collective-permute-done.4.refs_0_
  20.5 2.6 %collective-permute-done.5.refs_1_ = bf16[32,1152]{1,0:T(8,128)(2,1)S(1)} collective-permute-done((bf16[32,1152]{1,0:T(8,128)(2,1)S(1)}, bf16[32,1152]{1,0:T(8,128)(2,1)S(1)}, u32[]{:S(2)}, u32[]{:S(2)}) %collective-permute-start.5) | collective-permute-done | bytes 73760 | tf_op jit(solution)/shard_map/ppermute | solution.py:19
  23.1 0.0 collective-permute-done.2.refs_4_
  23.1 0.0 collective-permute-done.3.refs_5_
  23.1 1.9 %shard_map.65 = (s16[32,1152]{1,0:T(8,128)(2,1)S(1)}, s16[32,1152]{1,0:T(8,128)(2,1)S(1)}) custom-call(bf16[32,1152]{1,0:T(8,128)(2,1)S(1)} %collective-permute-done.4.refs_0_, bf16[32,1152]{1,0:T(8,128)(2,1)S(1)} %collective-permute-done.5.refs_1_, bf16[512,1024]{1,0:T(8,128)(2,1)S(1)} %get-tuple-element.23.refs_2_, ...), custom_call_target="tpu_custom_call" | custom-call | tf_op jit(solution)/shard_map/pallas_call | solution.py:280
  25.0 1.5 %collective-permute-start.7 = (s16[32,1152]{1,0:T(8,128)(2,1)S(1)}, s16[32,1152]{1,0:T(8,128)(2,1)S(1)}, u32[]{:S(2)}, u32[]{:S(2)}) collective-permute-start(s16[32,1152]{1,0:T(8,128)(2,1)S(1)} %get-tuple-element.28), channel_id=1, source_target_pairs={{0,3},{1,2},{2,1},{3,0},{4,7},{5,6},{6,5},{7,4},{8,11},{9,10},{10,... | collective-permute-start | bytes 221192 | tf_op jit(solution)/shard_map/ppermute | solution.py:19
  26.4 0.3 collective-permute-start.6
  26.8 1.8 %shard_map.64 = (f32[32,1024]{1,0:T(8,128)S(1)}, f32[32,1024]{1,0:T(8,128)S(1)}) custom-call(bf16[32,1152]{1,0:T(8,128)(2,1)S(1)} %queries.1.refs_0_, bf16[32,1152]{1,0:T(8,128)(2,1)S(1)} %collective-permute-done.1.refs_1_, bf16[512,1024]{1,0:T(8,128)(2,1)S(1)} %get-tuple-element.23.refs_2_, bf16[512,1024]{1,0:T(8,128)(2,1)S(1)} %get-tuple-element.24.refs_3_, ...), custom_call_target="tpu_custom_call" | custom-call | tf_op jit(solution)/shard_map/pallas_call | solution.py:280
  28.6 0.7 %collective-permute-done.7.refs_1_ = s16[32,1152]{1,0:T(8,128)(2,1)S(1)} collective-permute-done((s16[32,1152]{1,0:T(8,128)(2,1)S(1)}, s16[32,1152]{1,0:T(8,128)(2,1)S(1)}, u32[]{:S(2)}, u32[]{:S(2)}) %collective-permute-start.7) | collective-permute-done | bytes 73760 | tf_op jit(solution)/shard_map/ppermute | solution.py:19
  29.3 0.2 emit.2
  29.5 2.3 %collective-permute-start.9 = (s16[16,1152]{1,0:T(8,128)(2,1)S(1)}, s16[16,1152]{1,0:T(8,128)(2,1)S(1)}, u32[]{:S(2)}, u32[]{:S(2)}) collective-permute-start(s16[16,1152]{1,0:T(8,128)(2,1)S(1)} %get-tuple-element.30), channel_id=1, source_target_pairs={{0,5},{1,4},{2,7},{3,6},{4,1},{5,0},{6,3},{7,2},{8,13},{9,12},{10,... | collective-permute-start | bytes 110600 | tf_op jit(solution)/shard_map/ppermute | solution.py:19
  31.8 0.1 collective-permute-start.8
  31.9 0.0 collective-permute-done.6.refs_1_
  31.9 1.7 %collective-permute-done.9.refs_2_ = s16[16,1152]{1,0:T(8,128)(2,1)S(1)} collective-permute-done((s16[16,1152]{1,0:T(8,128)(2,1)S(1)}, s16[16,1152]{1,0:T(8,128)(2,1)S(1)}, u32[]{:S(2)}, u32[]{:S(2)}) %collective-permute-start.9) | collective-permute-done | bytes 36896 | tf_op jit(solution)/shard_map/ppermute | solution.py:19
  33.6 0.2 emit.3
  33.8 3.1 %collective-permute-start.10 = (s16[16,1152]{1,0:T(8,128)(2,1)S(1)}, s16[16,1152]{1,0:T(8,128)(2,1)S(1)}, u32[]{:S(2)}, u32[]{:S(2)}) collective-permute-start(s16[16,1152]{1,0:T(8,128)(2,1)S(1)} %emit.3), channel_id=1, source_target_pairs={{0,9},{1,8},{2,11},{3,10},{4,13},{5,12},{6,15},{7,14},{8,1},{9,0},... | collective-permute-start | bytes 110600 | tf_op jit(solution)/shard_map/ppermute | solution.py:19
  36.9 0.0 copy-start.1
  36.9 0.0 copy-start.3
  36.9 0.4 own.1
  37.3 0.0 collective-permute-done.8.refs_2_
  37.3 1.2 %collective-permute-done.10.refs_3_ = s16[16,1152]{1,0:T(8,128)(2,1)S(1)} collective-permute-done((s16[16,1152]{1,0:T(8,128)(2,1)S(1)}, s16[16,1152]{1,0:T(8,128)(2,1)S(1)}, u32[]{:S(2)}, u32[]{:S(2)}) %collective-permute-start.10) | collective-permute-done | bytes 36896 | tf_op jit(solution)/shard_map/ppermute | solution.py:19
  38.6 0.0 copy-done.1
  38.6 0.0 copy-done.3
  38.6 1.2 %finish.1 = bf16[16,1024]{1,0:T(8,128)(2,1)} custom-call(bf16[16,1024]{1,0:T(8,128)(2,1)S(1)} %copy-done.3, f32[16,1024]{1,0:T(8,128)S(1)} %get-tuple-element.21.term_ref, bf16[16,1024]{1,0:T(8,128)(2,1)S(1)} %get-tuple-element.22.gate_ref, bf16[1024,1024]{1,0:T(8,128)(2,1)S(1)} %copy-done.1, f32[32,1024]{1,0:T(8,128)S(1)} %get-tuple-element.25.refs_0_, ...), custom_call_target="tpu_custom_call" | custom-call | tf_op jit(solution)/shard_map/finish/pallas_call | solution.py:385
Async XLA Ops:
  0.7 3.4 %copy-start = (bf16[1024,4096]{1,0:T(8,128)(2,1)S(1)}, bf16[1024,4096]{1,0:T(8,128)(2,1)}, u32[]{:S(2)}) copy-start(bf16[1024,4096]{1,0:T(8,128)(2,1)} %refs_2_.1) | copy-start | bytes 25165828
  0.7 3.6 %copy-start.2 = (bf16[512,1024]{1,0:T(8,128)(2,1)S(1)}, bf16[512,1024]{1,0:T(8,128)(2,1)}, u32[]{:S(2)}) copy-start(bf16[512,1024]{1,0:T(8,128)(2,1)} %hist_ref.1) | copy-start | bytes 3145732
  6.2 16.9 %collective-permute-start.2 = (bf16[512,1024]{1,0:T(8,128)(2,1)S(1)}, bf16[512,1024]{1,0:T(8,128)(2,1)S(1)}, u32[]{:S(2)}, u32[]{:S(2)}) collective-permute-start(bf16[512,1024]{1,0:T(8,128)(2,1)S(1)} %get-tuple-element.23.refs_2_), channel_id=1, source_target_pairs={{0,1},{1,0},{2,3},{3,2},{4,5},{5,4},{6,7},{7,6},{8,9},{9,8},{10,11... | collective-permute-start | bytes 3145736 | tf_op jit(solution)/shard_map/ppermute | solution.py:19
  8.2 14.9 %collective-permute-start.3 = (bf16[512,1024]{1,0:T(8,128)(2,1)S(1)}, bf16[512,1024]{1,0:T(8,128)(2,1)S(1)}, u32[]{:S(2)}, u32[]{:S(2)}) collective-permute-start(bf16[512,1024]{1,0:T(8,128)(2,1)S(1)} %get-tuple-element.24.refs_3_), channel_id=1, source_target_pairs={{0,1},{1,0},{2,3},{3,2},{4,5},{5,4},{6,7},{7,6},{8,9},{9,8},{10,11... | collective-permute-start | bytes 3145736 | tf_op jit(solution)/shard_map/ppermute | solution.py:19
  8.2 5.4 %collective-permute-start = (bf16[16,1152]{1,0:T(8,128)(2,1)S(1)}, bf16[16,1152]{1,0:T(8,128)(2,1)S(1)}, u32[]{:S(2)}, u32[]{:S(2)}) collective-permute-start(bf16[16,1152]{1,0:T(8,128)(2,1)S(1)} %begin.1.packed_ref.refs_1_), channel_id=1, source_target_pairs={{0,9},{1,8},{2,11},{3,10},{4,13},{5,12},{6,15},{7,14},{8,1},{9,0},... | collective-permute-start | bytes 110600 | tf_op jit(solution)/shard_map/ppermute | solution.py:19
  14.1 4.4 %collective-permute-start.1 = (bf16[32,1152]{1,0:T(8,128)(2,1)S(1)}, bf16[32,1152]{1,0:T(8,128)(2,1)S(1)}, u32[]{:S(2)}, u32[]{:S(2)}) collective-permute-start(bf16[32,1152]{1,0:T(8,128)(2,1)S(1)} %queries.1.refs_0_), channel_id=1, source_target_pairs={{0,5},{1,4},{2,7},{3,6},{4,1},{5,0},{6,3},{7,2},{8,13},{9,12},{10,... | collective-permute-start | bytes 221192 | tf_op jit(solution)/shard_map/ppermute | solution.py:19
  16.0 4.5 %collective-permute-start.4 = (bf16[32,1152]{1,0:T(8,128)(2,1)S(1)}, bf16[32,1152]{1,0:T(8,128)(2,1)S(1)}, u32[]{:S(2)}, u32[]{:S(2)}) collective-permute-start(bf16[32,1152]{1,0:T(8,128)(2,1)S(1)} %queries.1.refs_0_), channel_id=1, source_target_pairs={{0,3},{1,2},{2,1},{3,0},{4,7},{5,6},{6,5},{7,4},{8,11},{9,10},{10,... | collective-permute-start | bytes 221192 | tf_op jit(solution)/shard_map/ppermute | solution.py:19
  18.5 4.5 %collective-permute-start.5 = (bf16[32,1152]{1,0:T(8,128)(2,1)S(1)}, bf16[32,1152]{1,0:T(8,128)(2,1)S(1)}, u32[]{:S(2)}, u32[]{:S(2)}) collective-permute-start(bf16[32,1152]{1,0:T(8,128)(2,1)S(1)} %collective-permute-done.1.refs_1_), channel_id=1, source_target_pairs={{0,3},{1,2},{2,1},{3,0},{4,7},{5,6},{6,5},{7,4},{8,11},{9,10},{10,... | collective-permute-start | bytes 221192 | tf_op jit(solution)/shard_map/ppermute | solution.py:19
  25.0 4.3 %collective-permute-start.7 = (s16[32,1152]{1,0:T(8,128)(2,1)S(1)}, s16[32,1152]{1,0:T(8,128)(2,1)S(1)}, u32[]{:S(2)}, u32[]{:S(2)}) collective-permute-start(s16[32,1152]{1,0:T(8,128)(2,1)S(1)} %get-tuple-element.28), channel_id=1, source_target_pairs={{0,3},{1,2},{2,1},{3,0},{4,7},{5,6},{6,5},{7,4},{8,11},{9,10},{10,... | collective-permute-start | bytes 221192 | tf_op jit(solution)/shard_map/ppermute | solution.py:19
  26.4 5.5 %collective-permute-start.6 = (s16[32,1152]{1,0:T(8,128)(2,1)S(1)}, s16[32,1152]{1,0:T(8,128)(2,1)S(1)}, u32[]{:S(2)}, u32[]{:S(2)}) collective-permute-start(s16[32,1152]{1,0:T(8,128)(2,1)S(1)} %get-tuple-element.26), channel_id=1, source_target_pairs={{0,3},{1,2},{2,1},{3,0},{4,7},{5,6},{6,5},{7,4},{8,11},{9,10},{10,... | collective-permute-start | bytes 221192 | tf_op jit(solution)/shard_map/ppermute | solution.py:19
  29.5 4.1 %collective-permute-start.9 = (s16[16,1152]{1,0:T(8,128)(2,1)S(1)}, s16[16,1152]{1,0:T(8,128)(2,1)S(1)}, u32[]{:S(2)}, u32[]{:S(2)}) collective-permute-start(s16[16,1152]{1,0:T(8,128)(2,1)S(1)} %get-tuple-element.30), channel_id=1, source_target_pairs={{0,5},{1,4},{2,7},{3,6},{4,1},{5,0},{6,3},{7,2},{8,13},{9,12},{10,... | collective-permute-start | bytes 110600 | tf_op jit(solution)/shard_map/ppermute | solution.py:19
  31.8 5.5 %collective-permute-start.8 = (s16[16,1152]{1,0:T(8,128)(2,1)S(1)}, s16[16,1152]{1,0:T(8,128)(2,1)S(1)}, u32[]{:S(2)}, u32[]{:S(2)}) collective-permute-start(s16[16,1152]{1,0:T(8,128)(2,1)S(1)} %get-tuple-element.29), channel_id=1, source_target_pairs={{0,5},{1,4},{2,7},{3,6},{4,1},{5,0},{6,3},{7,2},{8,13},{9,12},{10,... | collective-permute-start | bytes 110600 | tf_op jit(solution)/shard_map/ppermute | solution.py:19
  33.8 4.8 %collective-permute-start.10 = (s16[16,1152]{1,0:T(8,128)(2,1)S(1)}, s16[16,1152]{1,0:T(8,128)(2,1)S(1)}, u32[]{:S(2)}, u32[]{:S(2)}) collective-permute-start(s16[16,1152]{1,0:T(8,128)(2,1)S(1)} %emit.3), channel_id=1, source_target_pairs={{0,9},{1,8},{2,11},{3,10},{4,13},{5,12},{6,15},{7,14},{8,1},{9,0},... | collective-permute-start | bytes 110600 | tf_op jit(solution)/shard_map/ppermute | solution.py:19
  36.9 1.6 %copy-start.1 = (bf16[1024,1024]{1,0:T(8,128)(2,1)S(1)}, bf16[1024,1024]{1,0:T(8,128)(2,1)}, u32[]{:S(2)}) copy-start(bf16[1024,1024]{1,0:T(8,128)(2,1)} %w_ref.7) | copy-start | bytes 6291460
  36.9 1.6 %copy-start.3 = (bf16[16,1024]{1,0:T(8,128)(2,1)S(1)}, bf16[16,1024]{1,0:T(8,128)(2,1)}, u32[]{:S(2)}) copy-start(bf16[16,1024]{1,0:T(8,128)(2,1)} %cand_ref.3) | copy-start | bytes 98308

commit v4 on v3

--- a/solution.py
+++ b/solution.py
@@ -50,16 +50,8 @@
     return code[:, :width] * (jnp.exp2(code[:, width : width + 1]) * (1 / STEPS))
 
 
-def stay(array):
-    return pltpu.with_memory_space_constraint(array, pltpu.HBM)
-
-
 def near_by(*arrays):
     return [pltpu.with_memory_space_constraint(array, pltpu.VMEM) for array in arrays]
-
-
-def hbm():
-    return pl.BlockSpec(memory_space=pltpu.HBM)
 
 
 def limits_of(packed, width):
@@ -68,47 +60,35 @@
     return high * 256 + low
 
 
-def begin_kernel(length_ref, cand_ref, visible_ref, out_ref, cand, visible, sems):
-    rows, width = cand.shape
-    loads = [
-        pltpu.make_async_copy(cand_ref, cand, sems.at[0]),
-        pltpu.make_async_copy(visible_ref, visible, sems.at[1]),
-    ]
-    for load in loads:
-        load.start()
-    loads[1].wait()
-    seen = jnp.broadcast_to(visible[...], (rows, rows))
+def spark():
+    def body(out_ref):
+        out_ref[...] = jnp.zeros_like(out_ref)
+
+    return pl.pallas_call(
+        body,
+        out_shape=jax.ShapeDtypeStruct((8, 128), jnp.float32),
+        out_specs=whole(),
+        compiler_params=PARAMS,
+        cost_estimate=pl.CostEstimate(flops=6 * 10**9, bytes_accessed=2 * 10**7, transcendentals=0),
+        name="spark",
+    )()
+
+
+def normed(rows):
+    return norm(rows.astype(jnp.float32)).astype(jnp.bfloat16)
+
+
+def limit_columns(visible, length):
+    rows = visible.shape[1]
     diagonal = lax.broadcasted_iota(jnp.int32, (rows, rows), 0) == lax.broadcasted_iota(
         jnp.int32, (rows, rows), 1
     )
-    limit = jnp.minimum(seen, length_ref[0]).astype(jnp.float32)
+    limit = jnp.minimum(jnp.broadcast_to(visible, (rows, rows)), length).astype(jnp.float32)
     limit = jnp.sum(jnp.where(diagonal, limit, 0.0), axis=1, keepdims=True)
     high = jnp.floor(limit * (1 / 256))
     low = limit - high * 256
     lane = lax.broadcasted_iota(jnp.int32, (rows, EXTRA), 1)
-    out_ref[:, width:] = jnp.where(lane == 0, high, low).astype(jnp.bfloat16)
-    loads[0].wait()
-    out_ref[:, :width] = norm(cand[...].astype(jnp.float32)).astype(jnp.bfloat16)
-
-
-def begin(candidates, hist_length, visible):
-    rows, width = candidates.shape
-    return pl.pallas_call(
-        begin_kernel,
-        out_shape=jax.ShapeDtypeStruct((rows, width + EXTRA), jnp.bfloat16),
-        in_specs=[pl.BlockSpec(memory_space=pltpu.SMEM)] + [hbm()] * 2,
-        out_specs=whole(),
-        scratch_shapes=[
-            pltpu.VMEM((rows, width), jnp.bfloat16),
-            pltpu.VMEM((1, rows), jnp.int32),
-            pltpu.SemaphoreType.DMA((2,)),
-        ],
-        compiler_params=PARAMS,
-        cost_estimate=pl.CostEstimate(
-            flops=6 * width**3, bytes_accessed=20 * width**2, transcendentals=0
-        ),
-        name="begin",
-    )(hist_length, stay(candidates), stay(visible.reshape(1, rows)))
+    return jnp.where(lane == 0, high, low).astype(jnp.bfloat16)
 
 
 def project(rows_ref, w_ref, first, tile, n_keys, out_ref, self_ref):
@@ -125,14 +105,14 @@
         self_ref[:, at : at + tile] = made[n_keys:]
 
 
-def project_keys(history, packed, w_proj):
+def project_keys(history, candidates, w_proj, first_op):
     n_keys, width = history.shape
-    rows = packed.shape[0]
+    rows = candidates.shape[0]
     tile = min(256, width)
 
-    def body(hist_ref, packed_ref, w_ref, key_ref, self_ref, rows_ref):
-        rows_ref[n_keys:] = packed_ref[:, :width]
-        rows_ref[:n_keys] = norm(hist_ref[...].astype(jnp.float32)).astype(jnp.bfloat16)
+    def body(hist_ref, cand_ref, w_ref, first_ref, key_ref, self_ref, rows_ref):
+        rows_ref[n_keys:] = normed(cand_ref[...])
+        rows_ref[:n_keys] = normed(hist_ref[...])
         project(rows_ref, w_ref, 2 * width, tile, n_keys, key_ref, self_ref)
 
     return pl.pallas_call(
@@ -142,11 +122,11 @@
             jax.ShapeDtypeStruct((rows, width), jnp.bfloat16),
             jax.ShapeDtypeStruct((n_keys + rows, width), jnp.bfloat16),
         ),
-        in_specs=[whole()] * 3,
+        in_specs=[whole()] * 4,
         out_specs=[whole()] * 3,
         compiler_params=PARAMS,
         name="keys",
-    )(*near_by(history, packed, w_proj))
+    )(*near_by(history, candidates, w_proj, first_op))
 
 
 def project_values(rows_both, w_proj, rows):
@@ -170,15 +150,14 @@
     )(*near_by(rows_both, w_proj))
 
 
-def project_queries(packed, got, w_proj):
-    rows = packed.shape[0]
-    width = w_proj.shape[0]
+def project_queries(candidates, got, visible, got_visible, hist_length, w_proj):
+    rows, width = candidates.shape
     tile = min(256, width)
 
-    def body(packed_ref, got_ref, w_ref, out_ref):
-        out_ref[:rows, width:] = packed_ref[:, width:]
-        out_ref[rows:, width:] = got_ref[:, width:]
-        both = jnp.concatenate([packed_ref[:, :width], got_ref[:, :width]], axis=0)
+    def body(length_ref, cand_ref, got_ref, visible_ref, got_visible_ref, w_ref, out_ref):
+        out_ref[:rows, width:] = limit_columns(visible_ref[...], length_ref[0])
+        out_ref[rows:, width:] = limit_columns(got_visible_ref[...], length_ref[0])
+        both = jnp.concatenate([normed(cand_ref[...]), normed(got_ref[...])], axis=0)
         for at in range(0, width, tile):
             out_ref[:, at : at + tile] = silu(
                 jnp.dot(
@@ -190,12 +169,15 @@
 
     return pl.pallas_call(
         body,
-        out_shape=jax.ShapeDtypeStruct((2 * rows, packed.shape[1]), jnp.bfloat16),
-        in_specs=[whole()] * 3,
+        out_shape=jax.ShapeDtypeStruct((2 * rows, width + EXTRA), jnp.bfloat16),
+        in_specs=[pl.BlockSpec(memory_space=pltpu.SMEM)] + [whole()] * 5,
         out_specs=whole(),
         compiler_params=PARAMS,
         name="queries",
-    )(*near_by(packed, got, w_proj))
+    )(
+        hist_length,
+        *near_by(candidates, got, visible.reshape(1, rows), got_visible.reshape(1, rows), w_proj),
+    )
 
 
 def join(first, second):
@@ -248,7 +230,8 @@
         cols = slice(head * size, (head + 1) * size)
         total = None
         for side, (_, v) in enumerate(sides):
-            weight = (silu(scores[side] * size ** (-0.5)) * share[side]).astype(jnp.bfloat16)
+            half = scores[side] * (0.5 * size ** (-0.5))
+            weight = ((half + half * jnp.tanh(half)) * share[side]).astype(jnp.bfloat16)
             part = jnp.dot(weight, v[:, cols], preferred_element_type=jnp.float32)
             total = part if total is None else total + part
         acc_ref[:, cols] = total
@@ -256,42 +239,45 @@
     return made - jnp.mean(made, axis=-1, keepdims=True)
 
 
-def attend(queries, shards, heads, coded):
+def attend(queries, shards, heads, parts, coded):
     rows = queries[0].shape[0]
     _, width = shards[0].shape
     blocks = len(queries)
+    pieces = [rows // part for part in parts for _ in range(part)]
 
     def body(*refs):
         ins, shard_refs, outs = refs[:blocks], refs[blocks : blocks + 4], refs[blocks + 4 : -1]
         query = jnp.concatenate([ref[...] for ref in ins], axis=0)
         made = attend_kernel(heads, query, *shard_refs, refs[-1])
-        for block, out_ref in enumerate(outs):
-            part = made[block * rows : (block + 1) * rows]
+        first = 0
+        for piece, out_ref in zip(pieces, outs):
+            part = made[first : first + piece]
+            first += piece
             if coded:
                 encode(part, out_ref)
             else:
                 out_ref[...] = part
 
-    out = (
-        jax.ShapeDtypeStruct((rows, width + EXTRA), jnp.int16)
-        if coded
-        else jax.ShapeDtypeStruct((rows, width), jnp.float32)
-    )
-    return pl.pallas_call(
-        body,
-        out_shape=[out] * blocks,
+    return pl.pallas_call(
+        body,
+        out_shape=[
+            jax.ShapeDtypeStruct((piece, width + EXTRA), jnp.int16)
+            if coded
+            else jax.ShapeDtypeStruct((piece, width), jnp.float32)
+            for piece in pieces
+        ],
         in_specs=[whole()] * (blocks + 4),
-        out_specs=[whole()] * blocks,
+        out_specs=[whole()] * len(pieces),
         scratch_shapes=[pltpu.VMEM((blocks * rows, width), jnp.float32)],
         compiler_params=PARAMS,
     )(*near_by(*queries, *shards))
 
 
-def own_kernel(heads, tile, query_ref, packed_ref, w_ref, key_ref, value_ref, gate_ref, term_ref):
+def own_kernel(heads, tile, query_ref, rows_ref, w_ref, key_ref, value_ref, gate_ref, term_ref):
     rows, width = key_ref.shape
     size = width // heads
     query = query_ref[:rows, :width].astype(jnp.float32)
-    inverse = 1.0 / (limits_of(packed_ref[...], width) + 1.0)
+    inverse = 1.0 / (limits_of(query_ref[:rows], width) + 1.0)
     products = query * key_ref[...].astype(jnp.float32)
     for head in range(heads):
         cols = slice(head * size, (head + 1) * size)
@@ -301,14 +287,14 @@
     for at in range(0, width, tile):
         gate_ref[:, at : at + tile] = silu(
             jnp.dot(
-                packed_ref[:, :width],
+                rows_ref[rows_ref.shape[0] - rows :],
                 w_ref[:, at : at + tile],
                 preferred_element_type=jnp.float32,
             )
         ).astype(jnp.bfloat16)
 
 
-def own(query, packed, w_proj, self_key, self_value, heads):
+def own(query, rows_both, w_proj, self_key, self_value, heads):
     rows, width = self_key.shape
     tile = min(256, width)
 
@@ -325,7 +311,7 @@
         out_specs=[whole()] * 2,
         compiler_params=PARAMS,
         name="own",
-    )(*near_by(query, packed, w_proj, self_key, self_value))
+    )(*near_by(query, rows_both, w_proj, self_key, self_value))
 
 
 def total_of(terms, refs, rows, width):
@@ -353,18 +339,17 @@
     return arrays, lists
 
 
-def emit(pieces, rows, width):
-    arrays, lists = placed(pieces)
+def emit(terms, rows, width):
+    arrays, (listed,) = placed([terms])
 
     def body(*refs):
-        for terms, out_ref in zip(lists, refs[len(arrays) :]):
-            encode(total_of(terms, refs, rows, width), out_ref)
-
-    return pl.pallas_call(
-        body,
-        out_shape=[jax.ShapeDtypeStruct((rows, width + EXTRA), jnp.int16)] * len(pieces),
+        encode(total_of(listed, refs, rows, width), refs[-1])
+
+    return pl.pallas_call(
+        body,
+        out_shape=jax.ShapeDtypeStruct((rows, width + EXTRA), jnp.int16),
         in_specs=[whole()] * len(arrays),
-        out_specs=[whole()] * len(pieces),
+        out_specs=whole(),
         compiler_params=PARAMS,
         name="emit",
     )(*arrays)
@@ -400,47 +385,51 @@
     while bit > 1:
         masks.append(bit | 1)
         bit //= 2
-    packed = begin(candidates, hist_length, visible)
-    keys, self_key, rows_both = project_keys(history, packed, w_proj)
-    values, self_value = project_values(rows_both, w_proj, packed.shape[0])
+    rows = candidates.shape[0]
+    first_op = spark()
+    keys, self_key, rows_both = project_keys(history, candidates, w_proj, first_op)
+    values, self_value = project_values(rows_both, w_proj, rows)
     other_keys = swapped(keys, "hist", 1)
     other_values = swapped(values, "hist", 1)
-    inner = packed
-    for step, mask in enumerate(masks[:-2]):
+    got = swapped(candidates, "hist", masks[0])
+    got_visible = swapped(visible, "hist", masks[0])
+    inner = project_queries(candidates, got, visible, got_visible, hist_length, w_proj)
+    for mask in masks[1:-2]:
         got = swapped(inner, "hist", mask)
-        inner = join(inner, got) if step else project_queries(packed, got, w_proj)
+        inner = join(inner, got)
     outer = swapped(inner, "hist", masks[-2])
     far_inner = swapped(inner, "hist", masks[-1])
     far_outer = swapped(outer, "hist", masks[-1])
     shards = (keys, values, other_keys, other_values)
-    sent_inner, sent_outer = attend([far_inner, far_outer], shards, HEADS, True)
-    got_outer = swapped(sent_outer, "hist", masks[-1])
+    blocks = inner.shape[0] // rows
+    sides = min(blocks, 2)
+    sent_inner, *sent_outer = attend([far_inner, far_outer], shards, HEADS, (1, sides), True)
+    got_outer = [None] * sides
+    for side in reversed(range(sides)):
+        got_outer[side] = swapped(sent_outer[side], "hist", masks[-1])
     got_inner = swapped(sent_inner, "hist", masks[-1])
-    near_inner, near_outer = attend([inner, outer], shards, HEADS, False)
-    gate, term = own(inner, packed, w_proj, self_key, self_value, HEADS)
-    rows = packed.shape[0]
-    blocks = inner.shape[0] // rows
-    terms = [(near_outer, 0), (got_outer, 0)]
+    near_inner, near_outer = attend([inner, outer], shards, HEADS, (1, 1), False)
+    gate, term = own(inner, rows_both, w_proj, self_key, self_value, HEADS)
+    piece = blocks * rows // sides
+    terms = [[(near_outer, side * piece), (got_outer[side], 0)] for side in range(sides)]
     last = []
     stage = len(masks) - 2
     while True:
-        sides = 2 if blocks > 1 else 1
-        piece = blocks * rows // sides
-        sent = emit(
-            [[(array, first + side * piece) for array, first in terms] for side in range(sides)],
-            piece,
-            width,
-        )
         got = [None] * sides
         for side in reversed(range(sides)):
-            got[side] = swapped(sent[side], "hist", masks[stage])
+            sent = emit(terms[side], piece, width)
+            got[side] = swapped(sent, "hist", masks[stage])
         last.append(got[0])
-        if sides == 1:
+        if blocks == 1:
             break
         blocks //= 2
-        first = blocks * rows
-        terms = [(near_inner, first), (got_inner, first)]
-        terms += [(array, first) for array in last[:-1]] + [(got[1], 0)]
+        sides = min(blocks, 2)
+        piece = blocks * rows // sides
+        terms = []
+        for side in range(sides):
+            first = blocks * rows + side * piece
+            terms.append([(near_inner, first), (got_inner, first)])
+            terms[-1] += [(array, first) for array in last[:-1]] + [(got[1], side * piece)]
         stage -= 1
     terms = [(near_inner, 0), (got_inner, 0)] + [(array, 0) for array in last]
     return finish(candidates, terms, term, gate, w_out)

time: 40 us -> 41 us (1.025)
  local copies, waits for them, and re-layouts: 2.52 us -> 3.74 us
  waiting for transfers between devices: 8.66 us -> 9.73 us
  starting transfers between devices: 17.3 us -> 16.7 us
  Pallas kernels: 10.6 us -> 10 us
    unnamed x8 -> x10, local copies, waits for them, and re-layouts: 2.52 us -> 3.74 us
    ppermute x11 -> x13, waiting for transfers between devices: 8.66 us -> 9.73 us  [swapped(): return lax.ppermute(shard, axis, [(i, i ^ mask) for i in range(size)])]
    pallas_call x6 -> x7, Pallas kernels: 5.69 us -> 5.05 us  [the longest x2 3.88 us: attend(): pl.pallas_call(body, out_shape=[jax.ShapeDtypeStruct((piece, width + EXTR...]
    ppermute x11 -> x13, starting transfers between devices: 17.3 us -> 16.7 us  [swapped(): return lax.ppermute(shard, axis, [(i, i ^ mask) for i in range(size)])]
  transfers between devices with their start and end apart: 11 -> 13, of which waited for: 6 -> 7; matrix products, arithmetic and copies ran while one was open for 0% -> 0% of each run, Pallas kernels for 11% -> 12%
where the time goes in v4:
time: 41 us; the launch traced here: 40.9 us
  starting transfers between devices  16.7 us (41%)
  Pallas kernels  10 us (24%)
  waiting for transfers between devices  9.73 us (24%)
  local copies, waits for them, and re-layouts  3.74 us (9%)
  between operations  0.76 us (2%)
    ppermute x13, starting transfers between devices, swapped(): return lax.ppermute(shard, axis, [(i, i ^ mask) for i in range(size)])  16.7 us
    ppermute x13, waiting for transfers between devices, swapped(): return lax.ppermute(shard, axis, [(i, i ^ mask) for i in range(size)])  9.73 us
    pallas_call x2, Pallas kernels, attend(): pl.pallas_call(body, out_shape=[jax.ShapeDtypeStruct((piece, width + EXTR...  3.88 us
    unnamed x10, local copies, waits for them, and re-layouts  3.74 us
    pallas_call x1, Pallas kernels, project_keys(): pl.pallas_call(body, out_shape=(jax.ShapeDtypeStruct((n_keys, width), jnp...  1.88 us
    pallas_call x1, Pallas kernels, project_values(): pl.pallas_call(body, out_shape=(jax.ShapeDtypeStruct((n_keys, width), jnp...  1.43 us
    pallas_call x1, Pallas kernels, finish(): pl.pallas_call(body, out_shape=jax.ShapeDtypeStruct(candidates.shape, jnp...  1.25 us
  transfers between devices with their start and end apart: 13, of which 7 were waited for; matrix products, arithmetic and copies ran while one was open for 0% of the time, Pallas kernels for 12%

profile of v4, /device:TPU:0, one launch (start us, length us, event | category | flops | bytes accessed | tf_op | source)
XLA Modules:
  0.0 40.9 jit_solution(11815563795126617884)
XLA Ops:
  0.0 0.0 copy-start.3
  0.0 0.0 copy-start.2
  0.0 0.0 copy-start
  0.0 0.7 %copy-done.3 = bf16[16,1024]{1,0:T(8,128)(2,1)S(1)} copy-done((bf16[16,1024]{1,0:T(8,128)(2,1)S(1)}, bf16[16,1024]{1,0:T(8,128)(2,1)}, u32[]{:S(2)}) %copy-start.3) | copy-done | bytes 32792
  0.8 0.5 %copy-done.2 = bf16[512,1024]{1,0:T(8,128)(2,1)S(1)} copy-done((bf16[512,1024]{1,0:T(8,128)(2,1)S(1)}, bf16[512,1024]{1,0:T(8,128)(2,1)}, u32[]{:S(2)}) %copy-start.2) | copy-done | bytes 1048600
  1.2 2.5 %copy-done = bf16[1024,4096]{1,0:T(8,128)(2,1)S(1)} copy-done((bf16[1024,4096]{1,0:T(8,128)(2,1)S(1)}, bf16[1024,4096]{1,0:T(8,128)(2,1)}, u32[]{:S(2)}) %copy-start) | copy-done | bytes 8388632
  3.7 1.9 %keys.1 = (bf16[512,1024]{1,0:T(8,128)(2,1)S(1)}, bf16[16,1024]{1,0:T(8,128)(2,1)S(1)}, bf16[528,1024]{1,0:T(8,128)(2,1)S(1)}) custom-call(bf16[512,1024]{1,0:T(8,128)(2,1)S(1)} %copy-done.2, bf16[16,1024]{1,0:T(8,128)(2,1)S(1)} %copy-done.3, bf16[1024,4096]{1,0:T(8,128)(2,1)S(1)} %copy-done, f32[8,128]{1,0:T(8,128)S(1)} %spark.1.first_ref), custom_call_target="tpu_custom_call" | custom-call | tf_op jit(solution)/shard_map/keys/pallas_call | solution.py:118
  5.6 0.6 %collective-permute-start.3 = (bf16[512,1024]{1,0:T(8,128)(2,1)S(1)}, bf16[512,1024]{1,0:T(8,128)(2,1)S(1)}, u32[]{:S(2)}, u32[]{:S(2)}) collective-permute-start(bf16[512,1024]{1,0:T(8,128)(2,1)S(1)} %get-tuple-element.22.refs_2_), channel_id=1, source_target_pairs={{0,1},{1,0},{2,3},{3,2},{4,5},{5,4},{6,7},{7,6},{8,9},{9,8},{10,11... | collective-permute-start | bytes 3145736 | tf_op jit(solution)/shard_map/ppermute | solution.py:19
  6.2 0.0 copy-start.4
  6.2 1.4 %values.1 = (bf16[512,1024]{1,0:T(8,128)(2,1)S(1)}, bf16[16,1024]{1,0:T(8,128)(2,1)S(1)}) custom-call(bf16[528,1024]{1,0:T(8,128)(2,1)S(1)} %get-tuple-element.17.rows_ref.refs_1_, bf16[1024,4096]{1,0:T(8,128)(2,1)S(1)} %copy-done), custom_call_target="tpu_custom_call" | custom-call | tf_op jit(solution)/shard_map/values/pallas_call | solution.py:140
  7.6 0.1 collective-permute-start.4
  7.7 3.7 %collective-permute-start = (bf16[16,1024]{1,0:T(8,128)(2,1)S(1)}, bf16[16,1024]{1,0:T(8,128)(2,1)S(1)}, u32[]{:S(2)}, u32[]{:S(2)}) collective-permute-start(bf16[16,1024]{1,0:T(8,128)(2,1)S(1)} %copy-done.3), channel_id=1, source_target_pairs={{0,9},{1,8},{2,11},{3,10},{4,13},{5,12},{6,15},{7,14},{8,1},{9,0},... | collective-permute-start | bytes 98312 | tf_op jit(solution)/shard_map/ppermute | solution.py:19
  11.4 0.0 copy-done.4
  11.4 0.1 collective-permute-start.1
  12.2 3.2 %collective-permute-done.1 = s32[16]{0:T(128)S(1)} collective-permute-done((s32[16]{0:T(128)S(1)}, s32[16]{0:T(128)S(1)}, u32[]{:S(2)}, u32[]{:S(2)}) %collective-permute-start.1) | collective-permute-done | bytes 96 | tf_op jit(solution)/shard_map/ppermute | solution.py:19
  15.3 0.0 collective-permute-done.got_ref
  15.3 0.6 %queries.1.refs_0_ = bf16[32,1152]{1,0:T(8,128)(2,1)S(1)} custom-call(s32[1]{0:T(128)S(6)} %copy.7.length_ref, bf16[16,1024]{1,0:T(8,128)(2,1)S(1)} %copy-done.3, bf16[16,1024]{1,0:T(8,128)(2,1)S(1)} %collective-permute-done.got_ref, s32[1,16]{1,0:T(1,128)S(1)} %bitcast.2, s32[1,16]{1,0:T(1,128)S(1)} %bitcast.3, bf16[1024,4096]{1,0:T(8,128)(2,1)S(1)} %copy-done), custom_call_target="tpu_custom_call" | custom-call | tf_op jit(solution)/shard_map/queries/pallas_call | solution.py:170
  16.0 1.7 %collective-permute-start.2 = (bf16[32,1152]{1,0:T(8,128)(2,1)S(1)}, bf16[32,1152]{1,0:T(8,128)(2,1)S(1)}, u32[]{:S(2)}, u32[]{:S(2)}) collective-permute-start(bf16[32,1152]{1,0:T(8,128)(2,1)S(1)} %queries.1.refs_0_), channel_id=1, source_target_pairs={{0,5},{1,4},{2,7},{3,6},{4,1},{5,0},{6,3},{7,2},{8,13},{9,12},{10,... | collective-permute-start | bytes 221192 | tf_op jit(solution)/shard_map/ppermute | solution.py:19
  17.7 1.2 %collective-permute-start.5 = (bf16[32,1152]{1,0:T(8,128)(2,1)S(1)}, bf16[32,1152]{1,0:T(8,128)(2,1)S(1)}, u32[]{:S(2)}, u32[]{:S(2)}) collective-permute-start(bf16[32,1152]{1,0:T(8,128)(2,1)S(1)} %queries.1.refs_0_), channel_id=1, source_target_pairs={{0,3},{1,2},{2,1},{3,0},{4,7},{5,6},{6,5},{7,4},{8,11},{9,10},{10,... | collective-permute-start | bytes 221192 | tf_op jit(solution)/shard_map/ppermute | solution.py:19
  18.9 1.1 %collective-permute-done.2.refs_1_ = bf16[32,1152]{1,0:T(8,128)(2,1)S(1)} collective-permute-done((bf16[32,1152]{1,0:T(8,128)(2,1)S(1)}, bf16[32,1152]{1,0:T(8,128)(2,1)S(1)}, u32[]{:S(2)}, u32[]{:S(2)}) %collective-permute-start.2) | collective-permute-done | bytes 73760 | tf_op jit(solution)/shard_map/ppermute | solution.py:19
  20.0 1.6 %collective-permute-start.6 = (bf16[32,1152]{1,0:T(8,128)(2,1)S(1)}, bf16[32,1152]{1,0:T(8,128)(2,1)S(1)}, u32[]{:S(2)}, u32[]{:S(2)}) collective-permute-start(bf16[32,1152]{1,0:T(8,128)(2,1)S(1)} %collective-permute-done.2.refs_1_), channel_id=1, source_target_pairs={{0,3},{1,2},{2,1},{3,0},{4,7},{5,6},{6,5},{7,4},{8,11},{9,10},{10,... | collective-permute-start | bytes 221192 | tf_op jit(solution)/shard_map/ppermute | solution.py:19
  21.6 0.4 %collective-permute-done.5.refs_0_ = bf16[32,1152]{1,0:T(8,128)(2,1)S(1)} collective-permute-done((bf16[32,1152]{1,0:T(8,128)(2,1)S(1)}, bf16[32,1152]{1,0:T(8,128)(2,1)S(1)}, u32[]{:S(2)}, u32[]{:S(2)}) %collective-permute-start.5) | collective-permute-done | bytes 73760 | tf_op jit(solution)/shard_map/ppermute | solution.py:19
  22.0 2.0 %collective-permute-done.6.refs_1_ = bf16[32,1152]{1,0:T(8,128)(2,1)S(1)} collective-permute-done((bf16[32,1152]{1,0:T(8,128)(2,1)S(1)}, bf16[32,1152]{1,0:T(8,128)(2,1)S(1)}, u32[]{:S(2)}, u32[]{:S(2)}) %collective-permute-start.6) | collective-permute-done | bytes 73760 | tf_op jit(solution)/shard_map/ppermute | solution.py:19
  24.0 0.0 collective-permute-done.3.refs_4_
  24.0 0.0 collective-permute-done.4.refs_5_
  24.0 2.0 %shard_map.65 = (s16[32,1152]{1,0:T(8,128)(2,1)S(1)}, s16[16,1152]{1,0:T(8,128)(2,1)S(1)}, s16[16,1152]{1,0:T(8,128)(2,1)S(1)}) custom-call(bf16[32,1152]{1,0:T(8,128)(2,1)S(1)} %collective-permute-done.5.refs_0_, bf16[32,1152]{1,0:T(8,128)(2,1)S(1)} %collective-permute-done.6.refs_1_, bf16[512,1024]{1,0:T(8,128)(2,1)S(1)} %get-tuple-element.22.refs_2_, ...), custom_call_target="tpu_custom_call" | custom-call | tf_op jit(solution)/shard_map/pallas_call | solution.py:261
  26.0 1.6 %collective-permute-start.10 = (s16[16,1152]{1,0:T(8,128)(2,1)S(1)}, s16[16,1152]{1,0:T(8,128)(2,1)S(1)}, u32[]{:S(2)}, u32[]{:S(2)}) collective-permute-start(s16[16,1152]{1,0:T(8,128)(2,1)S(1)} %get-tuple-element.28), channel_id=1, source_target_pairs={{0,3},{1,2},{2,1},{3,0},{4,7},{5,6},{6,5},{7,4},{8,11},{9,10},{10,... | collective-permute-start | bytes 110600 | tf_op jit(solution)/shard_map/ppermute | solution.py:19
  27.6 0.2 collective-permute-start.7
  27.8 1.5 %collective-permute-start.8 = (s16[16,1152]{1,0:T(8,128)(2,1)S(1)}, s16[16,1152]{1,0:T(8,128)(2,1)S(1)}, u32[]{:S(2)}, u32[]{:S(2)}) collective-permute-start(s16[16,1152]{1,0:T(8,128)(2,1)S(1)} %get-tuple-element.27), channel_id=1, source_target_pairs={{0,3},{1,2},{2,1},{3,0},{4,7},{5,6},{6,5},{7,4},{8,11},{9,10},{10,... | collective-permute-start | bytes 110600 | tf_op jit(solution)/shard_map/ppermute | solution.py:19
  29.3 1.9 %shard_map.64 = (f32[32,1024]{1,0:T(8,128)S(1)}, f32[32,1024]{1,0:T(8,128)S(1)}) custom-call(bf16[32,1152]{1,0:T(8,128)(2,1)S(1)} %queries.1.refs_0_, bf16[32,1152]{1,0:T(8,128)(2,1)S(1)} %collective-permute-done.2.refs_1_, bf16[512,1024]{1,0:T(8,128)(2,1)S(1)} %get-tuple-element.22.refs_2_, bf16[512,1024]{1,0:T(8,128)(2,1)S(1)} %get-tuple-element.23.refs_3_, ...), custom_call_target="tpu_custom_call" | custom-call | tf_op jit(solution)/shard_map/pallas_call | solution.py:261
  31.2 0.0 collective-permute-done.10.refs_1_
  31.2 0.2 emit.4
  31.4 1.2 %collective-permute-start.11 = (s16[16,1152]{1,0:T(8,128)(2,1)S(1)}, s16[16,1152]{1,0:T(8,128)(2,1)S(1)}, u32[]{:S(2)}, u32[]{:S(2)}) collective-permute-start(s16[16,1152]{1,0:T(8,128)(2,1)S(1)} %emit.4), channel_id=1, source_target_pairs={{0,5},{1,4},{2,7},{3,6},{4,1},{5,0},{6,3},{7,2},{8,13},{9,12},{10,... | collective-permute-start | bytes 110600 | tf_op jit(solution)/shard_map/ppermute | solution.py:19
  32.6 0.1 collective-permute-done.8.refs_1_
  32.7 0.2 emit.3
  32.9 1.7 %collective-permute-start.9 = (s16[16,1152]{1,0:T(8,128)(2,1)S(1)}, s16[16,1152]{1,0:T(8,128)(2,1)S(1)}, u32[]{:S(2)}, u32[]{:S(2)}) collective-permute-start(s16[16,1152]{1,0:T(8,128)(2,1)S(1)} %emit.3), channel_id=1, source_target_pairs={{0,5},{1,4},{2,7},{3,6},{4,1},{5,0},{6,3},{7,2},{8,13},{9,12},{10,... | collective-permute-start | bytes 110600 | tf_op jit(solution)/shard_map/ppermute | solution.py:19
  34.5 0.5 %collective-permute-done.11.refs_2_ = s16[16,1152]{1,0:T(8,128)(2,1)S(1)} collective-permute-done((s16[16,1152]{1,0:T(8,128)(2,1)S(1)}, s16[16,1152]{1,0:T(8,128)(2,1)S(1)}, u32[]{:S(2)}, u32[]{:S(2)}) %collective-permute-start.11) | collective-permute-done | bytes 36896 | tf_op jit(solution)/shard_map/ppermute | solution.py:19
  35.0 0.0 collective-permute-done.7.refs_1_
  35.0 0.2 emit.5
  35.2 1.6 %collective-permute-start.12 = (s16[16,1152]{1,0:T(8,128)(2,1)S(1)}, s16[16,1152]{1,0:T(8,128)(2,1)S(1)}, u32[]{:S(2)}, u32[]{:S(2)}) collective-permute-start(s16[16,1152]{1,0:T(8,128)(2,1)S(1)} %emit.5), channel_id=1, source_target_pairs={{0,9},{1,8},{2,11},{3,10},{4,13},{5,12},{6,15},{7,14},{8,1},{9,0},... | collective-permute-start | bytes 110600 | tf_op jit(solution)/shard_map/ppermute | solution.py:19
  36.8 0.0 copy-start.1
  36.8 0.4 own.1
  37.2 0.0 collective-permute-done.9.refs_2_
  37.2 2.4 %collective-permute-done.12.refs_3_ = s16[16,1152]{1,0:T(8,128)(2,1)S(1)} collective-permute-done((s16[16,1152]{1,0:T(8,128)(2,1)S(1)}, s16[16,1152]{1,0:T(8,128)(2,1)S(1)}, u32[]{:S(2)}, u32[]{:S(2)}) %collective-permute-start.12) | collective-permute-done | bytes 36896 | tf_op jit(solution)/shard_map/ppermute | solution.py:19
  39.6 0.0 copy-done.1
  39.6 1.2 %finish.1 = bf16[16,1024]{1,0:T(8,128)(2,1)} custom-call(bf16[16,1024]{1,0:T(8,128)(2,1)S(1)} %copy-done.3, f32[16,1024]{1,0:T(8,128)S(1)} %get-tuple-element.20.term_ref, bf16[16,1024]{1,0:T(8,128)(2,1)S(1)} %get-tuple-element.21.gate_ref, bf16[1024,1024]{1,0:T(8,128)(2,1)S(1)} %copy-done.1, f32[32,1024]{1,0:T(8,128)S(1)} %get-tuple-element.24.refs_0_, ...), custom_call_target="tpu_custom_call" | custom-call | tf_op jit(solution)/shard_map/finish/pallas_call | solution.py:370
  (1 shorter events, 0.0 us)
Async XLA Ops:
  0.0 0.8 %copy-start.3 = (bf16[16,1024]{1,0:T(8,128)(2,1)S(1)}, bf16[16,1024]{1,0:T(8,128)(2,1)}, u32[]{:S(2)}) copy-start(bf16[16,1024]{1,0:T(8,128)(2,1)} %cand_ref.5) | copy-start | bytes 98308
  0.0 1.2 %copy-start.2 = (bf16[512,1024]{1,0:T(8,128)(2,1)S(1)}, bf16[512,1024]{1,0:T(8,128)(2,1)}, u32[]{:S(2)}) copy-start(bf16[512,1024]{1,0:T(8,128)(2,1)} %hist_ref.1) | copy-start | bytes 3145732
  0.0 3.7 %copy-start = (bf16[1024,4096]{1,0:T(8,128)(2,1)S(1)}, bf16[1024,4096]{1,0:T(8,128)(2,1)}, u32[]{:S(2)}) copy-start(bf16[1024,4096]{1,0:T(8,128)(2,1)} %refs_2_.1) | copy-start | bytes 25165828
  5.6 18.3 %collective-permute-start.3 = (bf16[512,1024]{1,0:T(8,128)(2,1)S(1)}, bf16[512,1024]{1,0:T(8,128)(2,1)S(1)}, u32[]{:S(2)}, u32[]{:S(2)}) collective-permute-start(bf16[512,1024]{1,0:T(8,128)(2,1)S(1)} %get-tuple-element.22.refs_2_), channel_id=1, source_target_pairs={{0,1},{1,0},{2,3},{3,2},{4,5},{5,4},{6,7},{7,6},{8,9},{9,8},{10,11... | collective-permute-start | bytes 3145736 | tf_op jit(solution)/shard_map/ppermute | solution.py:19
  6.2 5.3 %copy-start.4 = (s32[16]{0:T(128)S(1)}, s32[16]{0:T(128)}, u32[]{:S(2)}) copy-start(s32[16]{0:T(128)} %param.9) | copy-start | bytes 196
  7.6 16.3 %collective-permute-start.4 = (bf16[512,1024]{1,0:T(8,128)(2,1)S(1)}, bf16[512,1024]{1,0:T(8,128)(2,1)S(1)}, u32[]{:S(2)}, u32[]{:S(2)}) collective-permute-start(bf16[512,1024]{1,0:T(8,128)(2,1)S(1)} %get-tuple-element.23.refs_3_), channel_id=1, source_target_pairs={{0,1},{1,0},{2,3},{3,2},{4,5},{5,4},{6,7},{7,6},{8,9},{9,8},{10,11... | collective-permute-start | bytes 3145736 | tf_op jit(solution)/shard_map/ppermute | solution.py:19
  7.7 7.6 %collective-permute-start = (bf16[16,1024]{1,0:T(8,128)(2,1)S(1)}, bf16[16,1024]{1,0:T(8,128)(2,1)S(1)}, u32[]{:S(2)}, u32[]{:S(2)}) collective-permute-start(bf16[16,1024]{1,0:T(8,128)(2,1)S(1)} %copy-done.3), channel_id=1, source_target_pairs={{0,9},{1,8},{2,11},{3,10},{4,13},{5,12},{6,15},{7,14},{8,1},{9,0},... | collective-permute-start | bytes 98312 | tf_op jit(solution)/shard_map/ppermute | solution.py:19
  11.4 3.9 %collective-permute-start.1 = (s32[16]{0:T(128)S(1)}, s32[16]{0:T(128)S(1)}, u32[]{:S(2)}, u32[]{:S(2)}) collective-permute-start(s32[16]{0:T(128)S(1)} %copy-done.4), channel_id=1, source_target_pairs={{0,9},{1,8},{2,11},{3,10},{4,13},{5,12},{6,15},{7,14},{8,1},{9,0},... | collective-permute-start | bytes 200 | tf_op jit(solution)/shard_map/ppermute | solution.py:19
  16.0 4.0 %collective-permute-start.2 = (bf16[32,1152]{1,0:T(8,128)(2,1)S(1)}, bf16[32,1152]{1,0:T(8,128)(2,1)S(1)}, u32[]{:S(2)}, u32[]{:S(2)}) collective-permute-start(bf16[32,1152]{1,0:T(8,128)(2,1)S(1)} %queries.1.refs_0_), channel_id=1, source_target_pairs={{0,5},{1,4},{2,7},{3,6},{4,1},{5,0},{6,3},{7,2},{8,13},{9,12},{10,... | collective-permute-start | bytes 221192 | tf_op jit(solution)/shard_map/ppermute | solution.py:19
  17.7 4.3 %collective-permute-start.5 = (bf16[32,1152]{1,0:T(8,128)(2,1)S(1)}, bf16[32,1152]{1,0:T(8,128)(2,1)S(1)}, u32[]{:S(2)}, u32[]{:S(2)}) collective-permute-start(bf16[32,1152]{1,0:T(8,128)(2,1)S(1)} %queries.1.refs_0_), channel_id=1, source_target_pairs={{0,3},{1,2},{2,1},{3,0},{4,7},{5,6},{6,5},{7,4},{8,11},{9,10},{10,... | collective-permute-start | bytes 221192 | tf_op jit(solution)/shard_map/ppermute | solution.py:19
  20.0 4.0 %collective-permute-start.6 = (bf16[32,1152]{1,0:T(8,128)(2,1)S(1)}, bf16[32,1152]{1,0:T(8,128)(2,1)S(1)}, u32[]{:S(2)}, u32[]{:S(2)}) collective-permute-start(bf16[32,1152]{1,0:T(8,128)(2,1)S(1)} %collective-permute-done.2.refs_1_), channel_id=1, source_target_pairs={{0,3},{1,2},{2,1},{3,0},{4,7},{5,6},{6,5},{7,4},{8,11},{9,10},{10,... | collective-permute-start | bytes 221192 | tf_op jit(solution)/shard_map/ppermute | solution.py:19
  26.0 5.3 %collective-permute-start.10 = (s16[16,1152]{1,0:T(8,128)(2,1)S(1)}, s16[16,1152]{1,0:T(8,128)(2,1)S(1)}, u32[]{:S(2)}, u32[]{:S(2)}) collective-permute-start(s16[16,1152]{1,0:T(8,128)(2,1)S(1)} %get-tuple-element.28), channel_id=1, source_target_pairs={{0,3},{1,2},{2,1},{3,0},{4,7},{5,6},{6,5},{7,4},{8,11},{9,10},{10,... | collective-permute-start | bytes 110600 | tf_op jit(solution)/shard_map/ppermute | solution.py:19
  27.6 7.4 %collective-permute-start.7 = (s16[32,1152]{1,0:T(8,128)(2,1)S(1)}, s16[32,1152]{1,0:T(8,128)(2,1)S(1)}, u32[]{:S(2)}, u32[]{:S(2)}) collective-permute-start(s16[32,1152]{1,0:T(8,128)(2,1)S(1)} %get-tuple-element.25), channel_id=1, source_target_pairs={{0,3},{1,2},{2,1},{3,0},{4,7},{5,6},{6,5},{7,4},{8,11},{9,10},{10,... | collective-permute-start | bytes 221192 | tf_op jit(solution)/shard_map/ppermute | solution.py:19
  27.8 4.9 %collective-permute-start.8 = (s16[16,1152]{1,0:T(8,128)(2,1)S(1)}, s16[16,1152]{1,0:T(8,128)(2,1)S(1)}, u32[]{:S(2)}, u32[]{:S(2)}) collective-permute-start(s16[16,1152]{1,0:T(8,128)(2,1)S(1)} %get-tuple-element.27), channel_id=1, source_target_pairs={{0,3},{1,2},{2,1},{3,0},{4,7},{5,6},{6,5},{7,4},{8,11},{9,10},{10,... | collective-permute-start | bytes 110600 | tf_op jit(solution)/shard_map/ppermute | solution.py:19
  31.4 3.6 %collective-permute-start.11 = (s16[16,1152]{1,0:T(8,128)(2,1)S(1)}, s16[16,1152]{1,0:T(8,128)(2,1)S(1)}, u32[]{:S(2)}, u32[]{:S(2)}) collective-permute-start(s16[16,1152]{1,0:T(8,128)(2,1)S(1)} %emit.4), channel_id=1, source_target_pairs={{0,5},{1,4},{2,7},{3,6},{4,1},{5,0},{6,3},{7,2},{8,13},{9,12},{10,... | collective-permute-start | bytes 110600 | tf_op jit(solution)/shard_map/ppermute | solution.py:19
  32.9 4.3 %collective-permute-start.9 = (s16[16,1152]{1,0:T(8,128)(2,1)S(1)}, s16[16,1152]{1,0:T(8,128)(2,1)S(1)}, u32[]{:S(2)}, u32[]{:S(2)}) collective-permute-start(s16[16,1152]{1,0:T(8,128)(2,1)S(1)} %emit.3), channel_id=1, source_target_pairs={{0,5},{1,4},{2,7},{3,6},{4,1},{5,0},{6,3},{7,2},{8,13},{9,12},{10,... | collective-permute-start | bytes 110600 | tf_op jit(solution)/shard_map/ppermute | solution.py:19
  35.2 4.4 %collective-permute-start.12 = (s16[16,1152]{1,0:T(8,128)(2,1)S(1)}, s16[16,1152]{1,0:T(8,128)(2,1)S(1)}, u32[]{:S(2)}, u32[]{:S(2)}) collective-permute-start(s16[16,1152]{1,0:T(8,128)(2,1)S(1)} %emit.5), channel_id=1, source_target_pairs={{0,9},{1,8},{2,11},{3,10},{4,13},{5,12},{6,15},{7,14},{8,1},{9,0},... | collective-permute-start | bytes 110600 | tf_op jit(solution)/shard_map/ppermute | solution.py:19
  36.8 2.9 %copy-start.1 = (bf16[1024,1024]{1,0:T(8,128)(2,1)S(1)}, bf16[1024,1024]{1,0:T(8,128)(2,1)}, u32[]{:S(2)}) copy-start(bf16[1024,1024]{1,0:T(8,128)(2,1)} %w_ref.7) | copy-start | bytes 6291460

commit v5 on v4

--- a/solution.py
+++ b/solution.py
@@ -50,8 +50,16 @@
     return code[:, :width] * (jnp.exp2(code[:, width : width + 1]) * (1 / STEPS))
 
 
+def stay(array):
+    return pltpu.with_memory_space_constraint(array, pltpu.HBM)
+
+
 def near_by(*arrays):
     return [pltpu.with_memory_space_constraint(array, pltpu.VMEM) for array in arrays]
+
+
+def hbm():
+    return pl.BlockSpec(memory_space=pltpu.HBM)
 
 
 def limits_of(packed, width):
@@ -60,35 +68,47 @@
     return high * 256 + low
 
 
-def spark():
-    def body(out_ref):
-        out_ref[...] = jnp.zeros_like(out_ref)
-
-    return pl.pallas_call(
-        body,
-        out_shape=jax.ShapeDtypeStruct((8, 128), jnp.float32),
-        out_specs=whole(),
-        compiler_params=PARAMS,
-        cost_estimate=pl.CostEstimate(flops=6 * 10**9, bytes_accessed=2 * 10**7, transcendentals=0),
-        name="spark",
-    )()
-
-
 def normed(rows):
     return norm(rows.astype(jnp.float32)).astype(jnp.bfloat16)
 
 
-def limit_columns(visible, length):
-    rows = visible.shape[1]
-    diagonal = lax.broadcasted_iota(jnp.int32, (rows, rows), 0) == lax.broadcasted_iota(
-        jnp.int32, (rows, rows), 1
-    )
-    limit = jnp.minimum(jnp.broadcast_to(visible, (rows, rows)), length).astype(jnp.float32)
-    limit = jnp.sum(jnp.where(diagonal, limit, 0.0), axis=1, keepdims=True)
-    high = jnp.floor(limit * (1 / 256))
-    low = limit - high * 256
-    lane = lax.broadcasted_iota(jnp.int32, (rows, EXTRA), 1)
-    return jnp.where(lane == 0, high, low).astype(jnp.bfloat16)
+def in_halves(numbers):
+    high = jnp.floor(numbers * (1 / 256))
+    lane = lax.broadcasted_iota(jnp.int32, (numbers.shape[0], EXTRA), 1)
+    return jnp.where(lane == 0, high, numbers - high * 256).astype(jnp.bfloat16)
+
+
+def begin(candidates, visible):
+    rows, width = candidates.shape
+
+    def body(cand_ref, visible_ref, out_ref, offsets, sems):
+        loads = [
+            pltpu.make_async_copy(visible_ref, offsets, sems.at[0]),
+            pltpu.make_async_copy(cand_ref, out_ref.at[:, pl.ds(0, width)], sems.at[1]),
+        ]
+        for load in loads:
+            load.start()
+        loads[0].wait()
+        diagonal = lax.broadcasted_iota(jnp.int32, (rows, rows), 0) == lax.broadcasted_iota(
+            jnp.int32, (rows, rows), 1
+        )
+        across = jnp.broadcast_to(offsets[...], (rows, rows)).astype(jnp.float32)
+        down = jnp.sum(jnp.where(diagonal, across, 0.0), axis=1, keepdims=True)
+        out_ref[:, width:] = in_halves(down)
+        loads[1].wait()
+
+    return pl.pallas_call(
+        body,
+        out_shape=jax.ShapeDtypeStruct((rows, width + EXTRA), jnp.bfloat16),
+        in_specs=[hbm()] * 2,
+        out_specs=whole(),
+        scratch_shapes=[pltpu.VMEM((1, rows), jnp.int32), pltpu.SemaphoreType.DMA((2,))],
+        compiler_params=PARAMS,
+        cost_estimate=pl.CostEstimate(
+            flops=6 * width**3, bytes_accessed=20 * width**2, transcendentals=0
+        ),
+        name="begin",
+    )(stay(candidates), stay(visible.reshape(1, rows)))
 
 
 def project(rows_ref, w_ref, first, tile, n_keys, out_ref, self_ref):
@@ -105,13 +125,13 @@
         self_ref[:, at : at + tile] = made[n_keys:]
 
 
-def project_keys(history, candidates, w_proj, first_op):
+def project_keys(history, packed, w_proj):
     n_keys, width = history.shape
-    rows = candidates.shape[0]
+    rows = packed.shape[0]
     tile = min(256, width)
 
-    def body(hist_ref, cand_ref, w_ref, first_ref, key_ref, self_ref, rows_ref):
-        rows_ref[n_keys:] = normed(cand_ref[...])
+    def body(hist_ref, packed_ref, w_ref, key_ref, self_ref, rows_ref):
+        rows_ref[n_keys:] = normed(packed_ref[:, :width])
         rows_ref[:n_keys] = normed(hist_ref[...])
         project(rows_ref, w_ref, 2 * width, tile, n_keys, key_ref, self_ref)
 
@@ -122,11 +142,11 @@
             jax.ShapeDtypeStruct((rows, width), jnp.bfloat16),
             jax.ShapeDtypeStruct((n_keys + rows, width), jnp.bfloat16),
         ),
-        in_specs=[whole()] * 4,
+        in_specs=[whole()] * 3,
         out_specs=[whole()] * 3,
         compiler_params=PARAMS,
         name="keys",
-    )(*near_by(history, candidates, w_proj, first_op))
+    )(*near_by(history, packed, w_proj))
 
 
 def project_values(rows_both, w_proj, rows):
@@ -150,14 +170,19 @@
     )(*near_by(rows_both, w_proj))
 
 
-def project_queries(candidates, got, visible, got_visible, hist_length, w_proj):
-    rows, width = candidates.shape
+def project_queries(packed, got, hist_length, w_proj):
+    rows = packed.shape[0]
+    width = w_proj.shape[0]
     tile = min(256, width)
 
-    def body(length_ref, cand_ref, got_ref, visible_ref, got_visible_ref, w_ref, out_ref):
-        out_ref[:rows, width:] = limit_columns(visible_ref[...], length_ref[0])
-        out_ref[rows:, width:] = limit_columns(got_visible_ref[...], length_ref[0])
-        both = jnp.concatenate([normed(cand_ref[...]), normed(got_ref[...])], axis=0)
+    def body(length_ref, packed_ref, got_ref, w_ref, out_ref):
+        length = length_ref[0].astype(jnp.float32)
+        for first, ref in ((0, packed_ref), (rows, got_ref)):
+            limit = jnp.minimum(limits_of(ref[...], width), length)
+            out_ref[first : first + rows, width:] = in_halves(limit)
+        both = jnp.concatenate(
+            [normed(packed_ref[:, :width]), normed(got_ref[:, :width])], axis=0
+        )
         for at in range(0, width, tile):
             out_ref[:, at : at + tile] = silu(
                 jnp.dot(
@@ -170,14 +195,11 @@
     return pl.pallas_call(
         body,
         out_shape=jax.ShapeDtypeStruct((2 * rows, width + EXTRA), jnp.bfloat16),
-        in_specs=[pl.BlockSpec(memory_space=pltpu.SMEM)] + [whole()] * 5,
+        in_specs=[pl.BlockSpec(memory_space=pltpu.SMEM)] + [whole()] * 3,
         out_specs=whole(),
         compiler_params=PARAMS,
         name="queries",
-    )(
-        hist_length,
-        *near_by(candidates, got, visible.reshape(1, rows), got_visible.reshape(1, rows), w_proj),
-    )
+    )(hist_length, *near_by(packed, got, w_proj))
 
 
 def join(first, second):
@@ -386,14 +408,13 @@
         masks.append(bit | 1)
         bit //= 2
     rows = candidates.shape[0]
-    first_op = spark()
-    keys, self_key, rows_both = project_keys(history, candidates, w_proj, first_op)
+    packed = begin(candidates, visible)
+    keys, self_key, rows_both = project_keys(history, packed, w_proj)
     values, self_value = project_values(rows_both, w_proj, rows)
     other_keys = swapped(keys, "hist", 1)
     other_values = swapped(values, "hist", 1)
-    got = swapped(candidates, "hist", masks[0])
-    got_visible = swapped(visible, "hist", masks[0])
-    inner = project_queries(candidates, got, visible, got_visible, hist_length, w_proj)
+    got = swapped(packed, "hist", masks[0])
+    inner = project_queries(packed, got, hist_length, w_proj)
     for mask in masks[1:-2]:
         got = swapped(inner, "hist", mask)
         inner = join(inner, got)

time: 41 us -> 39.8 us (0.971)
  waiting for transfers between devices: 9.73 us -> 6.24 us
  starting transfers between devices: 16.7 us -> 19 us
  local copies, waits for them, and re-layouts: 3.74 us -> 2.7 us
  Pallas kernels: 10 us -> 10.9 us
    ppermute x13 -> x12, waiting for transfers between devices: 9.73 us -> 6.24 us  [swapped(): return lax.ppermute(shard, axis, [(i, i ^ mask) for i in range(size)])]
    ppermute x13 -> x12, starting transfers between devices: 16.7 us -> 19 us  [swapped(): return lax.ppermute(shard, axis, [(i, i ^ mask) for i in range(size)])]
    unnamed x10 -> x8, local copies, waits for them, and re-layouts: 3.74 us -> 2.7 us
    pallas_call x1, Pallas kernels: 0.01 us -> 0.94 us  [begin(): pl.pallas_call(body, out_shape=jax.ShapeDtypeStruct((rows, width + EXTRA)...]
  transfers between devices with their start and end apart: 13 -> 12, of which waited for: 7 -> 5; matrix products, arithmetic and copies ran while one was open for 0% -> 0% of each run, Pallas kernels for 12% -> 12%
where the time goes in v5:
time: 39.8 us; the launch traced here: 39.6 us
  starting transfers between devices  19 us (48%)
  Pallas kernels  10.9 us (27%)
  waiting for transfers between devices  6.24 us (16%)
  local copies, waits for them, and re-layouts  2.7 us (7%)
  between operations  0.76 us (2%)
    ppermute x12, starting transfers between devices, swapped(): return lax.ppermute(shard, axis, [(i, i ^ mask) for i in range(size)])  19 us
    ppermute x12, waiting for transfers between devices, swapped(): return lax.ppermute(shard, axis, [(i, i ^ mask) for i in range(size)])  6.24 us
    pallas_call x2, Pallas kernels, attend(): pl.pallas_call(body, out_shape=[jax.ShapeDtypeStruct((piece, width + EXTR...  3.87 us
    unnamed x8, local copies, waits for them, and re-layouts  2.7 us
    pallas_call x1, Pallas kernels, project_keys(): pl.pallas_call(body, out_shape=(jax.ShapeDtypeStruct((n_keys, width), jnp...  1.87 us
    pallas_call x1, Pallas kernels, project_values(): pl.pallas_call(body, out_shape=(jax.ShapeDtypeStruct((n_keys, width), jnp...  1.42 us
    pallas_call x1, Pallas kernels, finish(): pl.pallas_call(body, out_shape=jax.ShapeDtypeStruct(candidates.shape, jnp...  1.25 us
    pallas_call x1, Pallas kernels, begin(): pl.pallas_call(body, out_shape=jax.ShapeDtypeStruct((rows, width + EXTRA)...  0.94 us
  transfers between devices with their start and end apart: 12, of which 5 were waited for; matrix products, arithmetic and copies ran while one was open for 0% of the time, Pallas kernels for 12%

profile of v5, /device:TPU:0, one launch (start us, length us, event | category | flops | bytes accessed | tf_op | source)
XLA Modules:
  0.0 39.6 jit_solution(16763649270624595757)
XLA Ops:
  0.0 0.0 copy-start
  0.0 0.0 copy-start.2
  0.0 0.9 %begin.1.packed_ref = bf16[16,1152]{1,0:T(8,128)(2,1)S(1)} custom-call(bf16[16,1024]{1,0:T(8,128)(2,1)} %cand_ref.3, s32[1,16]{1,0:T(1,128)} %bitcast.1), custom_call_target="tpu_custom_call" | custom-call | flops 6442450944 | bytes 20971520 | tf_op jit(solution)/shard_map/begin/pallas_call | solution.py:100
  1.0 2.5 %copy-done = bf16[1024,4096]{1,0:T(8,128)(2,1)S(1)} copy-done((bf16[1024,4096]{1,0:T(8,128)(2,1)S(1)}, bf16[1024,4096]{1,0:T(8,128)(2,1)}, u32[]{:S(2)}) %copy-start) | copy-done | bytes 8388632
  3.4 0.2 copy-done.2
  3.6 1.9 %keys.1 = (bf16[512,1024]{1,0:T(8,128)(2,1)S(1)}, bf16[16,1024]{1,0:T(8,128)(2,1)S(1)}, bf16[528,1024]{1,0:T(8,128)(2,1)S(1)}) custom-call(bf16[512,1024]{1,0:T(8,128)(2,1)S(1)} %copy-done.2, bf16[16,1152]{1,0:T(8,128)(2,1)S(1)} %begin.1.packed_ref, bf16[1024,4096]{1,0:T(8,128)(2,1)S(1)} %copy-done), custom_call_target="tpu_custom_call" | custom-call | tf_op jit(solution)/shard_map/keys/pallas_call | solution.py:138
  5.5 0.6 %collective-permute-start.2 = (bf16[512,1024]{1,0:T(8,128)(2,1)S(1)}, bf16[512,1024]{1,0:T(8,128)(2,1)S(1)}, u32[]{:S(2)}, u32[]{:S(2)}) collective-permute-start(bf16[512,1024]{1,0:T(8,128)(2,1)S(1)} %get-tuple-element.22.refs_2_), channel_id=1, source_target_pairs={{0,1},{1,0},{2,3},{3,2},{4,5},{5,4},{6,7},{7,6},{8,9},{9,8},{10,11... | collective-permute-start | bytes 3145736 | tf_op jit(solution)/shard_map/ppermute | solution.py:19
  6.1 1.4 %values.1 = (bf16[512,1024]{1,0:T(8,128)(2,1)S(1)}, bf16[16,1024]{1,0:T(8,128)(2,1)S(1)}) custom-call(bf16[528,1024]{1,0:T(8,128)(2,1)S(1)} %get-tuple-element.17.rows_ref.refs_1_, bf16[1024,4096]{1,0:T(8,128)(2,1)S(1)} %copy-done), custom_call_target="tpu_custom_call" | custom-call | tf_op jit(solution)/shard_map/values/pallas_call | solution.py:160
  7.5 0.1 collective-permute-start.3
  7.6 3.7 %collective-permute-start = (bf16[16,1152]{1,0:T(8,128)(2,1)S(1)}, bf16[16,1152]{1,0:T(8,128)(2,1)S(1)}, u32[]{:S(2)}, u32[]{:S(2)}) collective-permute-start(bf16[16,1152]{1,0:T(8,128)(2,1)S(1)} %begin.1.packed_ref), channel_id=1, source_target_pairs={{0,9},{1,8},{2,11},{3,10},{4,13},{5,12},{6,15},{7,14},{8,1},{9,0},... | collective-permute-start | bytes 110600 | tf_op jit(solution)/shard_map/ppermute | solution.py:19
  12.0 1.0 %collective-permute-done.got_ref = bf16[16,1152]{1,0:T(8,128)(2,1)S(1)} collective-permute-done((bf16[16,1152]{1,0:T(8,128)(2,1)S(1)}, bf16[16,1152]{1,0:T(8,128)(2,1)S(1)}, u32[]{:S(2)}, u32[]{:S(2)}) %collective-permute-start) | collective-permute-done | bytes 36896 | tf_op jit(solution)/shard_map/ppermute | solution.py:19
  13.0 0.6 %queries.1.refs_0_ = bf16[32,1152]{1,0:T(8,128)(2,1)S(1)} custom-call(s32[1]{0:T(128)S(6)} %copy.7.length_ref, bf16[16,1152]{1,0:T(8,128)(2,1)S(1)} %begin.1.packed_ref, bf16[16,1152]{1,0:T(8,128)(2,1)S(1)} %collective-permute-done.got_ref, bf16[1024,4096]{1,0:T(8,128)(2,1)S(1)} %copy-done), custom_call_target="tpu_custom_call" | custom-call | tf_op jit(solution)/shard_map/queries/pallas_call | solution.py:195
  13.6 1.9 %collective-permute-start.1 = (bf16[32,1152]{1,0:T(8,128)(2,1)S(1)}, bf16[32,1152]{1,0:T(8,128)(2,1)S(1)}, u32[]{:S(2)}, u32[]{:S(2)}) collective-permute-start(bf16[32,1152]{1,0:T(8,128)(2,1)S(1)} %queries.1.refs_0_), channel_id=1, source_target_pairs={{0,5},{1,4},{2,7},{3,6},{4,1},{5,0},{6,3},{7,2},{8,13},{9,12},{10,... | collective-permute-start | bytes 221192 | tf_op jit(solution)/shard_map/ppermute | solution.py:19
  15.5 1.7 %collective-permute-start.4 = (bf16[32,1152]{1,0:T(8,128)(2,1)S(1)}, bf16[32,1152]{1,0:T(8,128)(2,1)S(1)}, u32[]{:S(2)}, u32[]{:S(2)}) collective-permute-start(bf16[32,1152]{1,0:T(8,128)(2,1)S(1)} %queries.1.refs_0_), channel_id=1, source_target_pairs={{0,3},{1,2},{2,1},{3,0},{4,7},{5,6},{6,5},{7,4},{8,11},{9,10},{10,... | collective-permute-start | bytes 221192 | tf_op jit(solution)/shard_map/ppermute | solution.py:19
  17.2 0.8 %collective-permute-done.1.refs_1_ = bf16[32,1152]{1,0:T(8,128)(2,1)S(1)} collective-permute-done((bf16[32,1152]{1,0:T(8,128)(2,1)S(1)}, bf16[32,1152]{1,0:T(8,128)(2,1)S(1)}, u32[]{:S(2)}, u32[]{:S(2)}) %collective-permute-start.1) | collective-permute-done | bytes 73760 | tf_op jit(solution)/shard_map/ppermute | solution.py:19
  18.0 2.0 %collective-permute-start.5 = (bf16[32,1152]{1,0:T(8,128)(2,1)S(1)}, bf16[32,1152]{1,0:T(8,128)(2,1)S(1)}, u32[]{:S(2)}, u32[]{:S(2)}) collective-permute-start(bf16[32,1152]{1,0:T(8,128)(2,1)S(1)} %collective-permute-done.1.refs_1_), channel_id=1, source_target_pairs={{0,3},{1,2},{2,1},{3,0},{4,7},{5,6},{6,5},{7,4},{8,11},{9,10},{10,... | collective-permute-start | bytes 221192 | tf_op jit(solution)/shard_map/ppermute | solution.py:19
  20.0 0.0 collective-permute-done.4.refs_0_
  20.0 2.5 %collective-permute-done.5.refs_1_ = bf16[32,1152]{1,0:T(8,128)(2,1)S(1)} collective-permute-done((bf16[32,1152]{1,0:T(8,128)(2,1)S(1)}, bf16[32,1152]{1,0:T(8,128)(2,1)S(1)}, u32[]{:S(2)}, u32[]{:S(2)}) %collective-permute-start.5) | collective-permute-done | bytes 73760 | tf_op jit(solution)/shard_map/ppermute | solution.py:19
  22.6 0.0 collective-permute-done.2.refs_4_
  22.6 0.0 collective-permute-done.3.refs_5_
  22.6 2.0 %shard_map.65 = (s16[32,1152]{1,0:T(8,128)(2,1)S(1)}, s16[16,1152]{1,0:T(8,128)(2,1)S(1)}, s16[16,1152]{1,0:T(8,128)(2,1)S(1)}) custom-call(bf16[32,1152]{1,0:T(8,128)(2,1)S(1)} %collective-permute-done.4.refs_0_, bf16[32,1152]{1,0:T(8,128)(2,1)S(1)} %collective-permute-done.5.refs_1_, bf16[512,1024]{1,0:T(8,128)(2,1)S(1)} %get-tuple-element.22.refs_2_, ...), custom_call_target="tpu_custom_call" | custom-call | tf_op jit(solution)/shard_map/pallas_call | solution.py:283
  24.6 1.5 %collective-permute-start.9 = (s16[16,1152]{1,0:T(8,128)(2,1)S(1)}, s16[16,1152]{1,0:T(8,128)(2,1)S(1)}, u32[]{:S(2)}, u32[]{:S(2)}) collective-permute-start(s16[16,1152]{1,0:T(8,128)(2,1)S(1)} %get-tuple-element.28), channel_id=1, source_target_pairs={{0,3},{1,2},{2,1},{3,0},{4,7},{5,6},{6,5},{7,4},{8,11},{9,10},{10,... | collective-permute-start | bytes 110600 | tf_op jit(solution)/shard_map/ppermute | solution.py:19
  26.1 0.3 collective-permute-start.6
  26.4 1.4 %collective-permute-start.7 = (s16[16,1152]{1,0:T(8,128)(2,1)S(1)}, s16[16,1152]{1,0:T(8,128)(2,1)S(1)}, u32[]{:S(2)}, u32[]{:S(2)}) collective-permute-start(s16[16,1152]{1,0:T(8,128)(2,1)S(1)} %get-tuple-element.27), channel_id=1, source_target_pairs={{0,3},{1,2},{2,1},{3,0},{4,7},{5,6},{6,5},{7,4},{8,11},{9,10},{10,... | collective-permute-start | bytes 110600 | tf_op jit(solution)/shard_map/ppermute | solution.py:19
  27.8 1.9 %shard_map.64 = (f32[32,1024]{1,0:T(8,128)S(1)}, f32[32,1024]{1,0:T(8,128)S(1)}) custom-call(bf16[32,1152]{1,0:T(8,128)(2,1)S(1)} %queries.1.refs_0_, bf16[32,1152]{1,0:T(8,128)(2,1)S(1)} %collective-permute-done.1.refs_1_, bf16[512,1024]{1,0:T(8,128)(2,1)S(1)} %get-tuple-element.22.refs_2_, bf16[512,1024]{1,0:T(8,128)(2,1)S(1)} %get-tuple-element.23.refs_3_, ...), custom_call_target="tpu_custom_call" | custom-call | tf_op jit(solution)/shard_map/pallas_call | solution.py:283
  29.7 0.0 collective-permute-done.9.refs_1_
  29.7 0.2 emit.4
  29.9 2.0 %collective-permute-start.10 = (s16[16,1152]{1,0:T(8,128)(2,1)S(1)}, s16[16,1152]{1,0:T(8,128)(2,1)S(1)}, u32[]{:S(2)}, u32[]{:S(2)}) collective-permute-start(s16[16,1152]{1,0:T(8,128)(2,1)S(1)} %emit.4), channel_id=1, source_target_pairs={{0,5},{1,4},{2,7},{3,6},{4,1},{5,0},{6,3},{7,2},{8,13},{9,12},{10,... | collective-permute-start | bytes 110600 | tf_op jit(solution)/shard_map/ppermute | solution.py:19
  31.9 0.0 collective-permute-done.7.refs_1_
  31.9 0.2 emit.3
  32.0 0.9 %collective-permute-start.8 = (s16[16,1152]{1,0:T(8,128)(2,1)S(1)}, s16[16,1152]{1,0:T(8,128)(2,1)S(1)}, u32[]{:S(2)}, u32[]{:S(2)}) collective-permute-start(s16[16,1152]{1,0:T(8,128)(2,1)S(1)} %emit.3), channel_id=1, source_target_pairs={{0,5},{1,4},{2,7},{3,6},{4,1},{5,0},{6,3},{7,2},{8,13},{9,12},{10,... | collective-permute-start | bytes 110600 | tf_op jit(solution)/shard_map/ppermute | solution.py:19
  33.0 0.6 %collective-permute-done.10.refs_2_ = s16[16,1152]{1,0:T(8,128)(2,1)S(1)} collective-permute-done((s16[16,1152]{1,0:T(8,128)(2,1)S(1)}, s16[16,1152]{1,0:T(8,128)(2,1)S(1)}, u32[]{:S(2)}, u32[]{:S(2)}) %collective-permute-start.10) | collective-permute-done | bytes 36896 | tf_op jit(solution)/shard_map/ppermute | solution.py:19
  33.6 0.0 collective-permute-done.6.refs_1_
  33.6 0.2 emit.5
  33.8 2.9 %collective-permute-start.11 = (s16[16,1152]{1,0:T(8,128)(2,1)S(1)}, s16[16,1152]{1,0:T(8,128)(2,1)S(1)}, u32[]{:S(2)}, u32[]{:S(2)}) collective-permute-start(s16[16,1152]{1,0:T(8,128)(2,1)S(1)} %emit.5), channel_id=1, source_target_pairs={{0,9},{1,8},{2,11},{3,10},{4,13},{5,12},{6,15},{7,14},{8,1},{9,0},... | collective-permute-start | bytes 110600 | tf_op jit(solution)/shard_map/ppermute | solution.py:19
  36.7 0.0 copy-start.1
  36.7 0.0 copy-start.3
  36.7 0.4 %own.1 = (bf16[16,1024]{1,0:T(8,128)(2,1)S(1)}, f32[16,1024]{1,0:T(8,128)S(1)}) custom-call(bf16[32,1152]{1,0:T(8,128)(2,1)S(1)} %queries.1.refs_0_, bf16[528,1024]{1,0:T(8,128)(2,1)S(1)} %get-tuple-element.17.rows_ref.refs_1_, bf16[1024,4096]{1,0:T(8,128)(2,1)S(1)} %copy-done, bf16[16,1024]{1,0:T(8,128)(2,1)S(1)} %get-tuple-element.18.refs_3_, ...), custom_call_target="tpu_custom_call" | custom-call | tf_op jit(solution)/shard_map/own/pallas_call | solution.py:326
  37.1 0.0 collective-permute-done.8.refs_2_
  37.1 1.2 %collective-permute-done.11.refs_3_ = s16[16,1152]{1,0:T(8,128)(2,1)S(1)} collective-permute-done((s16[16,1152]{1,0:T(8,128)(2,1)S(1)}, s16[16,1152]{1,0:T(8,128)(2,1)S(1)}, u32[]{:S(2)}, u32[]{:S(2)}) %collective-permute-start.11) | collective-permute-done | bytes 36896 | tf_op jit(solution)/shard_map/ppermute | solution.py:19
  38.3 0.0 copy-done.1
  38.3 0.0 copy-done.3
  38.3 1.2 %finish.1 = bf16[16,1024]{1,0:T(8,128)(2,1)} custom-call(bf16[16,1024]{1,0:T(8,128)(2,1)S(1)} %copy-done.3, f32[16,1024]{1,0:T(8,128)S(1)} %get-tuple-element.20.term_ref, bf16[16,1024]{1,0:T(8,128)(2,1)S(1)} %get-tuple-element.21.gate_ref, bf16[1024,1024]{1,0:T(8,128)(2,1)S(1)} %copy-done.1, f32[32,1024]{1,0:T(8,128)S(1)} %get-tuple-element.24.refs_0_, ...), custom_call_target="tpu_custom_call" | custom-call | tf_op jit(solution)/shard_map/finish/pallas_call | solution.py:392
Async XLA Ops:
  0.0 3.4 %copy-start = (bf16[1024,4096]{1,0:T(8,128)(2,1)S(1)}, bf16[1024,4096]{1,0:T(8,128)(2,1)}, u32[]{:S(2)}) copy-start(bf16[1024,4096]{1,0:T(8,128)(2,1)} %refs_2_.1) | copy-start | bytes 25165828
  0.0 3.6 %copy-start.2 = (bf16[512,1024]{1,0:T(8,128)(2,1)S(1)}, bf16[512,1024]{1,0:T(8,128)(2,1)}, u32[]{:S(2)}) copy-start(bf16[512,1024]{1,0:T(8,128)(2,1)} %hist_ref.1) | copy-start | bytes 3145732
  5.5 17.0 %collective-permute-start.2 = (bf16[512,1024]{1,0:T(8,128)(2,1)S(1)}, bf16[512,1024]{1,0:T(8,128)(2,1)S(1)}, u32[]{:S(2)}, u32[]{:S(2)}) collective-permute-start(bf16[512,1024]{1,0:T(8,128)(2,1)S(1)} %get-tuple-element.22.refs_2_), channel_id=1, source_target_pairs={{0,1},{1,0},{2,3},{3,2},{4,5},{5,4},{6,7},{7,6},{8,9},{9,8},{10,11... | collective-permute-start | bytes 3145736 | tf_op jit(solution)/shard_map/ppermute | solution.py:19
  7.5 15.1 %collective-permute-start.3 = (bf16[512,1024]{1,0:T(8,128)(2,1)S(1)}, bf16[512,1024]{1,0:T(8,128)(2,1)S(1)}, u32[]{:S(2)}, u32[]{:S(2)}) collective-permute-start(bf16[512,1024]{1,0:T(8,128)(2,1)S(1)} %get-tuple-element.23.refs_3_), channel_id=1, source_target_pairs={{0,1},{1,0},{2,3},{3,2},{4,5},{5,4},{6,7},{7,6},{8,9},{9,8},{10,11... | collective-permute-start | bytes 3145736 | tf_op jit(solution)/shard_map/ppermute | solution.py:19
  7.6 5.4 %collective-permute-start = (bf16[16,1152]{1,0:T(8,128)(2,1)S(1)}, bf16[16,1152]{1,0:T(8,128)(2,1)S(1)}, u32[]{:S(2)}, u32[]{:S(2)}) collective-permute-start(bf16[16,1152]{1,0:T(8,128)(2,1)S(1)} %begin.1.packed_ref), channel_id=1, source_target_pairs={{0,9},{1,8},{2,11},{3,10},{4,13},{5,12},{6,15},{7,14},{8,1},{9,0},... | collective-permute-start | bytes 110600 | tf_op jit(solution)/shard_map/ppermute | solution.py:19
  13.6 4.4 %collective-permute-start.1 = (bf16[32,1152]{1,0:T(8,128)(2,1)S(1)}, bf16[32,1152]{1,0:T(8,128)(2,1)S(1)}, u32[]{:S(2)}, u32[]{:S(2)}) collective-permute-start(bf16[32,1152]{1,0:T(8,128)(2,1)S(1)} %queries.1.refs_0_), channel_id=1, source_target_pairs={{0,5},{1,4},{2,7},{3,6},{4,1},{5,0},{6,3},{7,2},{8,13},{9,12},{10,... | collective-permute-start | bytes 221192 | tf_op jit(solution)/shard_map/ppermute | solution.py:19
  15.5 4.5 %collective-permute-start.4 = (bf16[32,1152]{1,0:T(8,128)(2,1)S(1)}, bf16[32,1152]{1,0:T(8,128)(2,1)S(1)}, u32[]{:S(2)}, u32[]{:S(2)}) collective-permute-start(bf16[32,1152]{1,0:T(8,128)(2,1)S(1)} %queries.1.refs_0_), channel_id=1, source_target_pairs={{0,3},{1,2},{2,1},{3,0},{4,7},{5,6},{6,5},{7,4},{8,11},{9,10},{10,... | collective-permute-start | bytes 221192 | tf_op jit(solution)/shard_map/ppermute | solution.py:19
  18.0 4.5 %collective-permute-start.5 = (bf16[32,1152]{1,0:T(8,128)(2,1)S(1)}, bf16[32,1152]{1,0:T(8,128)(2,1)S(1)}, u32[]{:S(2)}, u32[]{:S(2)}) collective-permute-start(bf16[32,1152]{1,0:T(8,128)(2,1)S(1)} %collective-permute-done.1.refs_1_), channel_id=1, source_target_pairs={{0,3},{1,2},{2,1},{3,0},{4,7},{5,6},{6,5},{7,4},{8,11},{9,10},{10,... | collective-permute-start | bytes 221192 | tf_op jit(solution)/shard_map/ppermute | solution.py:19
  24.6 5.1 %collective-permute-start.9 = (s16[16,1152]{1,0:T(8,128)(2,1)S(1)}, s16[16,1152]{1,0:T(8,128)(2,1)S(1)}, u32[]{:S(2)}, u32[]{:S(2)}) collective-permute-start(s16[16,1152]{1,0:T(8,128)(2,1)S(1)} %get-tuple-element.28), channel_id=1, source_target_pairs={{0,3},{1,2},{2,1},{3,0},{4,7},{5,6},{6,5},{7,4},{8,11},{9,10},{10,... | collective-permute-start | bytes 110600 | tf_op jit(solution)/shard_map/ppermute | solution.py:19
  26.1 7.5 %collective-permute-start.6 = (s16[32,1152]{1,0:T(8,128)(2,1)S(1)}, s16[32,1152]{1,0:T(8,128)(2,1)S(1)}, u32[]{:S(2)}, u32[]{:S(2)}) collective-permute-start(s16[32,1152]{1,0:T(8,128)(2,1)S(1)} %get-tuple-element.25), channel_id=1, source_target_pairs={{0,3},{1,2},{2,1},{3,0},{4,7},{5,6},{6,5},{7,4},{8,11},{9,10},{10,... | collective-permute-start | bytes 221192 | tf_op jit(solution)/shard_map/ppermute | solution.py:19
  26.4 5.5 %collective-permute-start.7 = (s16[16,1152]{1,0:T(8,128)(2,1)S(1)}, s16[16,1152]{1,0:T(8,128)(2,1)S(1)}, u32[]{:S(2)}, u32[]{:S(2)}) collective-permute-start(s16[16,1152]{1,0:T(8,128)(2,1)S(1)} %get-tuple-element.27), channel_id=1, source_target_pairs={{0,3},{1,2},{2,1},{3,0},{4,7},{5,6},{6,5},{7,4},{8,11},{9,10},{10,... | collective-permute-start | bytes 110600 | tf_op jit(solution)/shard_map/ppermute | solution.py:19
  29.9 3.7 %collective-permute-start.10 = (s16[16,1152]{1,0:T(8,128)(2,1)S(1)}, s16[16,1152]{1,0:T(8,128)(2,1)S(1)}, u32[]{:S(2)}, u32[]{:S(2)}) collective-permute-start(s16[16,1152]{1,0:T(8,128)(2,1)S(1)} %emit.4), channel_id=1, source_target_pairs={{0,5},{1,4},{2,7},{3,6},{4,1},{5,0},{6,3},{7,2},{8,13},{9,12},{10,... | collective-permute-start | bytes 110600 | tf_op jit(solution)/shard_map/ppermute | solution.py:19
  32.0 5.1 %collective-permute-start.8 = (s16[16,1152]{1,0:T(8,128)(2,1)S(1)}, s16[16,1152]{1,0:T(8,128)(2,1)S(1)}, u32[]{:S(2)}, u32[]{:S(2)}) collective-permute-start(s16[16,1152]{1,0:T(8,128)(2,1)S(1)} %emit.3), channel_id=1, source_target_pairs={{0,5},{1,4},{2,7},{3,6},{4,1},{5,0},{6,3},{7,2},{8,13},{9,12},{10,... | collective-permute-start | bytes 110600 | tf_op jit(solution)/shard_map/ppermute | solution.py:19
  33.8 4.5 %collective-permute-start.11 = (s16[16,1152]{1,0:T(8,128)(2,1)S(1)}, s16[16,1152]{1,0:T(8,128)(2,1)S(1)}, u32[]{:S(2)}, u32[]{:S(2)}) collective-permute-start(s16[16,1152]{1,0:T(8,128)(2,1)S(1)} %emit.5), channel_id=1, source_target_pairs={{0,9},{1,8},{2,11},{3,10},{4,13},{5,12},{6,15},{7,14},{8,1},{9,0},... | collective-permute-start | bytes 110600 | tf_op jit(solution)/shard_map/ppermute | solution.py:19
  36.7 1.6 %copy-start.1 = (bf16[1024,1024]{1,0:T(8,128)(2,1)S(1)}, bf16[1024,1024]{1,0:T(8,128)(2,1)}, u32[]{:S(2)}) copy-start(bf16[1024,1024]{1,0:T(8,128)(2,1)} %w_ref.7) | copy-start | bytes 6291460
  36.7 1.6 %copy-start.3 = (bf16[16,1024]{1,0:T(8,128)(2,1)S(1)}, bf16[16,1024]{1,0:T(8,128)(2,1)}, u32[]{:S(2)}) copy-start(bf16[16,1024]{1,0:T(8,128)(2,1)} %cand_ref.3) | copy-start | bytes 98308

commit v6 on v5

--- a/solution.py
+++ b/solution.py
@@ -219,17 +219,16 @@
     )(first, second)
 
 
-def attend_kernel(heads, query, k0, v0, k1, v1, acc_ref):
-    n_keys, width = k0.shape
+def attend_kernel(heads, query, sides, acc_ref, held_ref):
+    n_keys, width = sides[0][0].shape
     size = width // heads
     rows = query.shape[0]
     limit = limits_of(query, width)
     inverse = 1.0 / (limit + 1.0)
     position = lax.broadcasted_iota(jnp.int32, (rows, n_keys), 1).astype(jnp.float32)
-    sides = ((k0, v0), (k1, v1))
     share = []
-    for side in range(2):
-        base = ((lax.axis_index("hist") ^ side) * n_keys).astype(jnp.float32)
+    for _, _, twin in sides:
+        base = ((lax.axis_index("hist") ^ twin) * n_keys).astype(jnp.float32)
         share.append(jnp.where(position + base < limit, inverse, 0.0))
 
     def scores_of(head):
@@ -241,7 +240,7 @@
                 (((1,), (1,)), ((), ())),
                 preferred_element_type=jnp.float32,
             )
-            for k, _ in sides
+            for k, _, _ in sides
         ]
 
     ahead = scores_of(0)
@@ -250,29 +249,34 @@
         if head + 1 < heads:
             ahead = scores_of(head + 1)
         cols = slice(head * size, (head + 1) * size)
-        total = None
-        for side, (_, v) in enumerate(sides):
-            half = scores[side] * (0.5 * size ** (-0.5))
-            weight = ((half + half * jnp.tanh(half)) * share[side]).astype(jnp.bfloat16)
+        total = None if held_ref is None else held_ref[:, cols]
+        for place, (_, v, _) in enumerate(sides):
+            half = scores[place] * (0.5 * size ** (-0.5))
+            weight = ((half + half * jnp.tanh(half)) * share[place]).astype(jnp.bfloat16)
             part = jnp.dot(weight, v[:, cols], preferred_element_type=jnp.float32)
             total = part if total is None else total + part
         acc_ref[:, cols] = total
-    made = acc_ref[...]
-    return made - jnp.mean(made, axis=-1, keepdims=True)
-
-
-def attend(queries, shards, heads, parts, coded):
+
+
+def attend(queries, shards, twins, heads, held, pieces):
     rows = queries[0].shape[0]
     _, width = shards[0].shape
-    blocks = len(queries)
-    pieces = [rows // part for part in parts for _ in range(part)]
+    blocks, count = len(queries), len(shards)
+    given = [] if held is None else [held]
 
     def body(*refs):
-        ins, shard_refs, outs = refs[:blocks], refs[blocks : blocks + 4], refs[blocks + 4 : -1]
+        ins, shard_refs = refs[:blocks], refs[blocks : blocks + count]
+        held_ref = None if held is None else refs[blocks + count]
+        outs = refs[blocks + count + len(given) :]
+        acc_ref = outs[-1]
         query = jnp.concatenate([ref[...] for ref in ins], axis=0)
-        made = attend_kernel(heads, query, *shard_refs, refs[-1])
+        sides = [(*shard_refs[2 * i : 2 * i + 2], twin) for i, twin in enumerate(twins)]
+        attend_kernel(heads, query, sides, acc_ref, held_ref)
+        if pieces:
+            made = acc_ref[...]
+            made = made - jnp.mean(made, axis=-1, keepdims=True)
         first = 0
-        for piece, out_ref in zip(pieces, outs):
+        for (piece, coded), out_ref in zip(pieces, outs):
             part = made[first : first + piece]
             first += piece
             if coded:
@@ -280,19 +284,21 @@
             else:
                 out_ref[...] = part
 
-    return pl.pallas_call(
-        body,
-        out_shape=[
-            jax.ShapeDtypeStruct((piece, width + EXTRA), jnp.int16)
-            if coded
-            else jax.ShapeDtypeStruct((piece, width), jnp.float32)
-            for piece in pieces
-        ],
-        in_specs=[whole()] * (blocks + 4),
-        out_specs=[whole()] * len(pieces),
-        scratch_shapes=[pltpu.VMEM((blocks * rows, width), jnp.float32)],
-        compiler_params=PARAMS,
-    )(*near_by(*queries, *shards))
+    whole_acc = jax.ShapeDtypeStruct((blocks * rows, width), jnp.float32)
+    out = [
+        jax.ShapeDtypeStruct((piece, width + EXTRA), jnp.int16)
+        if coded
+        else jax.ShapeDtypeStruct((piece, width), jnp.float32)
+        for piece, coded in pieces
+    ]
+    return pl.pallas_call(
+        body,
+        out_shape=out or [whole_acc],
+        in_specs=[whole()] * (blocks + count + len(given)),
+        out_specs=[whole()] * (len(out) or 1),
+        scratch_shapes=[pltpu.VMEM((blocks * rows, width), jnp.float32)] if out else [],
+        compiler_params=PARAMS,
+    )(*near_by(*queries, *shards, *given))
 
 
 def own_kernel(heads, tile, query_ref, rows_ref, w_ref, key_ref, value_ref, gate_ref, term_ref):
@@ -301,11 +307,14 @@
     query = query_ref[:rows, :width].astype(jnp.float32)
     inverse = 1.0 / (limits_of(query_ref[:rows], width) + 1.0)
     products = query * key_ref[...].astype(jnp.float32)
+    terms = []
     for head in range(heads):
         cols = slice(head * size, (head + 1) * size)
         score = jnp.sum(products[:, cols], axis=-1, keepdims=True)
         weight = (silu(score * size ** (-0.5)) * inverse).astype(jnp.bfloat16)
-        term_ref[:, cols] = weight.astype(jnp.float32) * value_ref[:, cols].astype(jnp.float32)
+        terms.append(weight.astype(jnp.float32) * value_ref[:, cols].astype(jnp.float32))
+    term = jnp.concatenate(terms, axis=1)
+    term_ref[...] = term - jnp.mean(term, axis=-1, keepdims=True)
     for at in range(0, width, tile):
         gate_ref[:, at : at + tile] = silu(
             jnp.dot(
@@ -377,14 +386,33 @@
     )(*arrays)
 
 
-def finish(candidates, terms, term, gate, w_out):
+def gather_up(terms, term, width):
     arrays, (listed,) = placed([terms])
-
-    def body(cand_ref, term_ref, gate_ref, w_ref, *refs):
-        rows, width = cand_ref.shape
-        attended = total_of(listed, refs, rows, width) + term_ref[...]
-        mixed = (norm(attended) * gate_ref[...].astype(jnp.float32)).astype(jnp.bfloat16)
-        refs[-1][...] = (
+    rows = term.shape[0]
+
+    def body(term_ref, *refs):
+        refs[-1][...] = total_of(listed, refs, rows, width) + term_ref[...]
+
+    return pl.pallas_call(
+        body,
+        out_shape=jax.ShapeDtypeStruct((rows, width), jnp.float32),
+        in_specs=[whole()] * (1 + len(arrays)),
+        out_specs=whole(),
+        compiler_params=PARAMS,
+        name="gather_up",
+    )(term, *arrays)
+
+
+def finish(candidates, held, got, gate, w_out):
+    def body(cand_ref, held_ref, got_ref, gate_ref, w_ref, out_ref):
+        width = cand_ref.shape[1]
+        attended = held_ref[...] + decode(got_ref[...], width)
+        mean = jnp.mean(attended, axis=-1, keepdims=True)
+        square = jnp.mean(attended * attended, axis=-1, keepdims=True)
+        scale = lax.rsqrt(jnp.maximum(square - mean * mean, 0.0) + EPS)
+        normalised = (attended - mean) * scale
+        mixed = (normalised * gate_ref[...].astype(jnp.float32)).astype(jnp.bfloat16)
+        out_ref[...] = (
             cand_ref[...].astype(jnp.float32)
             + jnp.dot(mixed, w_ref[...], preferred_element_type=jnp.float32)
         ).astype(jnp.bfloat16)
@@ -392,11 +420,11 @@
     return pl.pallas_call(
         body,
         out_shape=jax.ShapeDtypeStruct(candidates.shape, jnp.bfloat16),
-        in_specs=[whole()] * (4 + len(arrays)),
+        in_specs=[whole()] * 5,
         out_specs=whole(),
         compiler_params=PARAMS,
         name="finish",
-    )(candidates, term, gate, w_out, *arrays)
+    )(candidates, held, got, gate, w_out)
 
 
 def layer(history, candidates, hist_length, visible, w_proj, w_out):
@@ -424,12 +452,22 @@
     shards = (keys, values, other_keys, other_values)
     blocks = inner.shape[0] // rows
     sides = min(blocks, 2)
-    sent_inner, *sent_outer = attend([far_inner, far_outer], shards, HEADS, (1, sides), True)
+    count = blocks * rows
+    early = [far_inner, inner, outer]
+    (held,) = attend(early, (keys, values), (0,), HEADS, None, ())
+    sent_inner, near_inner, near_outer = attend(
+        early,
+        (other_keys, other_values),
+        (1,),
+        HEADS,
+        held,
+        ((count, True), (count, False), (count, False)),
+    )
+    sent_outer = attend([far_outer], shards, (0, 1), HEADS, None, ((count // sides, True),) * sides)
     got_outer = [None] * sides
     for side in reversed(range(sides)):
         got_outer[side] = swapped(sent_outer[side], "hist", masks[-1])
     got_inner = swapped(sent_inner, "hist", masks[-1])
-    near_inner, near_outer = attend([inner, outer], shards, HEADS, (1, 1), False)
     gate, term = own(inner, rows_both, w_proj, self_key, self_value, HEADS)
     piece = blocks * rows // sides
     terms = [[(near_outer, side * piece), (got_outer[side], 0)] for side in range(sides)]
@@ -452,8 +490,9 @@
             terms.append([(near_inner, first), (got_inner, first)])
             terms[-1] += [(array, first) for array in last[:-1]] + [(got[1], side * piece)]
         stage -= 1
-    terms = [(near_inner, 0), (got_inner, 0)] + [(array, 0) for array in last]
-    return finish(candidates, terms, term, gate, w_out)
+    terms = [(near_inner, 0), (got_inner, 0)] + [(array, 0) for array in last[:-1]]
+    held = gather_up(terms, term, width)
+    return finish(candidates, held, last[-1], gate, w_out)
 
 
 def solution(mesh):

time: 39.8 us -> 43.1 us (1.083)
  waiting for transfers between devices: 6.24 us -> 9.97 us
  starting transfers between devices: 19 us -> 18.4 us
    ppermute x12, waiting for transfers between devices: 6.24 us -> 9.97 us  [swapped(): return lax.ppermute(shard, axis, [(i, i ^ mask) for i in range(size)])]
    ppermute x12, starting transfers between devices: 19 us -> 18.4 us  [swapped(): return lax.ppermute(shard, axis, [(i, i ^ mask) for i in range(size)])]
    pallas_call x2 -> x4, Pallas kernels: 3.87 us -> 4.1 us  [the longest x3 4 us: attend(): pl.pallas_call(body, out_shape=out or [whole_acc], in_specs=[whole()] * (...]
  transfers between devices with their start and end apart: 12 -> 12, of which waited for: 5 -> 5; matrix products, arithmetic and copies ran while one was open for 0% -> 0% of each run, Pallas kernels for 12% -> 17%
where the time goes in v6:
time: 43.1 us; the launch traced here: 42.9 us
  starting transfers between devices  18.4 us (43%)
  Pallas kernels  11.1 us (26%)
  waiting for transfers between devices  9.97 us (23%)
  local copies, waits for them, and re-layouts  2.7 us (6%)
  between operations  0.76 us (2%)
    ppermute x12, starting transfers between devices, swapped(): return lax.ppermute(shard, axis, [(i, i ^ mask) for i in range(size)])  18.4 us
    ppermute x12, waiting for transfers between devices, swapped(): return lax.ppermute(shard, axis, [(i, i ^ mask) for i in range(size)])  9.97 us
    pallas_call x3, Pallas kernels, attend(): pl.pallas_call(body, out_shape=out or [whole_acc], in_specs=[whole()] * (...  4 us
    unnamed x8, local copies, waits for them, and re-layouts  2.7 us
    pallas_call x1, Pallas kernels, project_keys(): pl.pallas_call(body, out_shape=(jax.ShapeDtypeStruct((n_keys, width), jnp...  1.87 us
    pallas_call x1, Pallas kernels, project_values(): pl.pallas_call(body, out_shape=(jax.ShapeDtypeStruct((n_keys, width), jnp...  1.42 us
    pallas_call x1, Pallas kernels, finish(): pl.pallas_call(body, out_shape=jax.ShapeDtypeStruct(candidates.shape, jnp...  1.15 us
    pallas_call x1, Pallas kernels, begin(): pl.pallas_call(body, out_shape=jax.ShapeDtypeStruct((rows, width + EXTRA)...  0.94 us
  transfers between devices with their start and end apart: 12, of which 5 were waited for; matrix products, arithmetic and copies ran while one was open for 0% of the time, Pallas kernels for 17%

profile of v6, /device:TPU:0, one launch (start us, length us, event | category | flops | bytes accessed | tf_op | source)
XLA Modules:
  0.0 42.9 jit_solution(13434416988845788924)
XLA Ops:
  0.0 0.0 copy-start
  0.0 0.0 copy-start.2
  0.0 0.9 %begin.1.packed_ref = bf16[16,1152]{1,0:T(8,128)(2,1)S(1)} custom-call(bf16[16,1024]{1,0:T(8,128)(2,1)} %cand_ref.3, s32[1,16]{1,0:T(1,128)} %bitcast.1), custom_call_target="tpu_custom_call" | custom-call | flops 6442450944 | bytes 20971520 | tf_op jit(solution)/shard_map/begin/pallas_call | solution.py:100
  1.0 2.5 %copy-done = bf16[1024,4096]{1,0:T(8,128)(2,1)S(1)} copy-done((bf16[1024,4096]{1,0:T(8,128)(2,1)S(1)}, bf16[1024,4096]{1,0:T(8,128)(2,1)}, u32[]{:S(2)}) %copy-start) | copy-done | bytes 8388632
  3.4 0.2 copy-done.2
  3.6 1.9 %keys.1 = (bf16[512,1024]{1,0:T(8,128)(2,1)S(1)}, bf16[16,1024]{1,0:T(8,128)(2,1)S(1)}, bf16[528,1024]{1,0:T(8,128)(2,1)S(1)}) custom-call(bf16[512,1024]{1,0:T(8,128)(2,1)S(1)} %copy-done.2, bf16[16,1152]{1,0:T(8,128)(2,1)S(1)} %begin.1.packed_ref, bf16[1024,4096]{1,0:T(8,128)(2,1)S(1)} %copy-done), custom_call_target="tpu_custom_call" | custom-call | tf_op jit(solution)/shard_map/keys/pallas_call | solution.py:138
  5.5 0.6 %collective-permute-start.3 = (bf16[512,1024]{1,0:T(8,128)(2,1)S(1)}, bf16[512,1024]{1,0:T(8,128)(2,1)S(1)}, u32[]{:S(2)}, u32[]{:S(2)}) collective-permute-start(bf16[512,1024]{1,0:T(8,128)(2,1)S(1)} %get-tuple-element.21.refs_3_.refs_1_), channel_id=1, source_target_pairs={{0,1},{1,0},{2,3},{3,2},{4,5},{5,4},{6,7},{7,6},{8,9},{9,8},{10,11... | collective-permute-start | bytes 3145736 | tf_op jit(solution)/shard_map/ppermute | solution.py:19
  6.1 1.4 %values.1 = (bf16[512,1024]{1,0:T(8,128)(2,1)S(1)}, bf16[16,1024]{1,0:T(8,128)(2,1)S(1)}) custom-call(bf16[528,1024]{1,0:T(8,128)(2,1)S(1)} %get-tuple-element.17.rows_ref.refs_1_, bf16[1024,4096]{1,0:T(8,128)(2,1)S(1)} %copy-done), custom_call_target="tpu_custom_call" | custom-call | tf_op jit(solution)/shard_map/values/pallas_call | solution.py:160
  7.5 0.1 collective-permute-start.4
  7.6 3.7 %collective-permute-start = (bf16[16,1152]{1,0:T(8,128)(2,1)S(1)}, bf16[16,1152]{1,0:T(8,128)(2,1)S(1)}, u32[]{:S(2)}, u32[]{:S(2)}) collective-permute-start(bf16[16,1152]{1,0:T(8,128)(2,1)S(1)} %begin.1.packed_ref), channel_id=1, source_target_pairs={{0,9},{1,8},{2,11},{3,10},{4,13},{5,12},{6,15},{7,14},{8,1},{9,0},... | collective-permute-start | bytes 110600 | tf_op jit(solution)/shard_map/ppermute | solution.py:19
  12.0 1.0 %collective-permute-done.got_ref = bf16[16,1152]{1,0:T(8,128)(2,1)S(1)} collective-permute-done((bf16[16,1152]{1,0:T(8,128)(2,1)S(1)}, bf16[16,1152]{1,0:T(8,128)(2,1)S(1)}, u32[]{:S(2)}, u32[]{:S(2)}) %collective-permute-start) | collective-permute-done | bytes 36896 | tf_op jit(solution)/shard_map/ppermute | solution.py:19
  13.0 0.6 %queries.1.refs_0_.refs_1_ = bf16[32,1152]{1,0:T(8,128)(2,1)S(1)} custom-call(s32[1]{0:T(128)S(6)} %copy.7.length_ref, bf16[16,1152]{1,0:T(8,128)(2,1)S(1)} %begin.1.packed_ref, bf16[16,1152]{1,0:T(8,128)(2,1)S(1)} %collective-permute-done.got_ref, bf16[1024,4096]{1,0:T(8,128)(2,1)S(1)} %copy-done), custom_call_target="tpu_custom_call" | custom-call | tf_op jit(solution)/shard_map/queries/pallas_call | solution.py:195
  13.6 1.9 %collective-permute-start.2 = (bf16[32,1152]{1,0:T(8,128)(2,1)S(1)}, bf16[32,1152]{1,0:T(8,128)(2,1)S(1)}, u32[]{:S(2)}, u32[]{:S(2)}) collective-permute-start(bf16[32,1152]{1,0:T(8,128)(2,1)S(1)} %queries.1.refs_0_.refs_1_), channel_id=1, source_target_pairs={{0,5},{1,4},{2,7},{3,6},{4,1},{5,0},{6,3},{7,2},{8,13},{9,12},{10,... | collective-permute-start | bytes 221192 | tf_op jit(solution)/shard_map/ppermute | solution.py:19
  15.5 2.5 %collective-permute-done.2.refs_2_ = bf16[32,1152]{1,0:T(8,128)(2,1)S(1)} collective-permute-done((bf16[32,1152]{1,0:T(8,128)(2,1)S(1)}, bf16[32,1152]{1,0:T(8,128)(2,1)S(1)}, u32[]{:S(2)}, u32[]{:S(2)}) %collective-permute-start.2) | collective-permute-done | bytes 73760 | tf_op jit(solution)/shard_map/ppermute | solution.py:19
  18.0 1.7 %collective-permute-start.6 = (bf16[32,1152]{1,0:T(8,128)(2,1)S(1)}, bf16[32,1152]{1,0:T(8,128)(2,1)S(1)}, u32[]{:S(2)}, u32[]{:S(2)}) collective-permute-start(bf16[32,1152]{1,0:T(8,128)(2,1)S(1)} %collective-permute-done.2.refs_2_), channel_id=1, source_target_pairs={{0,3},{1,2},{2,1},{3,0},{4,7},{5,6},{6,5},{7,4},{8,11},{9,10},{10,... | collective-permute-start | bytes 221192 | tf_op jit(solution)/shard_map/ppermute | solution.py:19
  19.7 0.1 collective-permute-start.1
  19.8 2.6 %collective-permute-done.6.refs_0_ = bf16[32,1152]{1,0:T(8,128)(2,1)S(1)} collective-permute-done((bf16[32,1152]{1,0:T(8,128)(2,1)S(1)}, bf16[32,1152]{1,0:T(8,128)(2,1)S(1)}, u32[]{:S(2)}, u32[]{:S(2)}) %collective-permute-start.6) | collective-permute-done | bytes 73760 | tf_op jit(solution)/shard_map/ppermute | solution.py:19
  22.4 0.0 collective-permute-done.3.refs_3_
  22.4 0.0 collective-permute-done.4.refs_4_
  22.4 1.7 %shard_map.66 = (s16[16,1152]{1,0:T(8,128)(2,1)S(1)}, s16[16,1152]{1,0:T(8,128)(2,1)S(1)}) custom-call(bf16[32,1152]{1,0:T(8,128)(2,1)S(1)} %collective-permute-done.6.refs_0_, bf16[512,1024]{1,0:T(8,128)(2,1)S(1)} %get-tuple-element.21.refs_3_.refs_1_, bf16[512,1024]{1,0:T(8,128)(2,1)S(1)} %get-tuple-element.22.refs_4_.refs_2_, ...), custom_call_target="tpu_custom_call" | custom-call | tf_op jit(solution)/shard_map/pallas_call | solution.py:294
  24.0 2.3 %collective-permute-start.9 = (s16[16,1152]{1,0:T(8,128)(2,1)S(1)}, s16[16,1152]{1,0:T(8,128)(2,1)S(1)}, u32[]{:S(2)}, u32[]{:S(2)}) collective-permute-start(s16[16,1152]{1,0:T(8,128)(2,1)S(1)} %get-tuple-element.27), channel_id=1, source_target_pairs={{0,3},{1,2},{2,1},{3,0},{4,7},{5,6},{6,5},{7,4},{8,11},{9,10},{10,... | collective-permute-start | bytes 110600 | tf_op jit(solution)/shard_map/ppermute | solution.py:19
  26.3 0.0 collective-permute-done.1.refs_0_
  26.3 1.1 %shard_map.64.refs_5_ = f32[96,1024]{1,0:T(8,128)S(1)} custom-call(bf16[32,1152]{1,0:T(8,128)(2,1)S(1)} %collective-permute-done.1.refs_0_, bf16[32,1152]{1,0:T(8,128)(2,1)S(1)} %queries.1.refs_0_.refs_1_, bf16[32,1152]{1,0:T(8,128)(2,1)S(1)} %collective-permute-done.2.refs_2_, bf16[512,1024]{1,0:T(8,128)(2,1)S(1)} %get-tuple-element.21.refs_3_.refs_1_, ...), custom_call_target="tpu_custom_call" | custom-call | tf_op jit(solution)/shard_map/pallas_call | solution.py:294
  27.4 1.2 %shard_map.65 = (s16[32,1152]{1,0:T(8,128)(2,1)S(1)}, f32[32,1024]{1,0:T(8,128)S(1)}, f32[32,1024]{1,0:T(8,128)S(1)}) custom-call(bf16[32,1152]{1,0:T(8,128)(2,1)S(1)} %collective-permute-done.1.refs_0_, bf16[32,1152]{1,0:T(8,128)(2,1)S(1)} %queries.1.refs_0_.refs_1_, bf16[32,1152]{1,0:T(8,128)(2,1)S(1)} %collective-permute-done.2.refs_2_, ...), custom_call_target="tpu_custom_call" | custom-call | tf_op jit(solution)/shard_map/pallas_call | solution.py:294
  28.7 0.1 collective-permute-start.5
  28.8 1.7 %collective-permute-start.7 = (s16[16,1152]{1,0:T(8,128)(2,1)S(1)}, s16[16,1152]{1,0:T(8,128)(2,1)S(1)}, u32[]{:S(2)}, u32[]{:S(2)}) collective-permute-start(s16[16,1152]{1,0:T(8,128)(2,1)S(1)} %get-tuple-element.26), channel_id=1, source_target_pairs={{0,3},{1,2},{2,1},{3,0},{4,7},{5,6},{6,5},{7,4},{8,11},{9,10},{10,... | collective-permute-start | bytes 110600 | tf_op jit(solution)/shard_map/ppermute | solution.py:19
  30.5 0.0 collective-permute-done.9.refs_1_
  30.5 0.2 emit.4
  30.7 1.4 %collective-permute-start.10 = (s16[16,1152]{1,0:T(8,128)(2,1)S(1)}, s16[16,1152]{1,0:T(8,128)(2,1)S(1)}, u32[]{:S(2)}, u32[]{:S(2)}) collective-permute-start(s16[16,1152]{1,0:T(8,128)(2,1)S(1)} %emit.4), channel_id=1, source_target_pairs={{0,5},{1,4},{2,7},{3,6},{4,1},{5,0},{6,3},{7,2},{8,13},{9,12},{10,... | collective-permute-start | bytes 110600 | tf_op jit(solution)/shard_map/ppermute | solution.py:19
  32.1 2.0 %collective-permute-done.7.refs_1_ = s16[16,1152]{1,0:T(8,128)(2,1)S(1)} collective-permute-done((s16[16,1152]{1,0:T(8,128)(2,1)S(1)}, s16[16,1152]{1,0:T(8,128)(2,1)S(1)}, u32[]{:S(2)}, u32[]{:S(2)}) %collective-permute-start.7) | collective-permute-done | bytes 36896 | tf_op jit(solution)/shard_map/ppermute | solution.py:19
  34.1 0.2 emit.3
  34.3 1.7 %collective-permute-start.8 = (s16[16,1152]{1,0:T(8,128)(2,1)S(1)}, s16[16,1152]{1,0:T(8,128)(2,1)S(1)}, u32[]{:S(2)}, u32[]{:S(2)}) collective-permute-start(s16[16,1152]{1,0:T(8,128)(2,1)S(1)} %emit.3), channel_id=1, source_target_pairs={{0,5},{1,4},{2,7},{3,6},{4,1},{5,0},{6,3},{7,2},{8,13},{9,12},{10,... | collective-permute-start | bytes 110600 | tf_op jit(solution)/shard_map/ppermute | solution.py:19
  36.0 0.0 collective-permute-done.10.refs_2_
  36.0 0.0 collective-permute-done.5.refs_1_
  36.0 0.2 emit.5
  36.1 3.2 %collective-permute-start.11 = (s16[16,1152]{1,0:T(8,128)(2,1)S(1)}, s16[16,1152]{1,0:T(8,128)(2,1)S(1)}, u32[]{:S(2)}, u32[]{:S(2)}) collective-permute-start(s16[16,1152]{1,0:T(8,128)(2,1)S(1)} %emit.5), channel_id=1, source_target_pairs={{0,9},{1,8},{2,11},{3,10},{4,13},{5,12},{6,15},{7,14},{8,1},{9,0},... | collective-permute-start | bytes 110600 | tf_op jit(solution)/shard_map/ppermute | solution.py:19
  39.4 0.0 copy-start.1
  39.4 0.0 copy-start.3
  39.4 0.4 own.1
  39.8 0.0 collective-permute-done.8.refs_2_
  39.8 0.1 gather_up.1.held_ref
  39.9 1.8 %collective-permute-done.11.got_ref = s16[16,1152]{1,0:T(8,128)(2,1)S(1)} collective-permute-done((s16[16,1152]{1,0:T(8,128)(2,1)S(1)}, s16[16,1152]{1,0:T(8,128)(2,1)S(1)}, u32[]{:S(2)}, u32[]{:S(2)}) %collective-permute-start.11) | collective-permute-done | bytes 36896 | tf_op jit(solution)/shard_map/ppermute | solution.py:19
  41.8 0.0 copy-done.1
  41.8 0.0 copy-done.3
  41.8 1.2 %finish.1 = bf16[16,1024]{1,0:T(8,128)(2,1)} custom-call(bf16[16,1024]{1,0:T(8,128)(2,1)S(1)} %copy-done.3, f32[16,1024]{1,0:T(8,128)S(1)} %gather_up.1.held_ref, s16[16,1152]{1,0:T(8,128)(2,1)S(1)} %collective-permute-done.11.got_ref, bf16[16,1024]{1,0:T(8,128)(2,1)S(1)} %get-tuple-element.28.gate_ref, bf16[1024,1024]{1,0:T(8,128)(2,1)S(1)} %copy-done.1), custom_call_target="tpu_custom_call" | custom-call | tf_op jit(solution)/shard_map/finish/pallas_call | solution.py:420
Async XLA Ops:
  0.0 3.4 %copy-start = (bf16[1024,4096]{1,0:T(8,128)(2,1)S(1)}, bf16[1024,4096]{1,0:T(8,128)(2,1)}, u32[]{:S(2)}) copy-start(bf16[1024,4096]{1,0:T(8,128)(2,1)} %refs_2_.1) | copy-start | bytes 25165828
  0.0 3.6 %copy-start.2 = (bf16[512,1024]{1,0:T(8,128)(2,1)S(1)}, bf16[512,1024]{1,0:T(8,128)(2,1)}, u32[]{:S(2)}) copy-start(bf16[512,1024]{1,0:T(8,128)(2,1)} %hist_ref.1) | copy-start | bytes 3145732
  5.5 16.8 %collective-permute-start.3 = (bf16[512,1024]{1,0:T(8,128)(2,1)S(1)}, bf16[512,1024]{1,0:T(8,128)(2,1)S(1)}, u32[]{:S(2)}, u32[]{:S(2)}) collective-permute-start(bf16[512,1024]{1,0:T(8,128)(2,1)S(1)} %get-tuple-element.21.refs_3_.refs_1_), channel_id=1, source_target_pairs={{0,1},{1,0},{2,3},{3,2},{4,5},{5,4},{6,7},{7,6},{8,9},{9,8},{10,11... | collective-permute-start | bytes 3145736 | tf_op jit(solution)/shard_map/ppermute | solution.py:19
  7.5 14.9 %collective-permute-start.4 = (bf16[512,1024]{1,0:T(8,128)(2,1)S(1)}, bf16[512,1024]{1,0:T(8,128)(2,1)S(1)}, u32[]{:S(2)}, u32[]{:S(2)}) collective-permute-start(bf16[512,1024]{1,0:T(8,128)(2,1)S(1)} %get-tuple-element.22.refs_4_.refs_2_), channel_id=1, source_target_pairs={{0,1},{1,0},{2,3},{3,2},{4,5},{5,4},{6,7},{7,6},{8,9},{9,8},{10,11... | collective-permute-start | bytes 3145736 | tf_op jit(solution)/shard_map/ppermute | solution.py:19
  7.6 5.4 %collective-permute-start = (bf16[16,1152]{1,0:T(8,128)(2,1)S(1)}, bf16[16,1152]{1,0:T(8,128)(2,1)S(1)}, u32[]{:S(2)}, u32[]{:S(2)}) collective-permute-start(bf16[16,1152]{1,0:T(8,128)(2,1)S(1)} %begin.1.packed_ref), channel_id=1, source_target_pairs={{0,9},{1,8},{2,11},{3,10},{4,13},{5,12},{6,15},{7,14},{8,1},{9,0},... | collective-permute-start | bytes 110600 | tf_op jit(solution)/shard_map/ppermute | solution.py:19
  13.6 4.4 %collective-permute-start.2 = (bf16[32,1152]{1,0:T(8,128)(2,1)S(1)}, bf16[32,1152]{1,0:T(8,128)(2,1)S(1)}, u32[]{:S(2)}, u32[]{:S(2)}) collective-permute-start(bf16[32,1152]{1,0:T(8,128)(2,1)S(1)} %queries.1.refs_0_.refs_1_), channel_id=1, source_target_pairs={{0,5},{1,4},{2,7},{3,6},{4,1},{5,0},{6,3},{7,2},{8,13},{9,12},{10,... | collective-permute-start | bytes 221192 | tf_op jit(solution)/shard_map/ppermute | solution.py:19
  18.0 4.3 %collective-permute-start.6 = (bf16[32,1152]{1,0:T(8,128)(2,1)S(1)}, bf16[32,1152]{1,0:T(8,128)(2,1)S(1)}, u32[]{:S(2)}, u32[]{:S(2)}) collective-permute-start(bf16[32,1152]{1,0:T(8,128)(2,1)S(1)} %collective-permute-done.2.refs_2_), channel_id=1, source_target_pairs={{0,3},{1,2},{2,1},{3,0},{4,7},{5,6},{6,5},{7,4},{8,11},{9,10},{10,... | collective-permute-start | bytes 221192 | tf_op jit(solution)/shard_map/ppermute | solution.py:19
  19.7 6.6 %collective-permute-start.1 = (bf16[32,1152]{1,0:T(8,128)(2,1)S(1)}, bf16[32,1152]{1,0:T(8,128)(2,1)S(1)}, u32[]{:S(2)}, u32[]{:S(2)}) collective-permute-start(bf16[32,1152]{1,0:T(8,128)(2,1)S(1)} %queries.1.refs_0_.refs_1_), channel_id=1, source_target_pairs={{0,3},{1,2},{2,1},{3,0},{4,7},{5,6},{6,5},{7,4},{8,11},{9,10},{10,... | collective-permute-start | bytes 221192 | tf_op jit(solution)/shard_map/ppermute | solution.py:19
  24.0 6.4 %collective-permute-start.9 = (s16[16,1152]{1,0:T(8,128)(2,1)S(1)}, s16[16,1152]{1,0:T(8,128)(2,1)S(1)}, u32[]{:S(2)}, u32[]{:S(2)}) collective-permute-start(s16[16,1152]{1,0:T(8,128)(2,1)S(1)} %get-tuple-element.27), channel_id=1, source_target_pairs={{0,3},{1,2},{2,1},{3,0},{4,7},{5,6},{6,5},{7,4},{8,11},{9,10},{10,... | collective-permute-start | bytes 110600 | tf_op jit(solution)/shard_map/ppermute | solution.py:19
  28.7 7.3 %collective-permute-start.5 = (s16[32,1152]{1,0:T(8,128)(2,1)S(1)}, s16[32,1152]{1,0:T(8,128)(2,1)S(1)}, u32[]{:S(2)}, u32[]{:S(2)}) collective-permute-start(s16[32,1152]{1,0:T(8,128)(2,1)S(1)} %get-tuple-element.24), channel_id=1, source_target_pairs={{0,3},{1,2},{2,1},{3,0},{4,7},{5,6},{6,5},{7,4},{8,11},{9,10},{10,... | collective-permute-start | bytes 221192 | tf_op jit(solution)/shard_map/ppermute | solution.py:19
  28.8 5.3 %collective-permute-start.7 = (s16[16,1152]{1,0:T(8,128)(2,1)S(1)}, s16[16,1152]{1,0:T(8,128)(2,1)S(1)}, u32[]{:S(2)}, u32[]{:S(2)}) collective-permute-start(s16[16,1152]{1,0:T(8,128)(2,1)S(1)} %get-tuple-element.26), channel_id=1, source_target_pairs={{0,3},{1,2},{2,1},{3,0},{4,7},{5,6},{6,5},{7,4},{8,11},{9,10},{10,... | collective-permute-start | bytes 110600 | tf_op jit(solution)/shard_map/ppermute | solution.py:19
  30.7 5.3 %collective-permute-start.10 = (s16[16,1152]{1,0:T(8,128)(2,1)S(1)}, s16[16,1152]{1,0:T(8,128)(2,1)S(1)}, u32[]{:S(2)}, u32[]{:S(2)}) collective-permute-start(s16[16,1152]{1,0:T(8,128)(2,1)S(1)} %emit.4), channel_id=1, source_target_pairs={{0,5},{1,4},{2,7},{3,6},{4,1},{5,0},{6,3},{7,2},{8,13},{9,12},{10,... | collective-permute-start | bytes 110600 | tf_op jit(solution)/shard_map/ppermute | solution.py:19
  34.3 5.6 %collective-permute-start.8 = (s16[16,1152]{1,0:T(8,128)(2,1)S(1)}, s16[16,1152]{1,0:T(8,128)(2,1)S(1)}, u32[]{:S(2)}, u32[]{:S(2)}) collective-permute-start(s16[16,1152]{1,0:T(8,128)(2,1)S(1)} %emit.3), channel_id=1, source_target_pairs={{0,5},{1,4},{2,7},{3,6},{4,1},{5,0},{6,3},{7,2},{8,13},{9,12},{10,... | collective-permute-start | bytes 110600 | tf_op jit(solution)/shard_map/ppermute | solution.py:19
  36.1 5.6 %collective-permute-start.11 = (s16[16,1152]{1,0:T(8,128)(2,1)S(1)}, s16[16,1152]{1,0:T(8,128)(2,1)S(1)}, u32[]{:S(2)}, u32[]{:S(2)}) collective-permute-start(s16[16,1152]{1,0:T(8,128)(2,1)S(1)} %emit.5), channel_id=1, source_target_pairs={{0,9},{1,8},{2,11},{3,10},{4,13},{5,12},{6,15},{7,14},{8,1},{9,0},... | collective-permute-start | bytes 110600 | tf_op jit(solution)/shard_map/ppermute | solution.py:19
  39.4 2.4 %copy-start.1 = (bf16[1024,1024]{1,0:T(8,128)(2,1)S(1)}, bf16[1024,1024]{1,0:T(8,128)(2,1)}, u32[]{:S(2)}) copy-start(bf16[1024,1024]{1,0:T(8,128)(2,1)} %w_ref.7) | copy-start | bytes 6291460
  39.4 2.4 %copy-start.3 = (bf16[16,1024]{1,0:T(8,128)(2,1)S(1)}, bf16[16,1024]{1,0:T(8,128)(2,1)}, u32[]{:S(2)}) copy-start(bf16[16,1024]{1,0:T(8,128)(2,1)} %cand_ref.3) | copy-start | bytes 98308
